TPU v7x, 32 devices: a whole 2x2x4 slice. The times are simulated.
32 devices in a mesh: dp: 8 (over z, y), tensor: 4 (over x, core).
Axes of the slice: x: 2, y: 2, z: 4, core: 2. Of those that a mesh axis runs over, the one named last changes fastest.
Arguments:
- tokens: bfloat16 [8192, 768], P('dp'), may hold values from -6 to 6
- cotangent: bfloat16 [8192, 768], P('dp'), may hold values from -6 to 6
- item_count: int32 [8], P('dp'), may hold values from 0 to 1, as said below
- timestep: int32 [8], P('dp'), may hold values from 0 to 999
- class_id: int32 [8], P('dp'), may hold values from 0 to 1000
- class_table: bfloat16 [1001, 768], replicated, may hold values from -6 to 6
- w_mod: bfloat16 [4608, 768], replicated, may hold values from -0.21875 to 0.21875
- b_mod: bfloat16 [4608], replicated, may hold values from -3 to 3
- k_att: bfloat16 [9, 768], replicated, may hold values from -2 to 2
- w_qkv: bfloat16 [768, 3, 768], P(None, None, 'tensor'), may hold values from -0.21875 to 0.21875
- w_out: bfloat16 [768, 768], P(None, 'tensor'), may hold values from -0.875 to 0.875
- b_out: bfloat16 [768], replicated, may hold values from -2 to 2
- w_up: bfloat16 [768, 3072], P(None, 'tensor'), may hold values from -0.21875 to 0.21875
- b_up: bfloat16 [3072], P('tensor'), may hold values from -2 to 2
- k_ffn: bfloat16 [9, 3072], P(None, 'tensor'), may hold values from -2 to 2
- w_down: bfloat16 [768, 3072], P(None, 'tensor'), may hold values from -0.109375 to 0.109375
- b_down: bfloat16 [768], replicated, may hold values from -2 to 2
Outputs:
- block_out: bfloat16 [8192, 768], P(('dp', 'tensor'))
- grad_tokens: float32 [8192, 768], P(('dp', 'tensor'))
- grad_class_table: float32 [1001, 768], replicated
- grad_w_mod: float32 [4608, 768], P('dp')
- grad_b_mod: float32 [4608], replicated
- grad_k_att: float32 [9, 768], replicated
- grad_w_qkv: float32 [768, 3, 768], P('dp', None, 'tensor')
- grad_w_out: float32 [768, 768], P('dp', 'tensor')
- grad_b_out: float32 [768], replicated
- grad_w_up: float32 [768, 3072], P('dp', 'tensor')
- grad_b_up: float32 [3072], P('tensor')
- grad_k_ffn: float32 [9, 3072], P(None, 'tensor')
- grad_w_down: float32 [768, 3072], P('dp', 'tensor')
- grad_b_down: float32 [768], replicated
Inputs may be any that keep to these rules, and one draw needn't show every extreme that they name: Item slots below item_count of their dp index hold live items, the others padding; some index of dp has all 1 slots live and some none.
All inputs are finite; a program needn't handle non-finite values.
Results may differ from a plain program's by a relative error of at most 0.028.
The roundings to bfloat16 on the way count: a program that leaves them out, or rounds other values in their place, can miss the bound.
Values may be sent and summed in bfloat16 or wider, within the bound.
No kernel may reach another device: no remote copies, remote signals or barrier semaphores. Data moves between devices by JAX's collectives and lax.ppermute only.
A program may use at most 192 MiB of HBM per device.

v0:
```python
import math

import jax
import jax.numpy as jnp
from jax import lax
from jax.sharding import PartitionSpec as P

HEAD_DIM = 64
SIDE = 32


norm_eps = 1e-06
score_scale = 0.125
highest = lax.Precision.HIGHEST


def layer_norm(values):
    center = values - jnp.mean(values, axis=-1, keepdims=True)
    return center * lax.rsqrt(jnp.mean(center * center, axis=-1, keepdims=True) + norm_eps)


def time_features(timestep, width):
    half_width = width // 2
    freqs = jnp.exp(-math.log(10000.0) * jnp.arange(half_width, dtype=jnp.float32) / half_width)
    angles = timestep.astype(jnp.float32)[:, None] * freqs[None, :]
    return jnp.concatenate([jnp.cos(angles), jnp.sin(angles)], axis=1)


def depthwise(field, kernel):
    grid_side = field.shape[1]
    padded = jnp.pad(field, ((0, 0), (1, 1), (1, 1), (0, 0)))
    total = jnp.zeros_like(field)
    for vertical in range(3):
        for horizontal in range(3):
            total = (
                total
                + kernel[vertical * 3 + horizontal]
                * padded[:, vertical : vertical + grid_side, horizontal : horizontal + grid_side]
            )
    return total


def depthwise_back(field, grad_field, kernel):
    grid_side = field.shape[1]
    padded_in = jnp.pad(field, ((0, 0), (1, 1), (1, 1), (0, 0)))
    padded_grad = jnp.pad(grad_field, ((0, 0), (1, 1), (1, 1), (0, 0)))
    input_grad = jnp.zeros_like(field)
    kernel_rows = []
    for vertical in range(3):
        for horizontal in range(3):
            input_grad = (
                input_grad
                + kernel[vertical * 3 + horizontal]
                * padded_grad[
                    :,
                    2 - vertical : 2 - vertical + grid_side,
                    2 - horizontal : 2 - horizontal + grid_side,
                ]
            )
            kernel_rows.append(
                jnp.sum(
                    grad_field
                    * padded_in[
                        :, vertical : vertical + grid_side, horizontal : horizontal + grid_side
                    ],
                    axis=(0, 1, 2),
                )
            )
    return (input_grad, jnp.stack(kernel_rows))


def to_groups(values, items_here):
    half_side = SIDE // 2
    trailing = values.shape[1:]
    shaped = values.reshape((items_here, half_side, 2, half_side, 2) + trailing)
    axes_order = (0, 2, 4, 1, 3) + tuple(range(5, 5 + len(trailing)))
    return shaped.transpose(axes_order).reshape((items_here * 4, half_side * half_side) + trailing)


def from_groups(values, items_here):
    half_side = SIDE // 2
    trailing = values.shape[2:]
    shaped = values.reshape((items_here, 2, 2, half_side, half_side) + trailing)
    axes_order = (0, 3, 1, 4, 2) + tuple(range(5, 5 + len(trailing)))
    return shaped.transpose(axes_order).reshape((items_here * SIDE * SIDE,) + trailing)


def split_project(project, items_here):
    grouped = to_groups(project.reshape(project.shape[0], 3, -1, HEAD_DIM), items_here)
    return (grouped[:, :, 0], grouped[:, :, 1], grouped[:, :, 2])


def attend(project, items_here):
    query, keys, vals = split_project(project, items_here)
    scores = (
        jnp.einsum("bqhd,bkhd->bhqk", query, keys, preferred_element_type=jnp.float32) * score_scale
    )
    top_score = jnp.max(scores, axis=-1, keepdims=True)
    log_total = top_score + jnp.log(jnp.sum(jnp.exp(scores - top_score), axis=-1, keepdims=True))
    probs_low = jnp.exp(scores - log_total).astype(jnp.bfloat16)
    attended = jnp.einsum("bhqk,bkhd->bqhd", probs_low, vals, preferred_element_type=jnp.float32)
    merged = from_groups(attended, items_here)
    return (merged.reshape(merged.shape[0], -1).astype(jnp.bfloat16), log_total)


def attend_back(project, log_total, grad_attended, items_here):
    query, keys, vals = split_project(project, items_here)
    grad_grouped = to_groups(
        grad_attended.reshape(grad_attended.shape[0], -1, HEAD_DIM), items_here
    )
    scores = (
        jnp.einsum("bqhd,bkhd->bhqk", query, keys, preferred_element_type=jnp.float32) * score_scale
    )
    probs = jnp.exp(scores - log_total)
    probs_low = probs.astype(jnp.bfloat16)
    grad_probs = jnp.einsum(
        "bqhd,bkhd->bhqk", grad_grouped, vals, preferred_element_type=jnp.float32
    )
    grad_scores = (
        probs * (grad_probs - jnp.sum(probs * grad_probs, axis=-1, keepdims=True))
    ).astype(jnp.bfloat16)
    grad_query = (
        jnp.einsum("bhqk,bkhd->bqhd", grad_scores, keys, preferred_element_type=jnp.float32)
        * score_scale
    )
    grad_keys = (
        jnp.einsum("bhqk,bqhd->bkhd", grad_scores, query, preferred_element_type=jnp.float32)
        * score_scale
    )
    grad_vals = jnp.einsum(
        "bhqk,bqhd->bkhd", probs_low, grad_grouped, preferred_element_type=jnp.float32
    )
    stacked = jnp.stack([grad_query, grad_keys, grad_vals], axis=2).astype(jnp.bfloat16)
    merged = from_groups(stacked, items_here)
    return merged.reshape(merged.shape[0], 3, -1)


def contract_last(left, right):
    return lax.dot_general(
        left, right, (((1,), (1,)), ((), ())), preferred_element_type=jnp.float32
    )


def contract_first(left, right):
    return lax.dot_general(
        left, right, (((0,), (0,)), ((), ())), preferred_element_type=jnp.float32
    )


def spread_rows(row_hot, table):
    return jnp.dot(row_hot, table, precision=highest, preferred_element_type=jnp.float32)


def item_sums(row_hot, values):
    return lax.dot_general(
        row_hot,
        values,
        (((0,), (0,)), ((), ())),
        precision=highest,
        preferred_element_type=jnp.float32,
    )


def shards(
    tokens,
    cotangent,
    item_count,
    timestep,
    class_id,
    class_table,
    w_mod,
    b_mod,
    k_att,
    w_qkv,
    w_out,
    b_out,
    w_up,
    b_up,
    k_ffn,
    w_down,
    b_down,
):
    items_here = timestep.shape[0]
    total_rows = tokens.shape[0]
    width = tokens.shape[1]
    item_rows = total_rows // items_here
    share_rows = total_rows // lax.axis_size("tensor")
    share_start = lax.axis_index("tensor") * share_rows
    live = (jnp.arange(items_here) < item_count[0]).astype(jnp.float32)
    row_item = (share_start + jnp.arange(share_rows)) // item_rows
    row_hot = (row_item[:, None] == jnp.arange(items_here)[None, :]).astype(jnp.float32)
    live_rows = spread_rows(row_hot, live[:, None])
    k_att_f = k_att.astype(jnp.float32)
    k_ffn_f = k_ffn.astype(jnp.float32)
    one_hot = class_id[:, None] == jnp.arange(class_table.shape[0])[None, :]
    cond = time_features(timestep, width) + jnp.dot(
        one_hot.astype(jnp.bfloat16), class_table, preferred_element_type=jnp.float32
    )
    act_low = jax.nn.silu(cond).astype(jnp.bfloat16)
    modulate = contract_last(act_low, w_mod) + b_mod.astype(jnp.float32)
    pieces = jnp.split(modulate, 6, axis=1)
    shift_att = pieces[0][:, None, :]
    scale_att = pieces[1][:, None, :]
    scale_att_rows = spread_rows(row_hot, pieces[1])
    gate_att_rows = spread_rows(row_hot, pieces[2])
    shift_ffn_rows = spread_rows(row_hot, pieces[3])
    scale_ffn_rows = spread_rows(row_hot, pieces[4])
    gate_ffn_rows = spread_rows(row_hot, pieces[5])
    x_flat = tokens.astype(jnp.float32)
    x_items = x_flat.reshape(items_here, item_rows, width)

    def forward_pass(source):
        normed = layer_norm(source)
        shaped = normed * (1.0 + scale_att) + shift_att
        mixed = (
            depthwise(shaped.reshape(items_here, SIDE, SIDE, width), k_att_f)
            .reshape(total_rows, width)
            .astype(jnp.bfloat16)
        )
        project = jnp.einsum(
            "td,dcj->tcj", mixed, w_qkv, preferred_element_type=jnp.float32
        ).astype(jnp.bfloat16)
        attended, log_total = attend(project, items_here)
        branch = lax.psum_scatter(
            contract_last(attended, w_out).astype(jnp.bfloat16),
            "tensor",
            scatter_dimension=0,
            tiled=True,
        ).astype(jnp.float32) + b_out.astype(jnp.float32)
        source_share = lax.dynamic_slice_in_dim(
            source.reshape(total_rows, width), share_start, share_rows, 0
        )
        middle = source_share + gate_att_rows * branch
        normed_ffn = layer_norm(middle)
        shaped_share = (normed_ffn * (1.0 + scale_ffn_rows) + shift_ffn_rows).astype(jnp.bfloat16)
        shaped_ffn = lax.all_gather(shaped_share, "tensor", axis=0, tiled=True)
        hidden = jnp.dot(shaped_ffn, w_up, preferred_element_type=jnp.float32) + b_up.astype(
            jnp.float32
        )
        convolved = depthwise(hidden.reshape(items_here, SIDE, SIDE, -1), k_ffn_f).reshape(
            total_rows, -1
        )
        activated = jax.nn.gelu(convolved).astype(jnp.bfloat16)
        branch_ffn = lax.psum_scatter(
            contract_last(activated, w_down).astype(jnp.bfloat16),
            "tensor",
            scatter_dimension=0,
            tiled=True,
        ).astype(jnp.float32) + b_down.astype(jnp.float32)
        result = middle + gate_ffn_rows * branch_ffn
        return (
            normed,
            shaped,
            mixed,
            project,
            attended,
            log_total,
            branch,
            middle,
            normed_ffn,
            shaped_ffn,
            hidden,
            convolved,
            activated,
            branch_ffn,
            result,
        )

    saved = forward_pass(x_items)
    block_out = (saved[14] * live_rows).astype(jnp.bfloat16)
    again = lax.optimization_barrier((x_items, block_out))[0]
    saved = forward_pass(again)
    (
        normed,
        shaped,
        mixed,
        project,
        attended,
        log_total,
        branch,
        middle,
        normed_ffn,
        shaped_ffn,
        hidden,
        convolved,
        activated,
        branch_ffn,
        result,
    ) = saved
    cot_share = lax.dynamic_slice_in_dim(cotangent, share_start, share_rows, 0)
    grad_out = cot_share.astype(jnp.float32) * live_rows
    grad_gate_ffn = item_sums(row_hot, grad_out * branch_ffn)
    grad_branch_share = (grad_out * gate_ffn_rows).astype(jnp.bfloat16)
    grad_branch_ffn = lax.all_gather(grad_branch_share, "tensor", axis=0, tiled=True)
    grad_b_down = jnp.sum(grad_branch_ffn.astype(jnp.float32), axis=0)
    grad_w_down = contract_first(grad_branch_ffn, activated)
    grad_activated = jnp.dot(grad_branch_ffn, w_down, preferred_element_type=jnp.float32)
    gelu_value, gelu_back = jax.vjp(jax.nn.gelu, convolved)
    grad_convolved = gelu_back(grad_activated)[0]
    grad_hidden, grad_k_ffn = depthwise_back(
        hidden.reshape(items_here, SIDE, SIDE, -1),
        grad_convolved.reshape(items_here, SIDE, SIDE, -1),
        k_ffn_f,
    )
    grad_hidden = grad_hidden.reshape(total_rows, -1).astype(jnp.bfloat16)
    grad_b_up = jnp.sum(grad_hidden.astype(jnp.float32), axis=0)
    grad_w_up = contract_first(shaped_ffn, grad_hidden)
    grad_shaped_ffn = lax.psum_scatter(
        contract_last(grad_hidden, w_up).astype(jnp.bfloat16),
        "tensor",
        scatter_dimension=0,
        tiled=True,
    ).astype(jnp.float32)
    grad_scale_ffn = item_sums(row_hot, grad_shaped_ffn * normed_ffn)
    grad_shift_ffn = item_sums(row_hot, grad_shaped_ffn)
    norm_value, norm_back_ffn = jax.vjp(layer_norm, middle)
    grad_middle = grad_out + norm_back_ffn(grad_shaped_ffn * (1.0 + scale_ffn_rows))[0]
    grad_gate_att = item_sums(row_hot, grad_middle * branch)
    grad_attn_share = (grad_middle * gate_att_rows).astype(jnp.bfloat16)
    grad_branch = lax.all_gather(grad_attn_share, "tensor", axis=0, tiled=True)
    grad_b_out = jnp.sum(grad_branch.astype(jnp.float32), axis=0)
    grad_w_out = contract_first(grad_branch, attended)
    grad_attended = jnp.dot(grad_branch, w_out, preferred_element_type=jnp.float32).astype(
        jnp.bfloat16
    )
    grad_project = attend_back(project, log_total, grad_attended, items_here)
    grad_w_qkv = jnp.einsum("td,tcj->dcj", mixed, grad_project, preferred_element_type=jnp.float32)
    grad_mixed_share = lax.psum_scatter(
        jnp.einsum("tcj,dcj->td", grad_project, w_qkv, preferred_element_type=jnp.float32).astype(
            jnp.bfloat16
        ),
        "tensor",
        scatter_dimension=0,
        tiled=True,
    )
    grad_mixed = lax.all_gather(grad_mixed_share, "tensor", axis=0, tiled=True).astype(jnp.float32)
    grad_shaped, grad_k_att = depthwise_back(
        shaped.reshape(items_here, SIDE, SIDE, width),
        grad_mixed.reshape(items_here, SIDE, SIDE, width),
        k_att_f,
    )
    grad_shaped_share = lax.dynamic_slice_in_dim(
        grad_shaped.reshape(total_rows, width), share_start, share_rows, 0
    )
    normed_share = lax.dynamic_slice_in_dim(
        normed.reshape(total_rows, width), share_start, share_rows, 0
    )
    grad_scale_att = item_sums(row_hot, grad_shaped_share * normed_share)
    grad_shift_att = item_sums(row_hot, grad_shaped_share)
    x_share = lax.dynamic_slice_in_dim(x_flat, share_start, share_rows, 0)
    norm_first, norm_back_att = jax.vjp(layer_norm, x_share)
    grad_tokens = grad_middle + norm_back_att(grad_shaped_share * (1.0 + scale_att_rows))[0]
    mod_partial = jnp.concatenate(
        [
            grad_shift_att,
            grad_scale_att,
            grad_gate_att,
            grad_shift_ffn,
            grad_scale_ffn,
            grad_gate_ffn,
        ],
        axis=1,
    )
    grad_modulate = lax.psum(mod_partial, "tensor").astype(jnp.bfloat16)
    grad_b_mod = jnp.sum(grad_modulate.astype(jnp.float32), axis=0)
    grad_w_mod = contract_first(grad_modulate, act_low)
    grad_act = jnp.dot(grad_modulate, w_mod, preferred_element_type=jnp.float32)
    silu_value, silu_back = jax.vjp(jax.nn.silu, cond)
    grad_cond = silu_back(grad_act)[0]
    grad_class = lax.dot_general(
        one_hot.astype(jnp.float32),
        grad_cond,
        (((0,), (0,)), ((), ())),
        precision=highest,
        preferred_element_type=jnp.float32,
    )
    summed_qkv, summed_out, summed_up, summed_down, summed_mod = (
        lax.psum_scatter(grad_w_qkv, "dp", scatter_dimension=0, tiled=True),
        lax.psum_scatter(grad_w_out, "dp", scatter_dimension=0, tiled=True),
        lax.psum_scatter(grad_w_up, "dp", scatter_dimension=0, tiled=True),
        lax.psum_scatter(grad_w_down, "dp", scatter_dimension=0, tiled=True),
        lax.psum_scatter(grad_w_mod, "dp", scatter_dimension=0, tiled=True),
    )
    small_sums = lax.psum(
        (grad_k_att, grad_k_ffn, grad_b_up, grad_b_out, grad_b_down, grad_b_mod, grad_class), "dp"
    )
    (
        summed_k_att,
        summed_k_ffn,
        summed_b_up,
        summed_b_out,
        summed_b_down,
        summed_b_mod,
        summed_class,
    ) = small_sums
    return (
        block_out,
        grad_tokens,
        summed_class,
        summed_mod,
        summed_b_mod,
        summed_k_att,
        summed_qkv,
        summed_out,
        summed_b_out,
        summed_up,
        summed_b_up,
        summed_k_ffn,
        summed_down,
        summed_b_down,
    )


def solution(mesh):
    placed = (
        P("dp", None),
        P("dp", None),
        P("dp"),
        P("dp"),
        P("dp"),
        P(),
        P(),
        P(),
        P(),
        P(None, None, "tensor"),
        P(None, "tensor"),
        P(),
        P(None, "tensor"),
        P("tensor"),
        P(None, "tensor"),
        P(None, "tensor"),
        P(),
    )
    return jax.shard_map(
        shards,
        mesh=mesh,
        in_specs=placed,
        out_specs=(
            P(("dp", "tensor"), None),
            P(("dp", "tensor"), None),
            P(),
            P("dp", None),
            P(),
            P(),
            P("dp", None, "tensor"),
            P("dp", "tensor"),
            P(),
            P("dp", "tensor"),
            P("tensor"),
            P(None, "tensor"),
            P("dp", "tensor"),
            P(),
        ),
        check_vma=False,
    )
```

profile of v0, /device:TPU:0, one launch (start us, length us, event | category | flops | bytes accessed | tf_op | source)
XLA Modules:
  0.0 1077.7 jit_solution(4446822066755356792)
XLA Ops:
  27.6 5.4 reshape_reshape.15
  42.9 27.1 %reduce-scatter.12.cloned.1.call-done = bf16[256,768]{1,0:T(8,128)(2,1)} async-done(((bf16[1024,768]{1,0:T(8,128)(2,1)}), bf16[256,768]{1,0:T(8,128)(2,1)}) %reduce-scatter.12.cloned.1.call-update) | async-done | bytes 393232 | tf_op jit(solution)/shard_map/reduce_scatter | solution.py:224
  76.5 19.5 %all-gather.6.cloned.1.call-done = bf16[1024,768]{1,0:T(8,128)(2,1)} async-done(((bf16[256,768]{1,0:T(8,128)(2,1)}), bf16[1024,768]{1,0:T(8,128)(2,1)}) %all-gather.6.cloned.1.call-update) | async-done | bytes 1572880 | tf_op jit(solution)/shard_map/all_gather | solution.py:236
  110.6 25.3 %reduce-scatter.14.cloned.1.call-done = bf16[256,768]{1,0:T(8,128)(2,1)} async-done(((bf16[1024,768]{1,0:T(8,128)(2,1)}), bf16[256,768]{1,0:T(8,128)(2,1)}) %reduce-scatter.14.cloned.1.call-update) | async-done | bytes 393232 | tf_op jit(solution)/shard_map/reduce_scatter | solution.py:244
  149.2 5.4 reshape_reshape.16
  167.4 28.3 %reduce-scatter.16.cloned.1.call-done = bf16[256,768]{1,0:T(8,128)(2,1)} async-done(((bf16[1024,768]{1,0:T(8,128)(2,1)}), bf16[256,768]{1,0:T(8,128)(2,1)}) %reduce-scatter.16.cloned.1.call-update) | async-done | bytes 393232 | tf_op jit(solution)/shard_map/reduce_scatter | solution.py:224
  200.1 18.9 %all-gather.10.cloned.1.call-done = bf16[1024,768]{1,0:T(8,128)(2,1)} async-done(((bf16[256,768]{1,0:T(8,128)(2,1)}), bf16[1024,768]{1,0:T(8,128)(2,1)}) %all-gather.10.cloned.1.call-update) | async-done | bytes 1572880 | tf_op jit(solution)/shard_map/all_gather | solution.py:236
  223.9 5.7 multiply_add_fusion
  229.6 10.6 all-gather.8.cloned.1.call-done
  240.2 8.5 multiply_reduce_fusion.4
  250.4 5.1 convert_reduce_fusion.1
  259.3 28.3 %reduce-scatter.18.cloned.1.call-done = bf16[256,768]{1,0:T(8,128)(2,1)} async-done(((bf16[1024,768]{1,0:T(8,128)(2,1)}), bf16[256,768]{1,0:T(8,128)(2,1)}) %reduce-scatter.18.cloned.1.call-update) | async-done | bytes 393232 | tf_op jit(solution)/shard_map/reduce_scatter | solution.py:308
  294.1 19.6 %all-gather.12.cloned.1.call-done = bf16[1024,768]{1,0:T(8,128)(2,1)} async-done(((bf16[256,768]{1,0:T(8,128)(2,1)}), bf16[1024,768]{1,0:T(8,128)(2,1)}) %all-gather.12.cloned.1.call-update) | async-done | bytes 1572880 | tf_op jit(solution)/shard_map/all_gather | solution.py:320
  339.5 28.3 %reduce-scatter.20.cloned.1.call-done = bf16[256,768]{1,0:T(8,128)(2,1)} async-done(((bf16[1024,768]{1,0:T(8,128)(2,1)}), bf16[256,768]{1,0:T(8,128)(2,1)}) %reduce-scatter.20.cloned.1.call-update) | async-done | bytes 393232 | tf_op jit(solution)/shard_map/reduce_scatter | solution.py:328
  400.9 18.9 %reduce-scatter.22.cloned.1.call-done = bf16[256,768]{1,0:T(8,128)(2,1)} async-done(((bf16[1024,768]{1,0:T(8,128)(2,1)}), bf16[256,768]{1,0:T(8,128)(2,1)}) %reduce-scatter.22.cloned.1.call-update) | async-done | bytes 393232 | tf_op jit(solution)/shard_map/reduce_scatter | solution.py:244
  421.5 11.8 %psum.56 = bf16[1,4608]{1,0:T(2,128)(2,1)S(1)} all-reduce(f32[1,4608]{1,0:T(1,128)S(1)} %convolution_dynamic-update-slice_fusion.1), channel_id=1, replica_groups=mesh['dp'=8,'tensor'=4] {'tensor'}, use_global_device_ids=true, to_apply=%region_25.26 | all-reduce | flops 4608 | bytes 27648 | tf_op jit(solution)/shard_map/psum | solution.py:364
  439.7 6.0 broadcast_multiply_fusion
  446.7 13.3 %multiply_reduce_fusion = (f32[768]{0:T(1024)S(1)}, f32[768]{0:T(1024)S(1)}, f32[768]{0:T(1024)S(1)}, f32[768]{0:T(1024)S(1)}, f32[768]{0:T(1024)S(1)}, /*index=...) fusion(f32[1,32,32,768]{3,2,1,0:T(8,128)} %bitcast.206, f32[1024,768]{1,0:T(8,128)} %copy-done.11), kind=kLoop, calls=%fused_computation.141 | loop fusion | flops 12576768 | bytes 6316032 | tf_op jit(solution)/shard_map/reduce_sum | solution.py:61
  468.2 40.3 %all-reduce.11 = (f32[4608]{0:T(1024)}, f32[9,768]{1,0:T(8,128)}, f32[768]{0:T(1024)}, f32[768]{0:T(1024)}, f32[9,768]{1,0:T(8,128)}, /*index=5*/f32[768]{0:T(1024)}) all-reduce(bf16[4608]{0:T(1024)(128)(2,1)S(1)} %convert_reduce_fusion.4, f32[9,768]{1,0:T(8,128)S(1)} %stack.85, ...), channel_id=1, replica_groups=mesh['dp'=8,'tensor'=4] {'dp'}, use_global_device_ids=true, to_apply=%region_28.29 | all-reduce | flops 20736 | bytes 156672 | tf_op jit(solution)/shard_map/psum | solution.py:384
  514.3 51.2 %reduce-scatter.32.cloned.1.call-done = f32[96,768]{1,0:T(8,128)} async-done(((f32[768,768]{1,0:T(8,128)}), f32[96,768]{1,0:T(8,128)}) %reduce-scatter.32.cloned.1.call-update) | async-done | bytes 294928 | tf_op jit(solution)/shard_map/reduce_scatter | solution.py:381
  565.5 65.3 %reduce-scatter.28.cloned.1.call-done = f32[96,192]{1,0:T(8,128)} async-done(((f32[768,192]{1,0:T(8,128)}), f32[96,192]{1,0:T(8,128)}) %reduce-scatter.28.cloned.1.call-update) | async-done | bytes 73744 | tf_op jit(solution)/shard_map/reduce_scatter | solution.py:379
  630.8 72.3 %reduce-scatter.26.cloned.1.call-done = f32[96,3,192]{2,0,1:T(8,128)} async-done(((f32[768,3,192]{2,0,1:T(8,128)}), f32[96,3,192]{2,0,1:T(8,128)}) %reduce-scatter.26.cloned.1.call-update) | async-done | bytes 221200 | tf_op jit(solution)/shard_map/reduce_scatter | solution.py:378
  703.1 131.2 %all-reduce.10.cloned.1.call-done = f32[1001,768]{1,0:T(8,128)} async-done(((f32[1001,768]{1,0:T(8,128)}), f32[1001,768]{1,0:T(8,128)}) %all-reduce.10.cloned.1.call-update) | async-done | bytes 3075088 | tf_op jit(solution)/shard_map/psum | solution.py:384
  834.2 233.0 %reduce-scatter.24.cloned.1.call-done = f32[576,768]{1,0:T(8,128)} async-done(((f32[4608,768]{1,0:T(8,128)}), f32[576,768]{1,0:T(8,128)}) %reduce-scatter.24.cloned.1.call-update) | async-done | bytes 1769488 | tf_op jit(solution)/shard_map/reduce_scatter | solution.py:382
  (423 shorter events, 180.2 us)
Async XLA Ops:
  7.2 62.8 %reduce-scatter.12.cloned.1.call-start = ((), (), s32[]{:S(2)}) async-start(), calls=%async_computation.11 | async-start | bytes 1966080 | tf_op jit(solution)/shard_map/reduce_scatter | solution.py:224
  19.2 116.7 %copy-start.29 = (f32[768]{0:T(1024)}, f32[768]{0:T(1024)S(1)}, u32[]{:S(2)}) copy-start(f32[768]{0:T(1024)S(1)} %get-tuple-element.59) | copy-start | bytes 9220
  19.5 122.3 %copy-start.56 = (f32[768]{0:T(1024)}, f32[768]{0:T(1024)S(1)}, u32[]{:S(2)}) copy-start(f32[768]{0:T(1024)S(1)} %get-tuple-element.45) | copy-start | bytes 9220
  39.0 57.0 %all-gather.6.cloned.1.call-start = ((), (), s32[]{:S(2)}) async-start(), calls=%async_computation.12 | async-start | bytes 1966080 | tf_op jit(solution)/shard_map/all_gather | solution.py:236
  39.4 96.5 %copy-start.26 = (f32[768]{0:T(1024)}, f32[768]{0:T(1024)S(1)}, u32[]{:S(2)}) copy-start(f32[768]{0:T(1024)S(1)} %convert_element_type.211) | copy-start | bytes 9220
  39.4 96.5 %copy-start.31 = (f32[256]{0:T(256)}, f32[256]{0:T(256)S(1)}, u32[]{:S(2)}) copy-start(f32[256]{0:T(256)S(1)} %fusion.141) | copy-start | bytes 3076
  42.9 96.5 %copy-start.2 = (f32[1,1024,768]{2,1,0:T(8,128)}, f32[1,1024,768]{2,1,0:T(8,128)S(1)}, u32[]{:S(2)}) copy-start(f32[1,1024,768]{2,1,0:T(8,128)S(1)} %get-tuple-element.15) | copy-start | bytes 9437188
  76.2 59.7 %reduce-scatter.14.cloned.1.call-start = ((), (), s32[]{:S(2)}) async-start(), calls=%async_computation.13 | async-start | bytes 1966080 | tf_op jit(solution)/shard_map/reduce_scatter | solution.py:244
  107.6 88.1 %reduce-scatter.16.cloned.1.call-start = ((), (), s32[]{:S(2)}) async-start(), calls=%async_computation.15 | async-start | bytes 1966080 | tf_op jit(solution)/shard_map/reduce_scatter | solution.py:224
  167.4 51.6 %all-gather.10.cloned.1.call-start = ((), (), s32[]{:S(2)}) async-start(), calls=%async_computation.16 | async-start | bytes 1966080 | tf_op jit(solution)/shard_map/all_gather | solution.py:236
  197.3 92.0 %copy-start.82 = (f32[256]{0:T(256)}, f32[256]{0:T(256)S(1)}, u32[]{:S(2)}) copy-start(f32[256]{0:T(256)S(1)} %broadcast_multiply_fusion.5) | copy-start | bytes 3076
  199.2 41.0 %all-gather.8.cloned.1.call-start = ((), (), s32[]{:S(2)}) async-start(), calls=%async_computation.14 | async-start | bytes 1966080 | tf_op jit(solution)/shard_map/all_gather | solution.py:294
  199.9 87.7 %reduce-scatter.18.cloned.1.call-start = ((), (), s32[]{:S(2)}) async-start(), calls=%async_computation.17 | async-start | bytes 1966080 | tf_op jit(solution)/shard_map/reduce_scatter | solution.py:308
  259.3 54.4 %all-gather.12.cloned.1.call-start = ((), (), s32[]{:S(2)}) async-start(), calls=%async_computation.18 | async-start | bytes 1966080 | tf_op jit(solution)/shard_map/all_gather | solution.py:320
  293.8 73.9 %reduce-scatter.20.cloned.1.call-start = ((), (), s32[]{:S(2)}) async-start(), calls=%async_computation.19 | async-start | bytes 1966080 | tf_op jit(solution)/shard_map/reduce_scatter | solution.py:328
  339.4 49.5 %all-gather.14.cloned.1.call-start = ((), (), s32[]{:S(2)}) async-start(), calls=%async_computation.20 | async-start | bytes 1966080 | tf_op jit(solution)/shard_map/all_gather | solution.py:336
  367.8 52.0 %reduce-scatter.22.cloned.1.call-start = ((), (), s32[]{:S(2)}) async-start(), calls=%async_computation.21 | async-start | bytes 1966080 | tf_op jit(solution)/shard_map/reduce_scatter | solution.py:244
  370.4 143.9 %reduce-scatter.30.cloned.1.call-start = ((), (), s32[]{:S(2)}) async-start(), calls=%async_computation.26 | async-start | bytes 2654208 | tf_op jit(solution)/shard_map/reduce_scatter | solution.py:380
  375.6 189.8 %reduce-scatter.32.cloned.1.call-start = ((), (), s32[]{:S(2)}) async-start(), calls=%async_computation.27 | async-start | bytes 2654208 | tf_op jit(solution)/shard_map/reduce_scatter | solution.py:381
  380.1 250.7 %reduce-scatter.28.cloned.1.call-start = ((), (), s32[]{:S(2)}) async-start(), calls=%async_computation.25 | async-start | bytes 884736 | tf_op jit(solution)/shard_map/reduce_scatter | solution.py:379
  383.1 319.9 %reduce-scatter.26.cloned.1.call-start = ((), (), s32[]{:S(2)}) async-start(), calls=%async_computation.24 | async-start | bytes 2654208 | tf_op jit(solution)/shard_map/reduce_scatter | solution.py:378
  388.0 446.3 %all-reduce.10.cloned.1.call-start = ((), (), s32[]{:S(2)}) async-start(), calls=%async_computation.22 | async-start | bytes 6193152 | tf_op jit(solution)/shard_map/psum | solution.py:384
  439.4 627.9 %reduce-scatter.24.cloned.1.call-start = ((), (), s32[]{:S(2)}) async-start(), calls=%async_computation.23 | async-start | bytes 15925248 | tf_op jit(solution)/shard_map/reduce_scatter | solution.py:382
  512.0 559.0 %copy-start.1 = (bf16[1001,768]{1,0:T(8,128)(2,1)S(1)}, bf16[1001,768]{1,0:T(8,128)(2,1)}, u32[]{:S(2)}) copy-start(bf16[1001,768]{1,0:T(8,128)(2,1)} %param.22) | copy-start | bytes 4612612
  (113 other events, 1560.4 us)
Sparse Core Ops, SparseCore 0:
  39.1 30.8 reduce-scatter.11
  76.3 19.6 all-gather.5
  107.7 28.1 reduce-scatter.13
  167.5 28.1 reduce-scatter.15
  199.3 19.6 all-gather.9
  220.5 19.6 all-gather.7
  259.4 28.1 reduce-scatter.17
  294.0 19.6 all-gather.11
  339.6 28.1 reduce-scatter.19
  369.2 19.6 all-gather.13
  391.6 28.1 reduce-scatter.21
  423.7 69.4 reduce-scatter.29
  497.3 68.1 reduce-scatter.31
  569.2 61.5 reduce-scatter.27
  635.1 67.8 reduce-scatter.25
  707.6 126.5 all-reduce.9
  838.8 228.4 reduce-scatter.23
where the time goes:
time: 1090 us; the launch traced here: 1080 us
  waiting for transfers between devices  779 us (71%)
  other arithmetic  99.6 us (9%)
  matrix products  75 us (7%)
  blocking collectives  52.1 us (5%)
  local copies, waits for them, and re-layouts  51.1 us (5%)
  between operations  18.2 us (2%)
    reduce_scatter x1, waiting for transfers between devices, shards(): lax.psum_scatter(grad_w_mod, 'dp', scatter_dimension=0, tiled=True)  233 us
    psum x1, waiting for transfers between devices, shards(): lax.psum((grad_k_att, grad_k_ffn, grad_b_up, grad_b_out, grad_b_down, gra...  131 us
    reduce_scatter x1, waiting for transfers between devices, shards(): lax.psum_scatter(grad_w_qkv, 'dp', scatter_dimension=0, tiled=True)  72.3 us
    reduce_scatter x1, waiting for transfers between devices, shards(): lax.psum_scatter(grad_w_out, 'dp', scatter_dimension=0, tiled=True)  65.3 us
    reduce_scatter x2, waiting for transfers between devices, forward_pass(): lax.psum_scatter(contract_last(attended, w_out).astype(jnp.bfloat16), 'te...  55.4 us
    reduce_scatter x1, waiting for transfers between devices, shards(): lax.psum_scatter(grad_w_down, 'dp', scatter_dimension=0, tiled=True)  51.2 us
    reduce_scatter x2, waiting for transfers between devices, forward_pass(): lax.psum_scatter(contract_last(activated, w_down).astype(jnp.bfloat16), '...  44.2 us
    psum x1, blocking collectives, shards(): lax.psum((grad_k_att, grad_k_ffn, grad_b_up, grad_b_out, grad_b_down, gra...  40.3 us
  transfers between devices with their start and end apart: 17, of which 16 were waited for; matrix products, arithmetic and copies ran while one was open for 8% of the time, Pallas kernels for 0%

commit v1 on v0

v1 whole, which is shorter than its diff:
```python
import math

import jax
import jax.numpy as jnp
from jax import lax
from jax.sharding import PartitionSpec as P

HEAD_DIM = 64
SIDE = 32
HALF = SIDE // 2
ITEM = SIDE * SIDE

norm_eps = 1e-06
score_scale = 0.125
highest = lax.Precision.HIGHEST
f32 = jnp.float32
bf16 = jnp.bfloat16


def swap(values, axis, bit):
    size = lax.axis_size(axis)
    return lax.ppermute(values, axis, [(i, i ^ bit) for i in range(size)])


def bits_of(axis):
    return [1 << b for b in range(lax.axis_size(axis).bit_length() - 1)]


def take(values, index):
    return lax.dynamic_index_in_dim(values, index, 0, keepdims=False)


def add_low(left, right):
    return (left.astype(f32) + right.astype(f32)).astype(bf16)


def scatter_sum(grad):
    size = lax.axis_size("dp")
    here = lax.axis_index("dp")
    held = grad.reshape((size, grad.shape[0] // size) + grad.shape[1:])
    for bit in bits_of("dp"):
        mine = (here // bit) % 2
        halves = held.reshape((held.shape[0] // 2, 2) + held.shape[1:])
        sent = lax.dynamic_index_in_dim(halves, 1 - mine, 1, keepdims=False).astype(bf16)
        kept = lax.dynamic_index_in_dim(halves, mine, 1, keepdims=False)
        held = kept.astype(f32) + swap(sent, "dp", bit).astype(f32)
    return held[0]


def butterfly(values, axis):
    for bit in bits_of(axis):
        values = values + swap(values, axis, bit)
    return values


def gather_xor(values):
    for bit in bits_of("dp"):
        values = jnp.concatenate([values, swap(values, "dp", bit)], axis=0)
    return values


def tree_sum(values):
    while values.shape[0] > 1:
        values = values[0::2] + values[1::2]
    return values[0]


def layer_norm(values):
    center = values - jnp.mean(values, axis=-1, keepdims=True)
    return center * lax.rsqrt(jnp.mean(center * center, axis=-1, keepdims=True) + norm_eps)


def time_features(timestep, width):
    half_width = width // 2
    freqs = jnp.exp(-math.log(10000.0) * jnp.arange(half_width, dtype=f32) / half_width)
    angles = timestep.astype(f32)[:, None] * freqs[None, :]
    return jnp.concatenate([jnp.cos(angles), jnp.sin(angles)], axis=1)


def depthwise(field, kernel):
    rows, cols = field.shape[:2]
    padded = jnp.pad(field, ((1, 1), (1, 1), (0, 0)))
    total = jnp.zeros_like(field)
    for a in range(3):
        for b in range(3):
            total = total + kernel[a * 3 + b] * padded[a : a + rows, b : b + cols]
    return total


def depthwise_back(field, grad_rows, kernel):
    rows, cols = field.shape[:2]
    padded = jnp.pad(grad_rows, ((0, 0), (1, 1), (0, 0)))
    total = jnp.zeros_like(field)
    kernel_rows = []
    for a in range(3):
        for b in range(3):
            seen = padded[2 - a : 2 - a + rows, 2 - b : 2 - b + cols]
            total = total + kernel[a * 3 + b] * seen
            kernel_rows.append(jnp.sum(field * seen, axis=(0, 1)))
    return (total, jnp.stack(kernel_rows))


def to_groups(values, rows):
    width = values.shape[-1]
    shaped = values.reshape((rows // 2, 2, HALF, 2, width))
    return shaped.transpose((1, 3, 0, 2, 4)).reshape((rows * SIDE, width))


def from_groups(values, rows):
    width = values.shape[-1]
    shaped = values.reshape((2, 2, rows // 2, HALF, width))
    return shaped.transpose((2, 0, 3, 1, 4)).reshape((rows * SIDE, width))


def to_halves(values):
    width = values.shape[-1]
    shaped = values.reshape((4, 2, 2, 64, width))
    return shaped.transpose((2, 1, 0, 3, 4)).reshape((2, ITEM // 2, width))


def from_halves(own, other, core):
    width = own.shape[-1]
    both = jnp.stack([jnp.where(core == 0, own, other), jnp.where(core == 0, other, own)])
    shaped = both.reshape((2, 2, 4, 64, width))
    return shaped.transpose((2, 1, 0, 3, 4)).reshape((ITEM, width))


def dot_nn(left, right):
    return lax.dot_general(left, right, (((1,), (0,)), ((), ())), preferred_element_type=f32)


def dot_nt(left, right):
    return lax.dot_general(left, right, (((1,), (1,)), ((), ())), preferred_element_type=f32)


def dot_tn(left, right):
    return lax.dot_general(left, right, (((0,), (0,)), ((), ())), preferred_element_type=f32)


def split_heads(values):
    return values.reshape(4, ITEM // 4, -1, HEAD_DIM)


def stage_a(tokens, mods, k_att, w_qkv, w_out):
    shaped = layer_norm(tokens.astype(f32)) * (1.0 + mods[1]) + mods[0]
    mixed = depthwise(shaped.reshape(SIDE, SIDE, -1), k_att.astype(f32))
    mixed = to_groups(mixed.reshape(ITEM, -1).astype(bf16), SIDE)
    project = [dot_nn(mixed, w_qkv[:, kind]).astype(bf16) for kind in range(3)]
    query, keys, vals = (split_heads(p) for p in project)
    scores = jnp.einsum("bqhd,bkhd->bhqk", query, keys, preferred_element_type=f32) * score_scale
    top = jnp.max(scores, axis=-1, keepdims=True)
    log_total = top + jnp.log(jnp.sum(jnp.exp(scores - top), axis=-1, keepdims=True))
    probs_low = jnp.exp(scores - log_total).astype(bf16)
    attended = jnp.einsum("bhqk,bkhd->bqhd", probs_low, vals, preferred_element_type=f32)
    attended = attended.reshape(ITEM, -1).astype(bf16)
    partial = to_halves(dot_nt(attended, w_out).astype(bf16))
    return mixed, project, attended, log_total, partial


def stage_b(source, summed, mods, b_out):
    branch = summed + b_out.astype(f32)
    middle = source + mods[2] * branch
    shaped = (layer_norm(middle) * (1.0 + mods[4]) + mods[3]).astype(bf16)
    return branch, middle, shaped


def stage_c(shaped, grad_branch, w_up, b_up, k_ffn, w_down):
    taps = k_ffn.astype(f32)
    hidden = dot_nn(shaped, w_up) + b_up.astype(f32)
    hidden = from_groups(hidden, SIDE).reshape(SIDE, SIDE, -1)
    convolved = depthwise(hidden, taps)
    activated, back = jax.vjp(jax.nn.gelu, convolved)
    activated = to_groups(activated.reshape(ITEM, -1).astype(bf16), SIDE)
    grad_activated = from_groups(dot_nn(grad_branch, w_down), SIDE)
    grad_convolved = back(grad_activated.reshape(convolved.shape))[0]
    padded = jnp.pad(grad_convolved, ((1, 1), (0, 0), (0, 0)))
    grad_hidden, grad_k = depthwise_back(hidden, padded, taps)
    grad_hidden = to_groups(grad_hidden.reshape(ITEM, -1).astype(bf16), SIDE)
    grad_b_up = jnp.sum(grad_hidden.astype(f32), axis=0)
    branch = to_halves(dot_nt(activated, w_down).astype(bf16))
    grad_shaped = to_halves(dot_nt(grad_hidden, w_up).astype(bf16))
    return activated, grad_hidden, grad_k, grad_b_up, branch, grad_shaped


def stage_d(middle, branch, grad_out, grad_shaped, mods):
    normed, back = jax.vjp(layer_norm, middle)
    grad_middle = grad_out + back(grad_shaped * (1.0 + mods[4]))[0]
    sums = (
        jnp.sum(grad_middle * branch, axis=0),
        jnp.sum(grad_shaped, axis=0),
        jnp.sum(grad_shaped * normed, axis=0),
    )
    return grad_middle, (grad_middle * mods[2]).astype(bf16), sums


def stage_e(grad_branch, project, log_total, w_qkv, w_out):
    grad_attended = dot_nn(grad_branch, w_out).astype(bf16)
    query, keys, vals = (split_heads(p) for p in project)
    grads = split_heads(grad_attended)
    scores = jnp.einsum("bqhd,bkhd->bhqk", query, keys, preferred_element_type=f32) * score_scale
    probs = jnp.exp(scores - log_total)
    grad_probs = jnp.einsum("bqhd,bkhd->bhqk", grads, vals, preferred_element_type=f32)
    grad_scores = probs * (grad_probs - jnp.sum(probs * grad_probs, axis=-1, keepdims=True))
    grad_scores = grad_scores.astype(bf16)
    g_query = jnp.einsum("bhqk,bkhd->bqhd", grad_scores, keys, preferred_element_type=f32)
    g_keys = jnp.einsum("bhqk,bqhd->bkhd", grad_scores, query, preferred_element_type=f32)
    g_vals = jnp.einsum("bhqk,bqhd->bkhd", probs.astype(bf16), grads, preferred_element_type=f32)
    grad_project = [
        g.reshape(ITEM, -1).astype(bf16)
        for g in (g_query * score_scale, g_keys * score_scale, g_vals)
    ]
    grad_mixed = sum(dot_nt(grad_project[kind], w_qkv[:, kind]) for kind in range(3))
    return grad_project, with_halos(grad_mixed.astype(bf16))


def with_halos(values):
    width = values.shape[-1]
    padded = jnp.pad(values.reshape(4, HALF, HALF, width), ((0, 0), (1, 1), (0, 0), (0, 0)))
    shares = []
    for share in range(4):
        first = 4 * share
        main = padded[:, first + 1 : first + 5].reshape(-1, width)
        above = padded[2:, first].reshape(-1, width)
        below = padded[:2, first + 5].reshape(-1, width)
        shares.append(jnp.concatenate([main, above, below]))
    return jnp.stack(shares).reshape(2, 2, -1, width).swapaxes(0, 1)


def stage_f(tokens, grad_middle, grad_mixed, mods, k_att):
    width = tokens.shape[-1]
    rows = tokens.shape[0] // SIDE
    inner = from_groups(grad_mixed[:256], rows).reshape(rows, SIDE, width)
    above = grad_mixed[256:288].reshape(2, HALF, width).swapaxes(0, 1).reshape(1, SIDE, width)
    below = grad_mixed[288:].reshape(2, HALF, width).swapaxes(0, 1).reshape(1, SIDE, width)
    grad_rows = jnp.concatenate([above, inner, below])
    normed, back = jax.vjp(layer_norm, tokens)
    shaped = normed * (1.0 + mods[1]) + mods[0]
    grad_shaped, grad_k = depthwise_back(
        shaped.reshape(rows, SIDE, width), grad_rows, k_att.astype(f32)
    )
    grad_shaped = grad_shaped.reshape(tokens.shape)
    grad_tokens = from_groups(grad_middle, rows) + back(grad_shaped * (1.0 + mods[1]))[0]
    sums = (jnp.sum(grad_shaped, axis=0), jnp.sum(grad_shaped * normed, axis=0))
    return grad_tokens, grad_k, sums


def shards(
    tokens,
    cotangent,
    item_count,
    timestep,
    class_id,
    class_table,
    w_mod,
    b_mod,
    k_att,
    w_qkv,
    w_out,
    b_out,
    w_up,
    b_up,
    k_ffn,
    w_down,
    b_down,
):
    width = tokens.shape[1]
    place = lax.axis_index("tensor")
    core = place % 2
    side = place // 2
    live = (item_count[0] > 0).astype(f32)

    cond = time_features(timestep, width) + class_table[class_id[0]].astype(f32)[None, :]
    act_low = jax.nn.silu(cond).astype(bf16)
    mods = (dot_nt(act_low, w_mod) + b_mod.astype(f32)).reshape(6, width)
    card = jnp.concatenate([cond, jnp.broadcast_to(class_id.astype(f32)[:, None], (1, 128))], axis=1)
    cards = gather_xor(card)

    mixed, project, attended, log_total, partial = stage_a(tokens, mods, k_att, w_qkv, w_out)
    chip = add_low(take(partial, core), swap(take(partial, 1 - core), "tensor", 1))
    summed = chip.astype(f32) + swap(chip, "tensor", 2).astype(f32)

    source = take(to_halves(to_groups(tokens, SIDE)), core).astype(f32)
    branch, middle, shaped_own = stage_b(source, summed, mods, b_out)
    shaped = from_halves(shaped_own, swap(shaped_own, "tensor", 1), core)

    cot_groups = to_groups(cotangent, SIDE)
    grad_branch_ffn = (cot_groups.astype(f32) * (live * mods[5])).astype(bf16)
    grad_out = take(to_halves(cot_groups), core).astype(f32) * live
    activated, grad_hidden, grad_k_ffn, grad_b_up, ffn_part, grad_part = stage_c(
        shaped, grad_branch_ffn, w_up, b_up, k_ffn, w_down
    )
    chip = add_low(take(grad_part, core), swap(take(grad_part, 1 - core), "tensor", 1))
    grad_shaped = chip.astype(f32) + swap(chip, "tensor", 2).astype(f32)
    grad_w_down = scatter_sum(dot_tn(grad_branch_ffn, activated))
    grad_w_up = scatter_sum(dot_tn(shaped, grad_hidden))

    def own_share(values):
        return take(values.reshape(2, 256, -1), side)

    def reduce_share(values):
        shares = values.reshape(2, -1, width)
        return take(shares, side).astype(f32) + swap(take(shares, 1 - side), "tensor", 2).astype(f32)

    chip = add_low(take(ffn_part, core), swap(take(ffn_part, 1 - core), "tensor", 1))
    branch_ffn = reduce_share(chip) + b_down.astype(f32)
    block_out = (own_share(middle) + mods[5] * branch_ffn) * live
    block_out = from_groups(block_out.astype(bf16), SIDE // 4)
    grad_gate_ffn = jnp.sum(own_share(grad_out) * branch_ffn, axis=0)

    grad_middle, grad_attn_own, sums_d = stage_d(middle, branch, grad_out, grad_shaped, mods)
    grad_branch = from_halves(grad_attn_own, swap(grad_attn_own, "tensor", 1), core)
    grad_project, halo_part = stage_e(grad_branch, project, log_total, w_qkv, w_out)
    chip = add_low(take(halo_part, core), swap(take(halo_part, 1 - core), "tensor", 1))
    grad_mixed = reduce_share(chip).astype(bf16).astype(f32)
    grad_w_out = scatter_sum(dot_tn(grad_branch, attended))
    grad_w_qkv = scatter_sum(
        jnp.stack([dot_tn(mixed, g) for g in grad_project], axis=1)
    )

    rows = ITEM // 4
    own_tokens = lax.dynamic_slice_in_dim(tokens, place * rows, rows, 0).astype(f32)
    grad_tokens, grad_k_att, sums_f = stage_f(
        own_tokens, own_share(grad_middle), grad_mixed, mods, k_att
    )

    early = jnp.concatenate(
        [
            grad_k_ffn,
            grad_b_up[None],
            jnp.sum(grad_branch_ffn.astype(f32), axis=0)[None],
            jnp.sum(grad_branch.astype(f32), axis=0)[None],
        ]
    )
    early = butterfly(early, "dp")

    once = jnp.where(side == 0, 1.0, 0.0)
    late = jnp.concatenate(
        [
            jnp.stack(
                [
                    sums_f[0],
                    sums_f[1],
                    sums_d[0] * once,
                    sums_d[1] * once,
                    sums_d[2] * once,
                    grad_gate_ffn,
                ]
            ),
            grad_k_att,
        ]
    )
    late = butterfly(late, "tensor")
    grad_k_att = butterfly(late[6:], "dp")
    grad_modulate = gather_xor(late[None, :6].reshape(1, -1).astype(bf16))

    grad_b_mod = tree_sum(grad_modulate.astype(f32))
    conds = cards[:, :width]
    classes = cards[:, width]
    act, silu_back = jax.vjp(jax.nn.silu, conds)
    share = w_mod.shape[0] // lax.axis_size("dp")
    own_rows = lax.dynamic_slice_in_dim(grad_modulate, lax.axis_index("dp") * share, share, 1)
    grad_w_mod = dot_tn(own_rows, act.astype(bf16))
    grad_cond = silu_back(dot_nn(grad_modulate, w_mod))[0]
    same = (classes[:, None] == classes[None, :]).astype(f32)
    class_rows = tree_sum(same[:, :, None] * grad_cond[:, None, :])
    grad_class = jnp.zeros(class_table.shape, f32).at[classes.astype(jnp.int32)].set(class_rows)

    return (
        block_out,
        grad_tokens,
        grad_class,
        grad_w_mod,
        grad_b_mod,
        grad_k_att,
        grad_w_qkv,
        grad_w_out,
        early[11],
        grad_w_up,
        early[9],
        early[:9],
        grad_w_down,
        early[10],
    )


def solution(mesh):
    placed = (
        P("dp", None),
        P("dp", None),
        P("dp"),
        P("dp"),
        P("dp"),
        P(),
        P(),
        P(),
        P(),
        P(None, None, "tensor"),
        P(None, "tensor"),
        P(),
        P(None, "tensor"),
        P("tensor"),
        P(None, "tensor"),
        P(None, "tensor"),
        P(),
    )
    return jax.shard_map(
        shards,
        mesh=mesh,
        in_specs=placed,
        out_specs=(
            P(("dp", "tensor"), None),
            P(("dp", "tensor"), None),
            P(),
            P("dp", None),
            P(),
            P(),
            P("dp", None, "tensor"),
            P("dp", "tensor"),
            P(),
            P("dp", "tensor"),
            P("tensor"),
            P(None, "tensor"),
            P("dp", "tensor"),
            P(),
        ),
        check_vma=False,
    )
```

time: 1090 us -> 353 us (0.32)
  waiting for transfers between devices: 779 us -> 49.3 us
  local copies, waits for them, and re-layouts: 51.1 us -> 113 us
  blocking collectives: 52.1 us -> 0 us
  starting transfers between devices: 2.48 us -> 39.6 us
  matrix products: 75 us -> 45.9 us
  between operations: 18.2 us -> 5.33 us
    reduce_scatter x11 -> x0, waiting for transfers between devices: 578 us -> none  [the longest x1 233 us: shards(): lax.psum_scatter(grad_w_mod, 'dp', scatter_dimension=0, tiled=True)]
    psum x1 -> x0, waiting for transfers between devices: 131 us -> none  [shards(): lax.psum((grad_k_att, grad_k_ffn, grad_b_up, grad_b_out, grad_b_down, gra...]
    all_gather x5 -> x0, waiting for transfers between devices: 69.5 us -> none  [the longest x2 38.4 us: forward_pass(): shaped_ffn = lax.all_gather(shaped_share, 'tensor', axis=0, tiled=True)]
    psum x2 -> x0, blocking collectives: 52.1 us -> none  [the longest x1 40.3 us: shards(): lax.psum((grad_k_att, grad_k_ffn, grad_b_up, grad_b_out, grad_b_down, gra...]
    ppermute x0 -> x36, waiting for transfers between devices: none -> 49.3 us  [swap(): return lax.ppermute(values, axis, [(i, i ^ bit) for i in range(size)])]
    ppermute x0 -> x36, starting transfers between devices: none -> 39.6 us  [swap(): return lax.ppermute(values, axis, [(i, i ^ bit) for i in range(size)])]
    dot_general x31 -> x27, matrix products: 72.7 us -> 45.9 us  [the longest x7 14.6 us: dot_nn(): lax.dot_general(left, right, (((1,), (0,)), ((), ())), preferred_element_...]
    reshape x0 -> x14, local copies, waits for them, and re-layouts: none -> 18.6 us  [the longest x2 6.16 us: to_groups(): shaped = values.reshape((rows // 2, 2, HALF, 2, width))]
  transfers between devices with their start and end apart: 17 -> 36, of which waited for: 16 -> 15; matrix products, arithmetic and copies ran while one was open for 8% -> 37% of each run, Pallas kernels for 0% -> 0%
where the time goes in v1:
time: 353 us; the launch traced here: 348 us
  local copies, waits for them, and re-layouts  113 us (32%)
  other arithmetic  94.7 us (27%)
  waiting for transfers between devices  49.3 us (14%)
  matrix products  45.9 us (13%)
  starting transfers between devices  39.6 us (11%)
  between operations  5.33 us (2%)
    ppermute x36, waiting for transfers between devices, swap(): return lax.ppermute(values, axis, [(i, i ^ bit) for i in range(size)])  49.3 us
    ppermute x36, starting transfers between devices, swap(): return lax.ppermute(values, axis, [(i, i ^ bit) for i in range(size)])  39.6 us
    add_any x1, other arithmetic, stage_c(): activated, back = jax.vjp(jax.nn.gelu, convolved)  16.1 us
    dot_general x7, matrix products, dot_nn(): lax.dot_general(left, right, (((1,), (0,)), ((), ())), preferred_element_...  14.6 us
    dot_general x4, local copies, waits for them, and re-layouts, dot_tn(): lax.dot_general(left, right, (((0,), (0,)), ((), ())), preferred_element_...  11.3 us
    dot_general x7, matrix products, dot_tn(): lax.dot_general(left, right, (((0,), (0,)), ((), ())), preferred_element_...  11.1 us
    unnamed x252, local copies, waits for them, and re-layouts  10.6 us
    dot_general x7, matrix products, dot_nt(): lax.dot_general(left, right, (((1,), (1,)), ((), ())), preferred_element_...  10.4 us
  transfers between devices with their start and end apart: 36, of which 15 were waited for; matrix products, arithmetic and copies ran while one was open for 37% of the time, Pallas kernels for 0%

profile of v1, /device:TPU:0, one launch (start us, length us, event | category | flops | bytes accessed | tf_op | source)
XLA Modules:
  0.0 347.8 jit_solution(5072757087610822791)
XLA Ops:
  2.9 5.1 %convolution_reduce_fusion = f32[4608]{0:T(1024)S(1)} fusion(bf16[4608,768]{1,0:T(8,128)(2,1)} %param.23, f32[1,768]{1,0:T(1,128)S(1)} %fusion.127), kind=kOutput, calls=%fused_computation.159 | convolution fusion | flops 7081728 | bytes 7099392 | tf_op jit(solution)/shard_map/dot_general | solution.py:133
  11.7 5.7 %fusion.20 = bf16[32,32,768]{2,1,0:T(8,128)(2,1)} fusion(f32[32,32,768]{2,1,0:T(8,128)S(1)} %bitcast.377, f32[768]{0:T(1024)S(1)} %get-tuple-element.56, f32[768]{0:T(1024)S(1)} %get-tuple-element.57, f32[768]{0:T(1024)S(1)} %get-tuple-element.58, f32[768]{0:T(1024)S(1)} %get-tuple-element.59, f32[768]{0:T(1024)S(1)} %get-tuple-element.60, ...), kind=kLoop, calls=%fused_computation.47 | loop fusion | flops 14155776 | bytes 4746240 | tf_op jit(solution)/shard_map/convert_element_type | solution.py:147
  17.4 4.5 %convert_element_type.427 = bf16[16,2,16,2,768]{4,3,2,1,0:T(2,128)(2,1)} reshape(bf16[32,32,768]{2,1,0:T(8,128)(2,1)} %fusion.20) | data formatting | bytes 3145728 | tf_op jit(solution)/shard_map/convert_element_type | solution.py:147
  44.3 4.7 %reshape.541 = bf16[16,2,16,2,768]{4,3,2,1,0:T(2,128)(2,1)} reshape(bf16[1024,768]{1,0:T(8,128)(2,1)} %param.18) | data formatting | bytes 3145728 | tf_op jit(solution)/shard_map/reshape | solution.py:105
  49.0 3.1 bitcast_convert_fusion
  57.9 4.9 %convolution_bitcast_fusion = f32[16,2,16,2,768]{4,2,0,3,1:T(8,128)} fusion(bf16[768,768]{1,0:T(8,128)(2,1)} %param.32, f32[768]{0:T(1024)} %get-tuple-element.64, bf16[16,2,16,2,768]{4,3,2,1,0:T(2,128)(2,1)} %reshape.541), kind=kOutput, calls=%fused_computation.101 | convolution fusion | flops 1210318848 | bytes 5901312 | tf_op jit(solution)/shard_map/dot_general | solution.py:129
  70.1 5.1 %collective-permute-done.1 = bf16[512,768]{1,0:T(8,128)(2,1)} collective-permute-done((bf16[512,768]{1,0:T(8,128)(2,1)S(1)}, bf16[512,768]{1,0:T(8,128)(2,1)}, u32[]{:S(2)}, u32[]{:S(2)}) %collective-permute-start.1) | collective-permute-done | bytes 786464 | tf_op jit(solution)/shard_map/ppermute | solution.py:22
  88.0 6.1 %copy.286 = f32[16,2,16,2,768]{4,3,2,1,0:T(2,128)} copy(f32[16,2,16,2,768]{4,2,0,3,1:T(8,128)} %convolution_bitcast_fusion) | data formatting | bytes 6291456 | tf_op jit(solution)/shard_map/transpose | solution.py:112
  94.1 5.3 %reshape_reshape.24 = f32[32,32,768]{2,1,0:T(8,128)} reshape(f32[16,2,16,2,768]{4,3,2,1,0:T(2,128)} %copy.286) | data formatting | bytes 6291456 | tf_op jit(solution)/shard_map/reshape;reshape | solution.py:175
  113.5 4.1 %copy.371 = f32[2,2,16,16,768]{4,1,3,0,2:T(2,128)} copy(f32[2,2,16,16,768]{4,3,2,1,0:T(8,128)S(1)} %bitcast.424) | data formatting | bytes 6291456 | tf_op jit(solution)/shard_map/reshape | solution.py:111
  117.6 5.3 %reshape_reshape.22 = f32[32,32,768]{2,1,0:T(8,128)} reshape(f32[16,2,16,2,768]{4,3,2,1,0:T(2,128)} %bitcast.376) | data formatting | bytes 6291456 | tf_op jit(solution)/shard_map/reshape;reshape | solution.py:170
  122.9 16.1 %fusion.10 = (f32[32,32,768]{2,1,0:T(8,128)}, f32[32,32,768]{2,1,0:T(8,128)S(1)}) fusion(f32[32,32,768]{2,1,0:T(8,128)} %reshape_reshape.24, f32[768]{0:T(1024)} %get-tuple-element.47, f32[768]{0:T(1024)} %get-tuple-element.48, f32[768]{0:T(1024)} %get-tuple-element.49, f32[768]{0:T(1024)} %get-tuple-element.50, f32[32,32,768]{2,1,0:T(8,128)} %reshape_reshape.22, ...), kind=kLoop, calls=%fused_computation.37 | loop fusion | flops 28311552 | bytes 12610560 | tf_op jit(solution)/shard_map/transpose(jvp())/add_any | solution.py:172
  142.9 8.8 %multiply_reduce_fusion = (f32[768]{0:T(1024)}, f32[768]{0:T(1024)}, f32[768]{0:T(1024)}, f32[768]{0:T(1024)}, f32[768]{0:T(1024)}, /*index=5*/f32[768]{0:T(1024...) fusion(f32[32,32,768]{2,1,0:T(8,128)S(1)} %copy-done.7, f32[34,32,768]{2,1,0:T(8,128)S(1)} %pad.24, ...), kind=kLoop, calls=%fused_computation.77 | loop fusion | flops 30663936 | bytes 17525760 | tf_op jit(solution)/shard_map/reduce_sum | solution.py:99
  151.8 6.9 %add_convert_fusion.1 = bf16[32,32,768]{2,1,0:T(8,128)(2,1)} fusion(f32[34,32,768]{2,1,0:T(8,128)S(1)} %pad.24, f32[768]{0:T(1024)S(1)} %copy-done.64, f32[768]{0:T(1024)S(1)} %copy-done.65, f32[768]{0:T(1024)S(1)} %copy-done.66, f32[768]{0:T(1024)S(1)} %copy-done.67, f32[768]{0:T(1024)S(1)} %copy-done.68, f32[768]{0:T(1024)S(1)} %copy-done.69, ...), kind=kLoop, calls=%fused_computation.89 | loop fusion | flops 29097984 | bytes 17534976 | tf_op jit(solution)/shard_map/convert_element_type | solution.py:178
  158.7 4.5 %convert_element_type.447 = bf16[16,2,16,2,768]{4,3,2,1,0:T(2,128)(2,1)} reshape(bf16[32,32,768]{2,1,0:T(8,128)(2,1)} %get-tuple-element.83) | data formatting | bytes 3145728 | tf_op jit(solution)/shard_map/convert_element_type | solution.py:173
  168.6 4.5 %convert_element_type.464 = bf16[16,2,16,2,768]{4,3,2,1,0:T(2,128)(2,1)} reshape(bf16[32,32,768]{2,1,0:T(8,128)(2,1)} %add_convert_fusion.1) | data formatting | bytes 3145728 | tf_op jit(solution)/shard_map/convert_element_type | solution.py:178
  173.1 3.3 convert_reduce_fusion.3
  182.2 3.4 fusion.154
  205.4 4.2 %collective-permute-done.34 = bf16[2,96,768]{2,1,0:T(8,128)(2,1)S(1)} collective-permute-done((bf16[2,96,768]{2,1,0:T(8,128)(2,1)S(1)}, bf16[2,96,768]{2,1,0:T(8,128)(2,1)S(1)}, u32[]{:S(2)}, u32[]{:S(2)}) %collective-permute-start.34) | collective-permute-done | bytes 294944 | tf_op jit(solution)/shard_map/ppermute | solution.py:22
  210.1 8.1 %collective-permute-done.31 = bf16[2,96,768]{2,1,0:T(8,128)(2,1)S(1)} collective-permute-done((bf16[2,96,768]{2,1,0:T(8,128)(2,1)S(1)}, bf16[2,96,768]{2,1,0:T(8,128)(2,1)S(1)}, u32[]{:S(2)}, u32[]{:S(2)}) %collective-permute-start.31) | collective-permute-done | bytes 294944 | tf_op jit(solution)/shard_map/ppermute | solution.py:22
  219.8 7.4 %collective-permute-done.32 = bf16[1,96,768]{2,1,0:T(8,128)(2,1)S(1)} collective-permute-done((bf16[1,96,768]{2,1,0:T(8,128)(2,1)S(1)}, bf16[1,96,768]{2,1,0:T(8,128)(2,1)S(1)}, u32[]{:S(2)}, u32[]{:S(2)}) %collective-permute-start.32) | collective-permute-done | bytes 147488 | tf_op jit(solution)/shard_map/ppermute | solution.py:22
  281.3 3.7 %collective-permute-done.29 = f32[12,768]{1,0:T(8,128)S(1)} collective-permute-done((f32[12,768]{1,0:T(8,128)S(1)}, f32[12,768]{1,0:T(8,128)S(1)}, u32[]{:S(2)}, u32[]{:S(2)}) %collective-permute-start.29) | collective-permute-done | bytes 36896 | tf_op jit(solution)/shard_map/ppermute | solution.py:22
  287.1 7.8 %collective-permute-done.21 = bf16[4,96,3,192]{3,1,0,2:T(8,128)(2,1)S(1)} collective-permute-done((bf16[4,96,3,192]{3,1,0,2:T(8,128)(2,1)S(1)}, bf16[4,96,3,192]{3,1,0,2:T(8,128)(2,1)S(1)}, u32[]{:S(2)}, u32[]{:S(2)}) %collective-permute-start.21) | collective-permute-done | bytes 442400 | tf_op jit(solution)/shard_map/ppermute | solution.py:22
  337.0 4.1 %fusion.117 = f32[8,768]{1,0:T(8,128)S(1)} fusion(f32[4,896]{1,0:T(4,128)} %collective-permute-done.12, f32[2,896]{1,0:T(2,128)S(1)} %copy-done.53, f32[1,896]{1,0:T(1,128)} %collective-permute-done.10, f32[1,896]{1,0:T(1,128)} %concatenate.69, bf16[8,4608]{1,0:T(8,128)(2,1)S(1)} %pad_maximum_fusion.4, bf16[4608,768]{1,0:T(8,128)(2,1)} %param.23), kind=kOutput, calls=%fused_computation.272 | convolution fusion | flops 56696832 | bytes 7204864 | tf_op jit(solution)/shard_map/dot_general | solution.py:129
  (539 shorter events, 205.8 us)
Async XLA Ops:
  39.9 13.5 %collective-permute-start = (bf16[512,768]{1,0:T(8,128)(2,1)S(1)}, bf16[512,768]{1,0:T(8,128)(2,1)}, u32[]{:S(2)}, u32[]{:S(2)}) collective-permute-start(bf16[512,768]{1,0:T(8,128)(2,1)S(1)} %dynamic-slice_bitcast_fusion.3), channel_id=1, source_target_pairs={{0,1},{1,0},{2,3},{3,2},{4,5},{5,4},{6,7},{7,6},{8,9},{9,8},{10,11... | collective-permute-start | bytes 2359304 | tf_op jit(solution)/shard_map/ppermute | solution.py:22
  41.7 25.9 %collective-permute-start.10 = (f32[1,896]{1,0:T(1,128)}, f32[1,896]{1,0:T(1,128)}, u32[]{:S(2)}, u32[]{:S(2)}) collective-permute-start(f32[1,896]{1,0:T(1,128)} %concatenate.69), channel_id=1, source_target_pairs={{0,4},{4,0},{8,12},{12,8},{16,20},{20,16},{24,28},{28,24},{1,5},{5... | collective-permute-start | bytes 10760 | tf_op jit(solution)/shard_map/ppermute | solution.py:22
  55.3 19.8 %collective-permute-start.1 = (bf16[512,768]{1,0:T(8,128)(2,1)S(1)}, bf16[512,768]{1,0:T(8,128)(2,1)}, u32[]{:S(2)}, u32[]{:S(2)}) collective-permute-start(bf16[512,768]{1,0:T(8,128)(2,1)S(1)} %fusion.49), channel_id=1, source_target_pairs={{0,2},{1,3},{2,0},{3,1},{4,6},{5,7},{6,4},{7,5},{8,10},{9,11},{10,... | collective-permute-start | bytes 2359304 | tf_op jit(solution)/shard_map/ppermute | solution.py:22
  68.4 11.2 %collective-permute-start.11 = (f32[2,896]{1,0:T(2,128)S(1)}, f32[2,896]{1,0:T(2,128)S(1)}, u32[]{:S(2)}, u32[]{:S(2)}) collective-permute-start(f32[2,896]{1,0:T(2,128)S(1)} %pad_maximum_fusion.11), channel_id=1, source_target_pairs={{0,8},{4,12},{8,0},{12,4},{16,24},{20,28},{24,16},{28,20},{1,9},{5... | collective-permute-start | bytes 21512 | tf_op jit(solution)/shard_map/ppermute | solution.py:22
  78.3 31.4 %collective-permute-start.2 = (bf16[512,768]{1,0:T(8,128)(2,1)}, bf16[512,768]{1,0:T(8,128)(2,1)}, u32[]{:S(2)}, u32[]{:S(2)}) collective-permute-start(bf16[512,768]{1,0:T(8,128)(2,1)} %add_convert_fusion.2), channel_id=1, source_target_pairs={{0,1},{1,0},{2,3},{3,2},{4,5},{5,4},{6,7},{7,6},{8,9},{9,8},{10,11... | collective-permute-start | bytes 2359304 | tf_op jit(solution)/shard_map/ppermute | solution.py:22
  81.5 26.0 %collective-permute-start.12 = (f32[4,896]{1,0:T(4,128)}, f32[4,896]{1,0:T(4,128)}, u32[]{:S(2)}, u32[]{:S(2)}) collective-permute-start(f32[4,896]{1,0:T(4,128)} %pad_maximum_fusion.10), channel_id=1, source_target_pairs={{0,16},{4,20},{8,24},{12,28},{16,0},{20,4},{24,8},{28,12},{1,17},{... | collective-permute-start | bytes 43016 | tf_op jit(solution)/shard_map/ppermute | solution.py:22
  168.1 30.4 %collective-permute-start.33 = (bf16[4,96,768]{2,1,0:T(8,128)(2,1)}, bf16[4,96,768]{2,1,0:T(8,128)(2,1)}, u32[]{:S(2)}, u32[]{:S(2)}) collective-permute-start(bf16[4,96,768]{2,1,0:T(8,128)(2,1)} %fusion.78), channel_id=1, source_target_pairs={{0,4},{4,0},{8,12},{12,8},{16,20},{20,16},{24,28},{28,24},{1,5},{5... | collective-permute-start | bytes 1769480 | tf_op jit(solution)/shard_map/ppermute | solution.py:22
  185.6 15.7 %collective-permute-start.30 = (bf16[4,96,768]{2,1,0:T(8,128)(2,1)S(1)}, bf16[4,96,768]{2,1,0:T(8,128)(2,1)S(1)}, u32[]{:S(2)}, u32[]{:S(2)}) collective-permute-start(bf16[4,96,768]{2,1,0:T(8,128)(2,1)S(1)} %fusion.77), channel_id=1, source_target_pairs={{0,4},{4,0},{8,12},{12,8},{16,20},{20,16},{24,28},{28,24},{1,5},{5... | collective-permute-start | bytes 1769480 | tf_op jit(solution)/shard_map/ppermute | solution.py:22
  188.9 13.8 %collective-permute-start.5 = (bf16[512,768]{1,0:T(8,128)(2,1)S(1)}, bf16[512,768]{1,0:T(8,128)(2,1)S(1)}, u32[]{:S(2)}, u32[]{:S(2)}) collective-permute-start(bf16[512,768]{1,0:T(8,128)(2,1)S(1)} %dynamic-slice_bitcast_fusion.1), channel_id=1, source_target_pairs={{0,1},{1,0},{2,3},{3,2},{4,5},{5,4},{6,7},{7,6},{8,9},{9,8},{10,11... | collective-permute-start | bytes 2359304 | tf_op jit(solution)/shard_map/ppermute | solution.py:22
  199.7 9.9 %collective-permute-start.34 = (bf16[2,96,768]{2,1,0:T(8,128)(2,1)S(1)}, bf16[2,96,768]{2,1,0:T(8,128)(2,1)S(1)}, u32[]{:S(2)}, u32[]{:S(2)}) collective-permute-start(bf16[2,96,768]{2,1,0:T(8,128)(2,1)S(1)} %fusion.97), channel_id=1, source_target_pairs={{0,8},{4,12},{8,0},{12,4},{16,24},{20,28},{24,16},{28,20},{1,9},{5... | collective-permute-start | bytes 884744 | tf_op jit(solution)/shard_map/ppermute | solution.py:22
  201.5 16.7 %collective-permute-start.31 = (bf16[2,96,768]{2,1,0:T(8,128)(2,1)S(1)}, bf16[2,96,768]{2,1,0:T(8,128)(2,1)S(1)}, u32[]{:S(2)}, u32[]{:S(2)}) collective-permute-start(bf16[2,96,768]{2,1,0:T(8,128)(2,1)S(1)} %fusion.96), channel_id=1, source_target_pairs={{0,8},{4,12},{8,0},{12,4},{16,24},{20,28},{24,16},{28,20},{1,9},{5... | collective-permute-start | bytes 884744 | tf_op jit(solution)/shard_map/ppermute | solution.py:22
  202.9 31.1 %collective-permute-start.6 = (bf16[512,768]{1,0:T(8,128)(2,1)S(1)}, bf16[512,768]{1,0:T(8,128)(2,1)}, u32[]{:S(2)}, u32[]{:S(2)}) collective-permute-start(bf16[512,768]{1,0:T(8,128)(2,1)S(1)} %fusion.47), channel_id=1, source_target_pairs={{0,2},{1,3},{2,0},{3,1},{4,6},{5,7},{6,4},{7,5},{8,10},{9,11},{10,... | collective-permute-start | bytes 2359304 | tf_op jit(solution)/shard_map/ppermute | solution.py:22
  204.8 25.4 %collective-permute-start.4 = (bf16[256,768]{1,0:T(8,128)(2,1)S(1)}, bf16[256,768]{1,0:T(8,128)(2,1)S(1)}, u32[]{:S(2)}, u32[]{:S(2)}) collective-permute-start(bf16[256,768]{1,0:T(8,128)(2,1)S(1)} %dynamic-slice_bitcast_fusion.5), channel_id=1, source_target_pairs={{0,2},{1,3},{2,0},{3,1},{4,6},{5,7},{6,4},{7,5},{8,10},{9,11},{10,... | collective-permute-start | bytes 1179656 | tf_op jit(solution)/shard_map/ppermute | solution.py:22
  209.7 9.4 %collective-permute-start.35 = (bf16[1,96,768]{2,1,0:T(8,128)(2,1)S(1)}, bf16[1,96,768]{2,1,0:T(8,128)(2,1)S(1)}, u32[]{:S(2)}, u32[]{:S(2)}) collective-permute-start(bf16[1,96,768]{2,1,0:T(8,128)(2,1)S(1)} %dynamic-slice_convert_fusion.4), channel_id=1, source_target_pairs={{0,16},{4,20},{8,24},{12,28},{16,0},{20,4},{24,8},{28,12},{1,17},{... | collective-permute-start | bytes 442376 | tf_op jit(solution)/shard_map/ppermute | solution.py:22
  218.3 8.9 %collective-permute-start.32 = (bf16[1,96,768]{2,1,0:T(8,128)(2,1)S(1)}, bf16[1,96,768]{2,1,0:T(8,128)(2,1)S(1)}, u32[]{:S(2)}, u32[]{:S(2)}) collective-permute-start(bf16[1,96,768]{2,1,0:T(8,128)(2,1)S(1)} %dynamic-slice_convert_fusion.5), channel_id=1, source_target_pairs={{0,16},{4,20},{8,24},{12,28},{16,0},{20,4},{24,8},{28,12},{1,17},{... | collective-permute-start | bytes 442376 | tf_op jit(solution)/shard_map/ppermute | solution.py:22
  265.2 9.5 %collective-permute-start.27 = (f32[12,768]{1,0:T(8,128)}, f32[12,768]{1,0:T(8,128)}, u32[]{:S(2)}, u32[]{:S(2)}) collective-permute-start(f32[12,768]{1,0:T(8,128)} %concatenate.77), channel_id=1, source_target_pairs={{0,4},{4,0},{8,12},{12,8},{16,20},{20,16},{24,28},{28,24},{1,5},{5... | collective-permute-start | bytes 110600 | tf_op jit(solution)/shard_map/ppermute | solution.py:22
  271.0 14.6 %collective-permute-start.24 = (bf16[4,96,192]{2,1,0:T(8,128)(2,1)S(1)}, bf16[4,96,192]{2,1,0:T(8,128)(2,1)S(1)}, u32[]{:S(2)}, u32[]{:S(2)}) collective-permute-start(bf16[4,96,192]{2,1,0:T(8,128)(2,1)S(1)} %fusion.114), channel_id=1, source_target_pairs={{0,4},{4,0},{8,12},{12,8},{16,20},{20,16},{24,28},{28,24},{1,5},{5... | collective-permute-start | bytes 442376 | tf_op jit(solution)/shard_map/ppermute | solution.py:22
  274.6 22.1 %collective-permute-start.8 = (bf16[2,320,768]{2,1,0:T(8,128)(2,1)S(1)}, bf16[2,320,768]{2,1,0:T(8,128)(2,1)S(1)}, u32[]{:S(2)}, u32[]{:S(2)}) collective-permute-start(bf16[2,320,768]{2,1,0:T(8,128)(2,1)S(1)} %dynamic-slice_bitcast_fusion), channel_id=1, source_target_pairs={{0,1},{1,0},{2,3},{3,2},{4,5},{5,4},{6,7},{7,6},{8,9},{9,8},{10,11... | collective-permute-start | bytes 2949128 | tf_op jit(solution)/shard_map/ppermute | solution.py:22
  280.2 14.7 %collective-permute-start.21 = (bf16[4,96,3,192]{3,1,0,2:T(8,128)(2,1)S(1)}, bf16[4,96,3,192]{3,1,0,2:T(8,128)(2,1)S(1)}, u32[]{:S(2)}, u32[]{:S(2)}) collective-permute-start(bf16[4,96,3,192]{3,1,0,2:T(8,128)(2,1)S(1)} %fusion.76), channel_id=1, source_target_pairs={{0,4},{4,0},{8,12},{12,8},{16,20},{20,16},{24,28},{28,24},{1,5},{5... | collective-permute-start | bytes 1327112 | tf_op jit(solution)/shard_map/ppermute | solution.py:22
  285.7 12.9 %collective-permute-start.25 = (bf16[2,96,192]{2,1,0:T(8,128)(2,1)S(1)}, bf16[2,96,192]{2,1,0:T(8,128)(2,1)S(1)}, u32[]{:S(2)}, u32[]{:S(2)}) collective-permute-start(bf16[2,96,192]{2,1,0:T(8,128)(2,1)S(1)} %fusion.115), channel_id=1, source_target_pairs={{0,8},{4,12},{8,0},{12,4},{16,24},{20,28},{24,16},{28,20},{1,9},{5... | collective-permute-start | bytes 221192 | tf_op jit(solution)/shard_map/ppermute | solution.py:22
  297.1 11.4 %collective-permute-start.9 = (bf16[320,768]{1,0:T(8,128)(2,1)S(1)}, bf16[320,768]{1,0:T(8,128)(2,1)S(1)}, u32[]{:S(2)}, u32[]{:S(2)}) collective-permute-start(bf16[320,768]{1,0:T(8,128)(2,1)S(1)} %dynamic-slice_bitcast_fusion.4), channel_id=1, source_target_pairs={{0,2},{1,3},{2,0},{3,1},{4,6},{5,7},{6,4},{7,5},{8,10},{9,11},{10,... | collective-permute-start | bytes 1474568 | tf_op jit(solution)/shard_map/ppermute | solution.py:22
  299.3 17.9 %collective-permute-start.26 = (bf16[1,96,192]{2,1,0:T(8,128)(2,1)}, bf16[1,96,192]{2,1,0:T(8,128)(2,1)}, u32[]{:S(2)}, u32[]{:S(2)}) collective-permute-start(bf16[1,96,192]{2,1,0:T(8,128)(2,1)} %dynamic-slice_convert_fusion.7), channel_id=1, source_target_pairs={{0,16},{4,20},{8,24},{12,28},{16,0},{20,4},{24,8},{28,12},{1,17},{... | collective-permute-start | bytes 110600 | tf_op jit(solution)/shard_map/ppermute | solution.py:22
  303.9 16.3 %collective-permute-start.23 = (bf16[1,96,3,192]{3,1,2,0:T(8,128)(2,1)}, bf16[1,96,3,192]{3,1,2,0:T(8,128)(2,1)}, u32[]{:S(2)}, u32[]{:S(2)}) collective-permute-start(bf16[1,96,3,192]{3,1,2,0:T(8,128)(2,1)} %dynamic-slice_convert_fusion.6), channel_id=1, source_target_pairs={{0,16},{4,20},{8,24},{12,28},{16,0},{20,4},{24,8},{28,12},{1,17},{... | collective-permute-start | bytes 331784 | tf_op jit(solution)/shard_map/ppermute | solution.py:22
  335.9 11.1 %collective-permute-start.20 = (f32[9,768]{1,0:T(8,128)S(1)}, f32[9,768]{1,0:T(8,128)S(1)}, u32[]{:S(2)}, u32[]{:S(2)}) collective-permute-start(f32[9,768]{1,0:T(8,128)S(1)} %add.575), channel_id=1, source_target_pairs={{0,16},{4,20},{8,24},{12,28},{16,0},{20,4},{24,8},{28,12},{1,17},{... | collective-permute-start | bytes 82952 | tf_op jit(solution)/shard_map/ppermute | solution.py:22
  (135 other events, 695.5 us)

commit v2 on v1

v2 whole, which is shorter than its diff:
```python
import functools
import math

import jax
import jax.numpy as jnp
from jax import lax
from jax.experimental import pallas as pl
from jax.experimental.pallas import tpu as pltpu
from jax.sharding import PartitionSpec as P

f32 = jnp.float32
bf16 = jnp.bfloat16

PITCH=40
GRID_ROWS=34*PITCH+8
SLOPE=math.sqrt(2.0/math.pi)
CUBIC=0.044715

def dot_nn(l,r): return lax.dot_general(l,r,(((1,),(0,)),((),())),preferred_element_type=f32)
def dot_nt(l,r): return lax.dot_general(l,r,(((1,),(1,)),((),())),preferred_element_type=f32)
def dot_tn(l,r): return lax.dot_general(l,r,(((0,),(0,)),((),())),preferred_element_type=f32)

def place(row, col):
    return (row+1)*PITCH+8+col

def strided(start):
    return pl.ds(start,16,stride=2)

def patch(ref, tile, i):
    return [[ref[tile, strided(place(2*i+row, col)), :] for col in range(-1,3)] for row in range(-1,3)]

def halves_out(values_ref, core, group, keep_ref, send_ref):
    for x in range(2):
        rows=pl.ds(x*256+group*64,64)
        rows=pl.ds(pl.multiple_of(x*256+group*64,64),64)
        keep_ref[rows,:]=values_ref[pl.ds(pl.multiple_of((2*x+core)*64,64),64),:].astype(bf16)
        send_ref[rows,:]=values_ref[pl.ds(pl.multiple_of((2*x+1-core)*64,64),64),:].astype(bf16)

def kernel_c(core_ref, own_ref, other_ref, gb_ref, up_ref, bup_ref, k_ref, down_ref,
             shaped_ref, act_ref, gh_ref, sums_ref, bkeep_ref, bsend_ref, gkeep_ref, gsend_ref,
             hid, gcv, gact, temp):
    core=core_ref[0]
    hid[...]=jnp.zeros_like(hid)
    gcv[...]=jnp.zeros_like(gcv)
    for half_ref, h in ((own_ref,core),(other_ref,1-core)):
        for x in range(2):
            for g in range(4):
                row=pl.multiple_of(g*256+(8*x+4*h)*16,64)
                shaped_ref[pl.ds(row,64),:]=half_ref[x*256+g*64:x*256+g*64+64,:]
    def up(g,_):
        rows=pl.ds(pl.multiple_of(g*256,256),256)
        a=g//2; b=g%2
        gact[rows,:]=dot_nn(gb_ref[rows,:],down_ref[...])
        temp[...]=dot_nn(shaped_ref[rows,:],up_ref[...])+bup_ref[...]
        def spread(i,_):
            for tile in range(6):
                hid[tile,strided(place(2*i+a,b)),:]=temp[pl.ds(pl.multiple_of(i*16,16),16),tile*128:tile*128+128]
            return 0
        lax.fori_loop(0,16,spread,0)
        return 0
    lax.fori_loop(0,4,up,0)
    def conv(tile,_):
        cols=pl.ds(pl.multiple_of(tile*128,128),128)
        taps=[k_ref[t:t+1,cols] for t in range(9)]
        def row(i,_):
            seen=patch(hid,tile,i)
            for a in range(2):
                for b in range(2):
                    g=2*a+b
                    rows=pl.ds(pl.multiple_of(g*256+i*16,16),16)
                    u=taps[0]*seen[a][b]
                    for t in range(1,9):
                        u=u+taps[t]*seen[a+t//3][b+t%3]
                    sq=u*u
                    th=jnp.tanh(SLOPE*u*(1.0+CUBIC*sq))
                    half=0.5+0.5*th
                    act_ref[rows,cols]=(u*half).astype(bf16)
                    slope=half+(0.5*SLOPE)*u*(1.0-th*th)*(1.0+(3*CUBIC)*sq)
                    gcv[tile,strided(place(2*i+a,b)),:]=gact[rows,cols]*slope
            return 0
        lax.fori_loop(0,16,row,0)
        return 0
    lax.fori_loop(0,6,conv,0)
    def back(tile,_):
        cols=pl.ds(pl.multiple_of(tile*128,128),128)
        taps=[k_ref[t:t+1,cols] for t in range(9)]
        def row(i,acc):
            seen=patch(gcv,tile,i)
            acc=list(acc)
            for a in range(2):
                for b in range(2):
                    g=2*a+b
                    rows=pl.ds(pl.multiple_of(g*256+i*16,16),16)
                    here=hid[tile,strided(place(2*i+a,b)),:]
                    total=None
                    for t in range(9):
                        s=seen[a+2-t//3][b+2-t%3]
                        total=taps[t]*s if total is None else total+taps[t]*s
                        p=here*s
                        acc[t]=acc[t]+(p[:8]+p[8:])
                    low=total.astype(bf16)
                    gh_ref[rows,cols]=low
                    p=low.astype(f32)
                    acc[9]=acc[9]+(p[:8]+p[8:])
            return tuple(acc)
        acc=lax.fori_loop(0,16,row,tuple(jnp.zeros((8,128),f32) for _ in range(10)))
        for t in range(10):
            sums_ref[t:t+1,cols]=jnp.sum(acc[t],axis=0,keepdims=True)
        return 0
    lax.fori_loop(0,6,back,0)
    def out(g,total):
        rows=pl.ds(pl.multiple_of(g*256,256),256)
        temp[...]=dot_nt(gh_ref[rows,:],up_ref[...])
        halves_out(temp,core,g,gkeep_ref,gsend_ref)
        temp[...]=dot_nt(act_ref[rows,:],down_ref[...])
        halves_out(temp,core,g,bkeep_ref,bsend_ref)
        return total+jnp.sum(gb_ref[rows,:].astype(f32),axis=0,keepdims=True)
    sums_ref[10:11,:]=lax.fori_loop(0,4,out,jnp.zeros((1,768),f32))

def call_c(core, own, other, gb, w_up, b_up, k, w_down):
    half=jax.ShapeDtypeStruct((512,768),bf16)
    full=jax.ShapeDtypeStruct((1024,768),bf16)
    vm=pl.BlockSpec(memory_space=pltpu.VMEM)
    return pl.pallas_call(kernel_c,
        out_shape=(full,full,full,jax.ShapeDtypeStruct((16,768),f32),half,half,half,half),
        in_specs=[pl.BlockSpec(memory_space=pltpu.SMEM)]+[vm]*7,
        out_specs=[vm]*8,
        scratch_shapes=[pltpu.VMEM((6,GRID_ROWS,128),f32),pltpu.VMEM((6,GRID_ROWS,128),f32),pltpu.VMEM((1024,768),f32),pltpu.VMEM((256,768),f32)],
        compiler_params=pltpu.CompilerParams(vmem_limit_bytes=56<<20),
        cost_estimate=pl.CostEstimate(flops=5*10**9,bytes_accessed=12*10**6,transcendentals=10**6),
    )(core,own,other,gb,w_up,b_up.astype(f32)[None],k.astype(f32),w_down)


eps=1e-6
def vm(): return pl.BlockSpec(memory_space=pltpu.VMEM)
def sm(): return pl.BlockSpec(memory_space=pltpu.SMEM)
def sds(shape,dt): return jax.ShapeDtypeStruct(shape,dt)
def at(start,size): return pl.ds(pl.multiple_of(start,size),size)

def normed_of(x):
    center=x-jnp.mean(x,axis=-1,keepdims=True)
    rs=lax.rsqrt(jnp.mean(center*center,axis=-1,keepdims=True)+eps)
    return center*rs, rs

def head_masks():
    lane=lax.broadcasted_iota(jnp.int32,(256,192),1)
    return [(lane>=64*h)&(lane<64*h+64) for h in range(3)]

def kernel_a(core_ref, tok_ref, mods_ref, k_ref, wqkv_ref, wout_ref,
             mixed_ref, q_ref, kk_ref, v_ref, att_ref, lse_ref, src_ref, keep_ref, send_ref,
             grid, xs, temp):
    core=core_ref[0]
    grid[...]=jnp.zeros_like(grid)
    shift=mods_ref[0:1,:]; scale=1.0+mods_ref[1:2,:]
    def norm(i,_):
        x=tok_ref[at(i*64,64),:].astype(f32)
        n,_r=normed_of(x)
        y=n*scale+shift
        for tile in range(6):
            cols=slice(tile*128,tile*128+128)
            xs[tile,at(i*64,64),:]=x[:,cols]
            for r in range(2):
                grid[tile,pl.ds(pl.multiple_of((2*i+r+1)*PITCH+8,8),32),:]=y[32*r:32*r+32,cols]
        return 0
    lax.fori_loop(0,16,norm,0)
    def conv(tile,_):
        cols=pl.ds(pl.multiple_of(tile*128,128),128)
        taps=[k_ref[t:t+1,cols] for t in range(9)]
        def row(i,_):
            seen=patch(grid,tile,i)
            for a in range(2):
                for b in range(2):
                    u=taps[0]*seen[a][b]
                    for t in range(1,9):
                        u=u+taps[t]*seen[a+t//3][b+t%3]
                    mixed_ref[at((2*a+b)*256+i*16,16),cols]=u.astype(bf16)
            return 0
        lax.fori_loop(0,16,row,0)
        for x in range(2):
            for g in range(4):
                for ii in range(4):
                    i=8*x+4*core+ii
                    src_ref[x*256+g*64+ii*16:x*256+g*64+ii*16+16,cols]=xs[tile,strided((2*i+g//2)*32+g%2),:]
        return 0
    lax.fori_loop(0,6,conv,0)
    masks=head_masks()
    lane=lax.broadcasted_iota(jnp.int32,(256,128),1)
    def attend(g,_):
        rows=at(g*256,256)
        m=mixed_ref[rows,:]
        q,k,v=(dot_nn(m,wqkv_ref[t]).astype(bf16) for t in range(3))
        q_ref[rows,:]=q; kk_ref[rows,:]=k; v_ref[rows,:]=v
        att=jnp.zeros((256,192),f32)
        lse=jnp.zeros((256,128),f32)
        for h in range(3):
            s=dot_nt(jnp.where(masks[h],q,jnp.zeros_like(q)),k)*0.125
            top=jnp.max(s,axis=-1,keepdims=True)
            lt=top+jnp.log(jnp.sum(jnp.exp(s-top),axis=-1,keepdims=True))
            p=jnp.exp(s-lt).astype(bf16)
            att=jnp.where(masks[h],dot_nn(p,v),att)
            lse=jnp.where(lane==h,lt,lse)
        lse_ref[rows,:]=lse
        att=att.astype(bf16)
        att_ref[rows,:]=att
        temp[...]=dot_nt(att,wout_ref[...])
        halves_out(temp,core,g,keep_ref,send_ref)
        return 0
    lax.fori_loop(0,4,attend,0)

def call_a(core,tokens,mods,k,wqkv,w_out):
    half=sds((512,768),bf16); head=sds((1024,192),bf16)
    return pl.pallas_call(kernel_a,
        out_shape=(sds((1024,768),bf16),head,head,head,head,sds((1024,128),f32),sds((512,768),f32),half,half),
        in_specs=[sm()]+[vm()]*5, out_specs=[vm()]*9,
        scratch_shapes=[pltpu.VMEM((6,GRID_ROWS,128),f32),pltpu.VMEM((6,1024,128),f32),pltpu.VMEM((256,768),f32)],
        compiler_params=pltpu.CompilerParams(vmem_limit_bytes=56<<20),
        cost_estimate=pl.CostEstimate(flops=3*10**9,bytes_accessed=12*10**6,transcendentals=2*10**6),
    )(core,tokens,mods,k.astype(f32),wqkv,w_out)

def kernel_b(chip_ref, far_ref, src_ref, mods_ref, bout_ref, branch_ref, middle_ref, shaped_ref):
    gate=mods_ref[2:3,:]; shift=mods_ref[3:4,:]; scale=1.0+mods_ref[4:5,:]
    bias=bout_ref[...]
    def step(r,_):
        rows=at(r*64,64)
        br=chip_ref[rows,:].astype(f32)+far_ref[rows,:].astype(f32)+bias
        mid=src_ref[rows,:]+gate*br
        branch_ref[rows,:]=br; middle_ref[rows,:]=mid
        shaped_ref[rows,:]=(normed_of(mid)[0]*scale+shift).astype(bf16)
        return 0
    lax.fori_loop(0,8,step,0)

def call_b(chip,far,src,mods,b_out):
    big=sds((512,768),f32)
    return pl.pallas_call(kernel_b,out_shape=(big,big,sds((512,768),bf16)),
        in_specs=[vm()]*5,out_specs=[vm()]*3,
        cost_estimate=pl.CostEstimate(flops=10**7,bytes_accessed=7*10**6,transcendentals=0),
    )(chip,far,src,mods,b_out.astype(f32)[None])

def kernel_d(chip_ref, far_ref, branch_ref, middle_ref, cot_ref, mods_ref, gm_ref, ga_ref, sums_ref):
    gate=mods_ref[2:3,:]; scale=1.0+mods_ref[4:5,:]
    def step(r,acc):
        rows=at(r*64,64)
        gs=chip_ref[rows,:].astype(f32)+far_ref[rows,:].astype(f32)
        n,rs=normed_of(middle_ref[rows,:])
        gn=gs*scale
        gm=cot_ref[rows,:].astype(f32)+rs*(gn-jnp.mean(gn,axis=-1,keepdims=True)-n*jnp.mean(gn*n,axis=-1,keepdims=True))
        gm_ref[rows,:]=gm
        ga_ref[rows,:]=(gm*gate).astype(bf16)
        return tuple(o+jnp.sum(v,axis=0,keepdims=True) for o,v in zip(acc,(gm*branch_ref[rows,:],gs,gs*n)))
    acc=lax.fori_loop(0,8,step,tuple(jnp.zeros((1,768),f32) for _ in range(3)))
    for t in range(3): sums_ref[t:t+1,:]=acc[t]

def call_d(chip,far,branch,middle,cot,mods):
    return pl.pallas_call(kernel_d,out_shape=(sds((512,768),f32),sds((512,768),bf16),sds((8,768),f32)),
        in_specs=[vm()]*6,out_specs=[vm()]*3,
        cost_estimate=pl.CostEstimate(flops=10**7,bytes_accessed=8*10**6,transcendentals=0),
    )(chip,far,branch,middle,cot,mods)

def kernel_e(core_ref, own_ref, other_ref, q_ref, k_ref, v_ref, lse_ref, wqkv_ref, wout_ref,
             gb_ref, gp_ref, sums_ref, keep_ref, send_ref, mix):
    core=core_ref[0]
    for half_ref, h in ((own_ref,core),(other_ref,1-core)):
        for x in range(2):
            for g in range(4):
                gb_ref[at(g*256+(8*x+4*h)*16,64),:]=half_ref[x*256+g*64:x*256+g*64+64,:]
    masks=head_masks()
    for g in range(4):
        mix[g,0:16,:]=jnp.zeros((16,768),bf16)
        mix[g,272:288,:]=jnp.zeros((16,768),bf16)
    def attend(g,total):
        rows=at(g*256,256)
        gb=gb_ref[rows,:]
        ga=dot_nn(gb,wout_ref[...]).astype(bf16)
        q=q_ref[rows,:]; k=k_ref[rows,:]; v=v_ref[rows,:]
        zero=jnp.zeros_like(q)
        gq=jnp.zeros((256,192),f32); gk=gq; gv=gq
        for h in range(3):
            s=dot_nt(jnp.where(masks[h],q,zero),k)*0.125
            p=jnp.exp(s-lse_ref[rows,h:h+1])
            gp=dot_nt(jnp.where(masks[h],ga,zero),v)
            ds=(p*(gp-jnp.sum(p*gp,axis=-1,keepdims=True))).astype(bf16)
            gq=jnp.where(masks[h],dot_nn(ds,k),gq)
            gk=jnp.where(masks[h],dot_tn(ds,q),gk)
            gv=jnp.where(masks[h],dot_tn(p.astype(bf16),ga),gv)
        gq=(gq*0.125).astype(bf16); gk=(gk*0.125).astype(bf16); gv=gv.astype(bf16)
        gp_ref[rows,:]=jnp.concatenate([gq,gk,gv],axis=1)
        gm=dot_nt(gq,wqkv_ref[0])+dot_nt(gk,wqkv_ref[1])+dot_nt(gv,wqkv_ref[2])
        mix[g,16:272,:]=gm.astype(bf16)
        return total+jnp.sum(gb.astype(f32),axis=0,keepdims=True)
    sums_ref[0:1,:]=lax.fori_loop(0,4,attend,jnp.zeros((1,768),f32))
    for out_ref, h in ((keep_ref,core),(send_ref,1-core)):
        for x in range(2):
            t=2*x+h
            for g in range(4):
                out_ref[x*320+g*64:x*320+g*64+64,:]=mix[g,pl.ds(pl.multiple_of((1+4*t)*16,16),64),:]
            for b in range(2):
                out_ref[x*320+256+b*16:x*320+272+b*16,:]=mix[2+b,pl.ds(pl.multiple_of(4*t*16,16),16),:]
                out_ref[x*320+288+b*16:x*320+304+b*16,:]=mix[b,pl.ds(pl.multiple_of((4*t+5)*16,16),16),:]

def call_e(core,own,other,q,k,v,lse,wqkv,w_out):
    head=sds((1024,192),bf16); halo=sds((640,768),bf16)
    return pl.pallas_call(kernel_e,out_shape=(sds((1024,768),bf16),sds((1024,576),bf16),sds((8,768),f32),halo,halo),
        in_specs=[sm()]+[vm()]*8,out_specs=[vm()]*5,
        scratch_shapes=[pltpu.VMEM((4,288,768),bf16)],
        compiler_params=pltpu.CompilerParams(vmem_limit_bytes=56<<20),
        cost_estimate=pl.CostEstimate(flops=3*10**9,bytes_accessed=12*10**6,transcendentals=10**6),
    )(core,own,other,q,k,v,lse,wqkv,w_out)

def kernel_f(pos_ref, chip_ref, far_ref, tok_ref, gmid_ref, mods_ref, k_ref, out_ref, sums_ref, grid, shp, gsh, gmn):
    side=pos_ref[1]; place_t=pos_ref[2]
    grid[...]=jnp.zeros_like(grid)
    shift=mods_ref[0:1,:]; scale=1.0+mods_ref[1:2,:]
    def fetch(start,rows):
        keep=chip_ref[pl.ds(pl.multiple_of(side*320+start,16),rows),:].astype(f32)
        return (keep+far_ref[start:start+rows,:].astype(f32)).astype(bf16).astype(f32)
    for g in range(4):
        a,b=g//2,g%2
        v=fetch(g*64,64)
        gm=gmid_ref[pl.ds(pl.multiple_of(side*256+g*64,64),64),:]
        for ii in range(4):
            for tile in range(6):
                cols=slice(tile*128,tile*128+128)
                grid[tile,strided(place(2*ii+a,b)),:]=v[ii*16:ii*16+16,cols]
                gmn[tile,strided((2*ii+a)*32+b),:]=gm[ii*16:ii*16+16,cols]
    for b in range(2):
        up=fetch(256+b*16,16); dn=fetch(288+b*16,16)
        for tile in range(6):
            cols=slice(tile*128,tile*128+128)
            grid[tile,strided(place(-1,b)),:]=up[:,cols]
            grid[tile,strided(place(8,b)),:]=dn[:,cols]
    def norm(r,_):
        n,_r=normed_of(tok_ref[pl.ds(pl.multiple_of(place_t*256+r*32,32),32),:].astype(f32))
        y=n*scale+shift
        for tile in range(6):
            shp[tile,at(r*32,32),:]=y[:,tile*128:tile*128+128]
        return 0
    lax.fori_loop(0,8,norm,0)
    def back(tile,_):
        cols=pl.ds(pl.multiple_of(tile*128,128),128)
        taps=[k_ref[t:t+1,cols] for t in range(9)]
        def row(i,acc):
            seen=patch(grid,tile,i)
            acc=list(acc)
            for a in range(2):
                for b in range(2):
                    here=shp[tile,strided((2*i+a)*32+b),:]
                    total=None
                    for t in range(9):
                        s=seen[a+2-t//3][b+2-t%3]
                        total=taps[t]*s if total is None else total+taps[t]*s
                        p=here*s
                        acc[t]=acc[t]+(p[:8]+p[8:])
                    gsh[tile,strided((2*i+a)*32+b),:]=total
            return tuple(acc)
        acc=lax.fori_loop(0,4,row,tuple(jnp.zeros((8,128),f32) for _ in range(9)))
        for t in range(9):
            sums_ref[t:t+1,cols]=jnp.sum(acc[t],axis=0,keepdims=True)
        return 0
    lax.fori_loop(0,6,back,0)
    def fin(r,acc):
        n,rs=normed_of(tok_ref[pl.ds(pl.multiple_of(place_t*256+r*32,32),32),:].astype(f32))
        gs=jnp.concatenate([gsh[tile,at(r*32,32),:] for tile in range(6)],axis=1)
        gm=jnp.concatenate([gmn[tile,at(r*32,32),:] for tile in range(6)],axis=1)
        gn=gs*scale
        out_ref[at(r*32,32),:]=gm+rs*(gn-jnp.mean(gn,axis=-1,keepdims=True)-n*jnp.mean(gn*n,axis=-1,keepdims=True))
        return (acc[0]+jnp.sum(gs,axis=0,keepdims=True),acc[1]+jnp.sum(gs*n,axis=0,keepdims=True))
    acc=lax.fori_loop(0,8,fin,tuple(jnp.zeros((1,768),f32) for _ in range(2)))
    sums_ref[9:10,:]=acc[0]; sums_ref[10:11,:]=acc[1]

def call_f(pos,chip,far,tokens,gmid,mods,k):
    return pl.pallas_call(kernel_f,out_shape=(sds((256,768),f32),sds((16,768),f32)),
        in_specs=[sm()]+[vm()]*6,out_specs=[vm()]*2,
        scratch_shapes=[pltpu.VMEM((6,10*PITCH+16,128),f32)]+[pltpu.VMEM((6,256,128),f32)]*3,
        compiler_params=pltpu.CompilerParams(vmem_limit_bytes=56<<20),
        cost_estimate=pl.CostEstimate(flops=10**7,bytes_accessed=6*10**6,transcendentals=0),
    )(pos,chip,far,tokens,gmid,mods,k.astype(f32))

def kernel_p(core_ref, live_ref, cot_ref, mods_ref, gb_ref, half_ref, xs):
    core=core_ref[0]; live=live_ref[0]
    def spread(i,_):
        x=cot_ref[at(i*64,64),:].astype(f32)*live
        for tile in range(6):
            xs[tile,at(i*64,64),:]=x[:,tile*128:tile*128+128]
        return 0
    lax.fori_loop(0,16,spread,0)
    def group(tile,_):
        cols=pl.ds(pl.multiple_of(tile*128,128),128)
        gate=mods_ref[5:6,cols]
        def row(i,_):
            for g in range(4):
                gb_ref[at(g*256+i*16,16),cols]=(xs[tile,strided((2*i+g//2)*32+g%2),:]*gate).astype(bf16)
            return 0
        lax.fori_loop(0,16,row,0)
        for x in range(2):
            for g in range(4):
                for ii in range(4):
                    i=8*x+4*core+ii
                    half_ref[x*256+g*64+ii*16:x*256+g*64+ii*16+16,cols]=xs[tile,strided((2*i+g//2)*32+g%2),:].astype(bf16)
        return 0
    lax.fori_loop(0,6,group,0)

def call_p(core,live,cot,mods):
    return pl.pallas_call(kernel_p,out_shape=(sds((1024,768),bf16),sds((512,768),bf16)),
        in_specs=[sm(),sm(),vm(),vm()],out_specs=[vm()]*2,
        scratch_shapes=[pltpu.VMEM((6,1024,128),f32)],
        compiler_params=pltpu.CompilerParams(vmem_limit_bytes=56<<20),
        cost_estimate=pl.CostEstimate(flops=10**7,bytes_accessed=4*10**6,transcendentals=0),
    )(core,live,cot,mods)

def kernel_o(pos_ref, live_ref, chip_ref, far_ref, middle_ref, cot_ref, mods_ref, bias_ref, out_ref, sums_ref, nat):
    side=pos_ref[1]; live=live_ref[0]
    gate=mods_ref[5:6,:]; bias=bias_ref[...]
    total=jnp.zeros((1,768),f32)
    for g in range(4):
        a,b=g//2,g%2
        rows=pl.ds(pl.multiple_of(side*256+g*64,64),64)
        br=chip_ref[rows,:].astype(f32)+far_ref[g*64:g*64+64,:].astype(f32)+bias
        res=(middle_ref[rows,:]+gate*br)*live
        total=total+jnp.sum(cot_ref[rows,:].astype(f32)*br,axis=0,keepdims=True)
        for ii in range(4):
            for tile in range(6):
                nat[tile,strided((2*ii+a)*32+b),:]=res[ii*16:ii*16+16,tile*128:tile*128+128]
    sums_ref[0:1,:]=total
    for tile in range(6):
        out_ref[:,tile*128:tile*128+128]=nat[tile,:,:].astype(bf16)

def call_o(pos,live,chip,far,middle,cot,mods,bias):
    return pl.pallas_call(kernel_o,out_shape=(sds((256,768),bf16),sds((8,768),f32)),
        in_specs=[sm(),sm()]+[vm()]*6,out_specs=[vm()]*2,
        scratch_shapes=[pltpu.VMEM((6,256,128),f32)],
        compiler_params=pltpu.CompilerParams(vmem_limit_bytes=56<<20),
        cost_estimate=pl.CostEstimate(flops=10**7,bytes_accessed=4*10**6,transcendentals=0),
    )(pos,live,chip,far,middle,cot,mods,bias.astype(f32)[None])


def kernel_w(split, pos_ref, a_ref, b_ref, *outs):
    m=a_ref.shape[1];
    if split:
        keep_ref,send_ref,total=outs
    else:
        (total,)=outs
    def step(i,_):
        total[at(i*256,256),:]=dot_tn(a_ref[:,at(i*256,256)],b_ref[...])
        return 0
    lax.fori_loop(0,m//256,step,0)
    if split:
        mine=pos_ref[3]%2
        block=m//split
        for j in range(split//2):
            keep_ref[j*block:(j+1)*block,:]=total[pl.ds(pl.multiple_of((2*j+mine)*block,8),block),:]
            send_ref[j*block:(j+1)*block,:]=total[pl.ds(pl.multiple_of((2*j+1-mine)*block,8),block),:].astype(bf16)

def call_w(pos,a,b,n):
    m,w=a.shape[1],b.shape[1]
    split=n if (m//n)%16==0 else 0
    params=dict(in_specs=[sm(),vm(),vm()],
        compiler_params=pltpu.CompilerParams(vmem_limit_bytes=56<<20),
        cost_estimate=pl.CostEstimate(flops=2*1024*m*w,bytes_accessed=6*10**6,transcendentals=0))
    if split:
        return pl.pallas_call(functools.partial(kernel_w,split),out_shape=(sds((m//2,w),f32),sds((m//2,w),bf16)),
            out_specs=[vm()]*2,scratch_shapes=[pltpu.VMEM((m,w),f32)],**params)(pos,a,b)
    return pl.pallas_call(functools.partial(kernel_w,0),out_shape=sds((m,w),f32),out_specs=vm(),**params)(pos,a,b)


def swap(values, axis, bit):
    size = lax.axis_size(axis)
    return lax.ppermute(values, axis, [(i, i ^ bit) for i in range(size)])


def bits_of(axis):
    return [1 << b for b in range(lax.axis_size(axis).bit_length() - 1)]


def take(values, index):
    return lax.dynamic_index_in_dim(values, index, 0, keepdims=False)


def add_low(left, right):
    return (left.astype(f32) + right.astype(f32)).astype(bf16)


def scatter_sum(grad):
    size = lax.axis_size("dp")
    width = grad.shape[1]
    return scatter_rest(grad.reshape(size, grad.shape[0] // size, width), bits_of("dp"))


def scatter_rest(held, bits):
    here = lax.axis_index("dp")
    for bit in bits:
        mine = (here // bit) % 2
        halves = held.reshape((held.shape[0] // 2, 2) + held.shape[1:])
        sent = lax.dynamic_index_in_dim(halves, 1 - mine, 1, keepdims=False).astype(bf16)
        kept = lax.dynamic_index_in_dim(halves, mine, 1, keepdims=False)
        held = kept + swap(sent, "dp", bit).astype(f32)
    return held[0]


def weight_grad(pos, left, right):
    size = lax.axis_size("dp")
    if right.shape[1] % 256:
        return scatter_sum(dot_tn(left, right))
    made = call_w(pos, left, right, size)
    if not isinstance(made, (tuple, list)):
        return scatter_sum(made)
    keep, send = made
    held = keep + swap(send, "dp", 1).astype(f32)
    return scatter_rest(held.reshape(size // 2, -1, held.shape[1]), bits_of("dp")[1:])


def butterfly(values, axis):
    for bit in bits_of(axis):
        values = values + swap(values, axis, bit)
    return values


def gather_xor(values):
    for bit in bits_of("dp"):
        values = jnp.concatenate([values, swap(values, "dp", bit)], axis=0)
    return values


def tree_sum(values):
    while values.shape[0] > 1:
        values = values[0::2] + values[1::2]
    return values[0]


def time_features(timestep, width):
    half_width = width // 2
    freqs = jnp.exp(-math.log(10000.0) * jnp.arange(half_width, dtype=f32) / half_width)
    angles = timestep.astype(f32)[:, None] * freqs[None, :]
    return jnp.concatenate([jnp.cos(angles), jnp.sin(angles)], axis=1)


def shards(
    tokens,
    cotangent,
    item_count,
    timestep,
    class_id,
    class_table,
    w_mod,
    b_mod,
    k_att,
    w_qkv,
    w_out,
    b_out,
    w_up,
    b_up,
    k_ffn,
    w_down,
    b_down,
):
    width = tokens.shape[1]
    place_t = lax.axis_index("tensor")
    core = place_t % 2
    side = place_t // 2
    here = lax.axis_index("dp")
    pos = jnp.stack([core, side, place_t, here]).astype(jnp.int32)
    live = (item_count > 0).astype(f32)

    cond = time_features(timestep, width) + class_table[class_id[0]].astype(f32)[None, :]
    act_low = jax.nn.silu(cond).astype(bf16)
    mods = (dot_nt(act_low, w_mod) + b_mod.astype(f32)).reshape(6, width)
    card = jnp.concatenate([cond, jnp.broadcast_to(class_id.astype(f32)[:, None], (1, 128))], axis=1)
    cards = gather_xor(card)
    w_three = jnp.swapaxes(w_qkv, 0, 1)

    mixed, query, keys, vals, attended, log_total, source, keep, send = call_a(
        pos, tokens, mods, k_att, w_three, w_out
    )
    chip = add_low(keep, swap(send, "tensor", 1))
    far = swap(chip, "tensor", 2)
    grad_branch_ffn, cot_half = call_p(pos, live, cotangent, mods)
    branch, middle, shaped_own = call_b(chip, far, source, mods, b_out)
    shaped_other = swap(shaped_own, "tensor", 1)

    shaped, activated, grad_hidden, sums_c, b_keep, b_send, g_keep, g_send = call_c(
        pos, shaped_own, shaped_other, grad_branch_ffn, w_up, b_up, k_ffn, w_down
    )
    chip = add_low(g_keep, swap(g_send, "tensor", 1))
    far = swap(chip, "tensor", 2)
    grad_w_down = weight_grad(pos, grad_branch_ffn, activated)
    grad_w_up = weight_grad(pos, shaped, grad_hidden)
    grad_middle, attn_own, sums_d = call_d(chip, far, branch, middle, cot_half, mods)
    attn_other = swap(attn_own, "tensor", 1)

    chip = add_low(b_keep, swap(b_send, "tensor", 1))
    far = swap(take(chip.reshape(2, -1, width), 1 - side), "tensor", 2)
    block_out, sums_o = call_o(pos, live, chip, far, middle, cot_half, mods, b_down)

    grad_branch, grad_project, sums_e, h_keep, h_send = call_e(
        pos, attn_own, attn_other, query, keys, vals, log_total, w_three, w_out
    )
    chip = add_low(h_keep, swap(h_send, "tensor", 1))
    far = swap(take(chip.reshape(2, -1, width), 1 - side), "tensor", 2)
    grad_w_out = weight_grad(pos, grad_branch, attended)
    grad_w_qkv = weight_grad(pos, mixed, grad_project)
    grad_w_qkv = grad_w_qkv.reshape(grad_w_qkv.shape[0], 3, -1)
    grad_tokens, sums_f = call_f(pos, chip, far, tokens, grad_middle, mods, k_att)

    early = butterfly(jnp.concatenate([sums_c[:11], sums_e[:1]]), "dp")

    once = jnp.where(side == 0, 1.0, 0.0)
    late = jnp.concatenate([sums_f[9:11], sums_d[:3] * once, sums_o[:1], sums_f[:9]])
    late = butterfly(late, "tensor")
    grad_k_att = butterfly(late[6:], "dp")
    grad_modulate = gather_xor(late[:6].reshape(1, -1).astype(bf16))

    grad_b_mod = tree_sum(grad_modulate.astype(f32))
    conds = cards[:, :width]
    classes = cards[:, width]
    act, silu_back = jax.vjp(jax.nn.silu, conds)
    share = w_mod.shape[0] // lax.axis_size("dp")
    own_rows = lax.dynamic_slice_in_dim(grad_modulate, here * share, share, 1)
    grad_w_mod = dot_tn(own_rows, act.astype(bf16))
    grad_cond = silu_back(dot_nn(grad_modulate, w_mod))[0]
    same = (classes[:, None] == classes[None, :]).astype(f32)
    class_rows = tree_sum(same[:, :, None] * grad_cond[:, None, :])
    grad_class = jnp.zeros(class_table.shape, f32).at[classes.astype(jnp.int32)].set(class_rows)

    return (
        block_out,
        grad_tokens,
        grad_class,
        grad_w_mod,
        grad_b_mod,
        grad_k_att,
        grad_w_qkv,
        grad_w_out,
        early[11],
        grad_w_up,
        early[9],
        early[:9],
        grad_w_down,
        early[10],
    )


def solution(mesh):
    placed = (
        P("dp", None),
        P("dp", None),
        P("dp"),
        P("dp"),
        P("dp"),
        P(),
        P(),
        P(),
        P(),
        P(None, None, "tensor"),
        P(None, "tensor"),
        P(),
        P(None, "tensor"),
        P("tensor"),
        P(None, "tensor"),
        P(None, "tensor"),
        P(),
    )
    return jax.shard_map(
        shards,
        mesh=mesh,
        in_specs=placed,
        out_specs=(
            P(("dp", "tensor"), None),
            P(("dp", "tensor"), None),
            P(),
            P("dp", None),
            P(),
            P(),
            P("dp", None, "tensor"),
            P("dp", "tensor"),
            P(),
            P("dp", "tensor"),
            P("tensor"),
            P(None, "tensor"),
            P("dp", "tensor"),
            P(),
        ),
        check_vma=False,
    )
```

time: 353 us -> 267 us (0.76); the launches traced: 348 us -> 266 us
  local copies, waits for them, and re-layouts: 113 us -> 18.5 us
  Pallas kernels: 0 us -> 91.9 us
  other arithmetic: 94.7 us -> 17.8 us
  matrix products: 45.9 us -> 15.5 us
  waiting for transfers between devices: 49.3 us -> 79 us
    pallas_call x0 -> x10, Pallas kernels: none -> 91.9 us  [the longest x1 22.7 us: call_c(): pl.pallas_call(kernel_c, out_shape=(full, full, full, jax.ShapeDtypeStruc...]
    dot_general x27 -> x5, matrix products: 45.9 us -> 15.5 us  [the longest x3 6.44 us: dot_tn(): lax.dot_general(l, r, (((0,), (0,)), ((), ())), preferred_element_type=f32)]
    ppermute x36, waiting for transfers between devices: 49.3 us -> 79 us  [swap(): return lax.ppermute(values, axis, [(i, i ^ bit) for i in range(size)])]
    reduce_sum x18 -> x0, other arithmetic: 26.9 us -> none  [the longest x2 9.72 us: depthwise_back(): kernel_rows.append(jnp.sum(field * seen, axis=(0, 1)))]
    convert_element_type x13 -> x2, other arithmetic: 23.4 us -> 1.25 us  [the longest x1 0.62 us: call_a(): k.astype(f32)]
    convert_element_type x23 -> x9, local copies, waits for them, and re-layouts: 22.5 us -> 0.92 us  [scatter_rest(): lax.dynamic_index_in_dim(halves, 1 - mine, 1, keepdims=False).astype(bf16)]
    reshape x14 -> x1, local copies, waits for them, and re-layouts: 18.6 us -> 0.61 us  [shards(): mods = (dot_nt(act_low, w_mod) + b_mod.astype(f32)).reshape(6, width)]
    another operation x26 -> x1, local copies, waits for them, and re-layouts: 18.5 us -> 1.11 us  [scatter_rest(): halves = held.reshape((held.shape[0] // 2, 2) + held.shape[1:])]
  transfers between devices with their start and end apart: 36 -> 36, of which waited for: 15 -> 21; matrix products, arithmetic and copies ran while one was open for 37% -> 13% of each run, Pallas kernels for 0% -> 21%
where the time goes in v2:
time: 267 us; the launch traced here: 266 us
  Pallas kernels  91.9 us (34%)
  waiting for transfers between devices  79 us (30%)
  starting transfers between devices  40.1 us (15%)
  local copies, waits for them, and re-layouts  18.5 us (7%)
  other arithmetic  17.8 us (7%)
  matrix products  15.5 us (6%)
  between operations  3.19 us (1%)
    ppermute x36, waiting for transfers between devices, swap(): return lax.ppermute(values, axis, [(i, i ^ bit) for i in range(size)])  79 us
    ppermute x36, starting transfers between devices, swap(): return lax.ppermute(values, axis, [(i, i ^ bit) for i in range(size)])  40.1 us
    pallas_call x1, Pallas kernels, call_c(): pl.pallas_call(kernel_c, out_shape=(full, full, full, jax.ShapeDtypeStruc...  22.7 us
    pallas_call x1, Pallas kernels, call_a(): pl.pallas_call(kernel_a, out_shape=(sds((1024, 768), bf16), head, head, h...  17.2 us
    pallas_call x1, Pallas kernels, call_e(): pl.pallas_call(kernel_e, out_shape=(sds((1024, 768), bf16), sds((1024, 57...  13.3 us
    pallas_call x2, Pallas kernels, call_w(): pl.pallas_call(functools.partial(kernel_w, split), out_shape=(sds((m // 2...  10.4 us
    unnamed x76, local copies, waits for them, and re-layouts  8.55 us
    pallas_call x1, Pallas kernels, call_f(): pl.pallas_call(kernel_f, out_shape=(sds((256, 768), f32), sds((16, 768),...  8.55 us
  transfers between devices with their start and end apart: 36, of which 21 were waited for; matrix products, arithmetic and copies ran while one was open for 13% of the time, Pallas kernels for 21%

profile of v2, /device:TPU:0, one launch (start us, length us, event | category | flops | bytes accessed | tf_op | source)
XLA Modules:
  0.0 266.0 jit_solution(14848535850357404257)
XLA Ops:
  2.8 5.0 %convolution_reduce_fusion = f32[4608]{0:T(1024)S(1)} fusion(bf16[4608,768]{1,0:T(8,128)(2,1)} %param.23, f32[1,768]{1,0:T(1,128)S(1)} %fusion.20), kind=kOutput, calls=%fused_computation.9 | convolution fusion | flops 7081728 | bytes 7099392 | tf_op jit(solution)/shard_map/dot_general | solution.py:20
  12.1 17.2 %shard_map.272 = (bf16[1024,768]{1,0:T(8,128)(2,1)}, bf16[1024,192]{1,0:T(8,128)(2,1)}, bf16[1024,192]{1,0:T(8,128)(2,1)}, bf16[1024,192]{1,0:T(8,128)(2,1)}, bf...) custom-call(s32[4]{0:T(128)} %pad_add_fusion.core_ref.pos_ref, ...), custom_call_target="tpu_custom_call" | custom-call | flops 3000000000 | bytes 12000000 | tf_op jit(solution)/shard_map/pallas_call | solution.py:212
  33.2 2.9 %collective-permute-start.1 = (bf16[512,768]{1,0:T(8,128)(2,1)S(1)}, bf16[512,768]{1,0:T(8,128)(2,1)S(1)}, u32[]{:S(2)}, u32[]{:S(2)}) collective-permute-start(bf16[512,768]{1,0:T(8,128)(2,1)S(1)} %add_convert_fusion.3.chip_ref), channel_id=1, source_target_pairs={{0,2},{1,3},{2,0},{3,1},{4,6},{5,7},{6,4},{7,5},{8,10},{9,11},{10,... | collective-permute-start | bytes 2359304 | tf_op jit(solution)/shard_map/ppermute | solution.py:467
  36.7 17.3 %collective-permute-done.1.far_ref = bf16[512,768]{1,0:T(8,128)(2,1)S(1)} collective-permute-done((bf16[512,768]{1,0:T(8,128)(2,1)S(1)}, bf16[512,768]{1,0:T(8,128)(2,1)S(1)}, u32[]{:S(2)}, u32[]{:S(2)}) %collective-permute-start.1) | collective-permute-done | bytes 786464 | tf_op jit(solution)/shard_map/ppermute | solution.py:467
  54.9 5.4 %shard_map.273 = (f32[512,768]{1,0:T(8,128)}, f32[512,768]{1,0:T(8,128)}, bf16[512,768]{1,0:T(8,128)(2,1)}) custom-call(bf16[512,768]{1,0:T(8,128)(2,1)} %copy-done.2, bf16[512,768]{1,0:T(8,128)(2,1)} %copy-done.12, f32[512,768]{1,0:T(8,128)} %get-tuple-element.54.src_ref, f32[6,768]{1,0:T(8,128)} %reshape.168.mods_ref, f32[1,768]{1,0:T(1,128)} %reshape.173.bout_ref), custom_call_target="tpu_custom_call" | custom-call | flops 10000000 | bytes 7000000 | tf_op jit(solution)/shard_map/pallas_call | solution.py:234
  64.0 4.5 %shard_map.274 = (bf16[1024,768]{1,0:T(8,128)(2,1)}, bf16[512,768]{1,0:T(8,128)(2,1)}) custom-call(s32[4]{0:T(128)} %pad_add_fusion.core_ref.pos_ref, f32[1]{0:T(128)S(6)} %convert_element_type.189.live_ref, bf16[1024,768]{1,0:T(8,128)(2,1)} %cot_ref.1, f32[6,768]{1,0:T(8,128)} %reshape.168.mods_ref), custom_call_target="tpu_custom_call" | custom-call | flops 10000000 | bytes 4000000 | tf_op jit(solution)/shard_map/pallas_call | solution.py:403
  71.0 22.7 %shard_map.275 = (bf16[1024,768]{1,0:T(8,128)(2,1)}, bf16[1024,768]{1,0:T(8,128)(2,1)}, bf16[1024,768]{1,0:T(8,128)(2,1)}, f32[16,768]{1,0:T(8,128)}, bf16[512,7...) custom-call(s32[4]{0:T(128)} %pad_add_fusion.core_ref.pos_ref, ...), custom_call_target="tpu_custom_call" | custom-call | flops 5000000000 | bytes 12000000 | tf_op jit(solution)/shard_map/pallas_call | solution.py:124
  93.8 5.1 %shard_map.280 = (f32[384,768]{1,0:T(8,128)}, bf16[384,768]{1,0:T(8,128)(2,1)}) custom-call(s32[4]{0:T(128)} %pad_add_fusion.core_ref.pos_ref, bf16[1024,768]{1,0:T(8,128)(2,1)} %get-tuple-element.83.a_ref, bf16[1024,768]{1,0:T(8,128)(2,1)} %get-tuple-element.84.b_ref), custom_call_target="tpu_custom_call" | custom-call | flops 1207959552 | bytes 6000000 | tf_op jit(solution)/shard_map/pallas_call | solution.py:460
  99.4 2.7 %collective-permute-start.12 = (f32[4,896]{1,0:T(4,128)S(1)}, f32[4,896]{1,0:T(4,128)S(1)}, u32[]{:S(2)}, u32[]{:S(2)}) collective-permute-start(f32[4,896]{1,0:T(4,128)S(1)} %pad_maximum_fusion.8), channel_id=1, source_target_pairs={{0,16},{4,20},{8,24},{12,28},{16,0},{20,4},{24,8},{28,12},{1,17},{... | collective-permute-start | bytes 43016 | tf_op jit(solution)/shard_map/ppermute | solution.py:467
  104.9 5.3 %shard_map.281 = (f32[384,768]{1,0:T(8,128)}, bf16[384,768]{1,0:T(8,128)(2,1)}) custom-call(s32[4]{0:T(128)} %pad_add_fusion.core_ref.pos_ref, bf16[1024,768]{1,0:T(8,128)(2,1)} %get-tuple-element.56.gb_ref.a_ref, bf16[1024,768]{1,0:T(8,128)(2,1)} %get-tuple-element.87.b_ref), custom_call_target="tpu_custom_call" | custom-call | flops 1207959552 | bytes 6000000 | tf_op jit(solution)/shard_map/pallas_call | solution.py:460
  116.0 10.9 %collective-permute-done.33 = bf16[384,768]{1,0:T(8,128)(2,1)S(1)} collective-permute-done((bf16[384,768]{1,0:T(8,128)(2,1)}, bf16[384,768]{1,0:T(8,128)(2,1)S(1)}, u32[]{:S(2)}, u32[]{:S(2)}) %collective-permute-start.33) | collective-permute-done | bytes 589856 | tf_op jit(solution)/shard_map/ppermute | solution.py:467
  136.6 12.1 %collective-permute-done.6.far_ref = bf16[512,768]{1,0:T(8,128)(2,1)S(1)} collective-permute-done((bf16[512,768]{1,0:T(8,128)(2,1)S(1)}, bf16[512,768]{1,0:T(8,128)(2,1)S(1)}, u32[]{:S(2)}, u32[]{:S(2)}) %collective-permute-start.6) | collective-permute-done | bytes 786464 | tf_op jit(solution)/shard_map/ppermute | solution.py:467
  149.6 6.6 %shard_map.277 = (f32[512,768]{1,0:T(8,128)}, bf16[512,768]{1,0:T(8,128)(2,1)}, f32[8,768]{1,0:T(8,128)}) custom-call(bf16[512,768]{1,0:T(8,128)(2,1)} %copy-done.3, bf16[512,768]{1,0:T(8,128)(2,1)} %copy-done.13, f32[512,768]{1,0:T(8,128)} %get-tuple-element.64.branch_ref, f32[512,768]{1,0:T(8,128)} %get-tuple-element.59.middle_ref, ...), custom_call_target="tpu_custom_call" | custom-call | flops 10000000 | bytes 8000000 | tf_op jit(solution)/shard_map/pallas_call | solution.py:254
  160.5 6.1 %collective-permute-done.35 = bf16[1,96,768]{2,1,0:T(8,128)(2,1)S(1)} collective-permute-done((bf16[1,96,768]{2,1,0:T(8,128)(2,1)S(1)}, bf16[1,96,768]{2,1,0:T(8,128)(2,1)S(1)}, u32[]{:S(2)}, u32[]{:S(2)}) %collective-permute-start.35) | collective-permute-done | bytes 147488 | tf_op jit(solution)/shard_map/ppermute | solution.py:467
  167.3 3.2 %shard_map.276 = (bf16[256,768]{1,0:T(8,128)(2,1)}, f32[8,768]{1,0:T(8,128)}) custom-call(s32[4]{0:T(128)} %pad_add_fusion.core_ref.pos_ref, f32[1]{0:T(128)S(6)} %convert_element_type.189.live_ref, bf16[512,768]{1,0:T(8,128)(2,1)} %copy-done.1, bf16[256,768]{1,0:T(8,128)(2,1)} %collective-permute-done.4.far_ref, f32[512,768]{1,0:T(8,128)} %get-tuple-element.59.middle_ref, ...), custom_call_target="tpu_custom_call" | custom-call | flops 10000000 | bytes 4000000 | tf_op jit(solution)/shard_map/pallas_call | solution.py:428
  172.1 13.3 %shard_map.278 = (bf16[1024,768]{1,0:T(8,128)(2,1)}, bf16[1024,576]{1,0:T(8,128)(2,1)}, f32[8,768]{1,0:T(8,128)}, bf16[640,768]{1,0:T(8,128)(2,1)}, bf16[640,768]{1,0:T(8,128)(2,1)}) custom-call(s32[4]{0:T(128)} %pad_add_fusion.core_ref.pos_ref, bf16[512,768]{1,0:T(8,128)(2,1)} %get-tuple-element.65.own_ref, bf16[512,768]{1,0:T(8,128)(2,1)} %copy-done.32, ...), custom_call_target="tpu_custom_call" | custom-call | flops 3000000000 | bytes 12000000 | tf_op jit(solution)/shard_map/pallas_call | solution.py:302
  192.3 2.7 %fusion.32 = f32[768,576]{1,0:T(8,128)S(1)} fusion(bf16[1024,768]{1,0:T(8,128)(2,1)S(1)} %copy-done.34, bf16[1024,576]{1,0:T(8,128)(2,1)} %get-tuple-element.78), kind=kOutput, calls=%fused_computation.95 | convolution fusion | flops 905969664 | bytes 4521984 | tf_op jit(solution)/shard_map/dot_general | solution.py:21
  195.0 2.8 %collective-permute-done.27 = f32[12,768]{1,0:T(8,128)S(1)} collective-permute-done((f32[12,768]{1,0:T(8,128)S(1)}, f32[12,768]{1,0:T(8,128)S(1)}, u32[]{:S(2)}, u32[]{:S(2)}) %collective-permute-start.27) | collective-permute-done | bytes 36896 | tf_op jit(solution)/shard_map/ppermute | solution.py:467
  198.8 3.1 %collective-permute-done.28 = f32[12,768]{1,0:T(8,128)S(1)} collective-permute-done((f32[12,768]{1,0:T(8,128)S(1)}, f32[12,768]{1,0:T(8,128)S(1)}, u32[]{:S(2)}, u32[]{:S(2)}) %collective-permute-start.28) | collective-permute-done | bytes 36896 | tf_op jit(solution)/shard_map/ppermute | solution.py:467
  204.5 3.1 %collective-permute-done.29 = f32[12,768]{1,0:T(8,128)} collective-permute-done((f32[12,768]{1,0:T(8,128)S(1)}, f32[12,768]{1,0:T(8,128)}, u32[]{:S(2)}, u32[]{:S(2)}) %collective-permute-start.29) | collective-permute-done | bytes 36896 | tf_op jit(solution)/shard_map/ppermute | solution.py:467
  215.6 3.3 %collective-permute-done.26 = bf16[1,96,192]{2,1,0:T(8,128)(2,1)S(1)} collective-permute-done((bf16[1,96,192]{2,1,0:T(8,128)(2,1)S(1)}, bf16[1,96,192]{2,1,0:T(8,128)(2,1)S(1)}, u32[]{:S(2)}, u32[]{:S(2)}) %collective-permute-start.26) | collective-permute-done | bytes 36896 | tf_op jit(solution)/shard_map/ppermute | solution.py:467
  221.8 8.5 %shard_map.279 = (f32[256,768]{1,0:T(8,128)}, f32[16,768]{1,0:T(8,128)}) custom-call(s32[4]{0:T(128)} %pad_add_fusion.core_ref.pos_ref, bf16[640,768]{1,0:T(8,128)(2,1)} %copy-done, bf16[320,768]{1,0:T(8,128)(2,1)} %copy-done.15, bf16[1024,768]{1,0:T(8,128)(2,1)} %tok_ref.3, f32[512,768]{1,0:T(8,128)} %get-tuple-element.72.gmid_ref, ...), custom_call_target="tpu_custom_call" | custom-call | flops 10000000 | bytes 6000000 | tf_op jit(solution)/shard_map/pallas_call | solution.py:371
  238.1 4.9 %collective-permute-done.22 = bf16[2,96,576]{2,1,0:T(8,128)(2,1)S(1)} collective-permute-done((bf16[2,96,576]{2,1,0:T(8,128)(2,1)S(1)}, bf16[2,96,576]{2,1,0:T(8,128)(2,1)S(1)}, u32[]{:S(2)}, u32[]{:S(2)}) %collective-permute-start.22) | collective-permute-done | bytes 221216 | tf_op jit(solution)/shard_map/ppermute | solution.py:467
  256.1 4.0 %fusion.8 = f32[8,768]{1,0:T(8,128)S(1)} fusion(f32[4,896]{1,0:T(4,128)S(1)} %copy-done.20, f32[2,896]{1,0:T(2,128)S(1)} %collective-permute-done.11, f32[1,896]{1,0:T(1,128)S(1)} %collective-permute-done.10, f32[1,896]{1,0:T(1,128)S(1)} %concatenate.38, bf16[8,4608]{1,0:T(8,128)(2,1)S(1)} %pad_maximum_fusion, bf16[4608,768]{1,0:T(8,128)(2,1)} %param.23), kind=kOutput, calls=%fused_computation.46 | convolution fusion | flops 56696832 | bytes 7204864 | tf_op jit(solution)/shard_map/dot_general | solution.py:19
  (217 shorter events, 90.1 us)
Async XLA Ops:
  33.2 20.8 %collective-permute-start.1 = (bf16[512,768]{1,0:T(8,128)(2,1)S(1)}, bf16[512,768]{1,0:T(8,128)(2,1)S(1)}, u32[]{:S(2)}, u32[]{:S(2)}) collective-permute-start(bf16[512,768]{1,0:T(8,128)(2,1)S(1)} %add_convert_fusion.3.chip_ref), channel_id=1, source_target_pairs={{0,2},{1,3},{2,0},{3,1},{4,6},{5,7},{6,4},{7,5},{8,10},{9,11},{10,... | collective-permute-start | bytes 2359304 | tf_op jit(solution)/shard_map/ppermute | solution.py:467
  60.3 9.8 %collective-permute-start.2 = (bf16[512,768]{1,0:T(8,128)(2,1)}, bf16[512,768]{1,0:T(8,128)(2,1)S(1)}, u32[]{:S(2)}, u32[]{:S(2)}) collective-permute-start(bf16[512,768]{1,0:T(8,128)(2,1)} %get-tuple-element.55.own_ref), channel_id=1, source_target_pairs={{0,1},{1,0},{2,3},{3,2},{4,5},{5,4},{6,7},{7,6},{8,9},{9,8},{10,11... | collective-permute-start | bytes 2359304 | tf_op jit(solution)/shard_map/ppermute | solution.py:467
  60.3 8.2 %collective-permute-start.10 = (f32[1,896]{1,0:T(1,128)S(1)}, f32[1,896]{1,0:T(1,128)S(1)}, u32[]{:S(2)}, u32[]{:S(2)}) collective-permute-start(f32[1,896]{1,0:T(1,128)S(1)} %concatenate.38), channel_id=1, source_target_pairs={{0,4},{4,0},{8,12},{12,8},{16,20},{20,16},{24,28},{28,24},{1,5},{5... | collective-permute-start | bytes 10760 | tf_op jit(solution)/shard_map/ppermute | solution.py:467
  68.5 30.9 %collective-permute-start.11 = (f32[2,896]{1,0:T(2,128)S(1)}, f32[2,896]{1,0:T(2,128)S(1)}, u32[]{:S(2)}, u32[]{:S(2)}) collective-permute-start(f32[2,896]{1,0:T(2,128)S(1)} %pad_maximum_fusion.9), channel_id=1, source_target_pairs={{0,8},{4,12},{8,0},{12,4},{16,24},{20,28},{24,16},{28,20},{1,9},{5... | collective-permute-start | bytes 21512 | tf_op jit(solution)/shard_map/ppermute | solution.py:467
  98.9 16.4 %collective-permute-start.30 = (bf16[384,768]{1,0:T(8,128)(2,1)}, bf16[384,768]{1,0:T(8,128)(2,1)S(1)}, u32[]{:S(2)}, u32[]{:S(2)}) collective-permute-start(bf16[384,768]{1,0:T(8,128)(2,1)} %get-tuple-element.86), channel_id=1, source_target_pairs={{0,4},{4,0},{8,12},{12,8},{16,20},{20,16},{24,28},{28,24},{1,5},{5... | collective-permute-start | bytes 1769480 | tf_op jit(solution)/shard_map/ppermute | solution.py:467
  110.2 16.7 %collective-permute-start.33 = (bf16[384,768]{1,0:T(8,128)(2,1)}, bf16[384,768]{1,0:T(8,128)(2,1)S(1)}, u32[]{:S(2)}, u32[]{:S(2)}) collective-permute-start(bf16[384,768]{1,0:T(8,128)(2,1)} %get-tuple-element.89), channel_id=1, source_target_pairs={{0,4},{4,0},{8,12},{12,8},{16,20},{20,16},{24,28},{28,24},{1,5},{5... | collective-permute-start | bytes 1769480 | tf_op jit(solution)/shard_map/ppermute | solution.py:467
  112.4 17.3 %collective-permute-start.3 = (bf16[512,768]{1,0:T(8,128)(2,1)S(1)}, bf16[512,768]{1,0:T(8,128)(2,1)S(1)}, u32[]{:S(2)}, u32[]{:S(2)}) collective-permute-start(bf16[512,768]{1,0:T(8,128)(2,1)S(1)} %copy-done.30), channel_id=1, source_target_pairs={{0,1},{1,0},{2,3},{3,2},{4,5},{5,4},{6,7},{7,6},{8,9},{9,8},{10,11... | collective-permute-start | bytes 2359304 | tf_op jit(solution)/shard_map/ppermute | solution.py:467
  112.4 15.1 %collective-permute-start.5 = (bf16[512,768]{1,0:T(8,128)(2,1)S(1)}, bf16[512,768]{1,0:T(8,128)(2,1)S(1)}, u32[]{:S(2)}, u32[]{:S(2)}) collective-permute-start(bf16[512,768]{1,0:T(8,128)(2,1)S(1)} %copy-done.31), channel_id=1, source_target_pairs={{0,1},{1,0},{2,3},{3,2},{4,5},{5,4},{6,7},{7,6},{8,9},{9,8},{10,11... | collective-permute-start | bytes 2359304 | tf_op jit(solution)/shard_map/ppermute | solution.py:467
  115.5 15.9 %collective-permute-start.31 = (bf16[2,96,768]{2,1,0:T(8,128)(2,1)S(1)}, bf16[2,96,768]{2,1,0:T(8,128)(2,1)S(1)}, u32[]{:S(2)}, u32[]{:S(2)}) collective-permute-start(bf16[2,96,768]{2,1,0:T(8,128)(2,1)S(1)} %fusion.3), channel_id=1, source_target_pairs={{0,8},{4,12},{8,0},{12,4},{16,24},{20,28},{24,16},{28,20},{1,9},{5... | collective-permute-start | bytes 884744 | tf_op jit(solution)/shard_map/ppermute | solution.py:467
  127.0 9.6 %collective-permute-start.34 = (bf16[2,96,768]{2,1,0:T(8,128)(2,1)S(1)}, bf16[2,96,768]{2,1,0:T(8,128)(2,1)S(1)}, u32[]{:S(2)}, u32[]{:S(2)}) collective-permute-start(bf16[2,96,768]{2,1,0:T(8,128)(2,1)S(1)} %fusion.4), channel_id=1, source_target_pairs={{0,8},{4,12},{8,0},{12,4},{16,24},{20,28},{24,16},{28,20},{1,9},{5... | collective-permute-start | bytes 884744 | tf_op jit(solution)/shard_map/ppermute | solution.py:467
  128.2 20.5 %collective-permute-start.6 = (bf16[512,768]{1,0:T(8,128)(2,1)S(1)}, bf16[512,768]{1,0:T(8,128)(2,1)S(1)}, u32[]{:S(2)}, u32[]{:S(2)}) collective-permute-start(bf16[512,768]{1,0:T(8,128)(2,1)S(1)} %add_convert_fusion.1.chip_ref), channel_id=1, source_target_pairs={{0,2},{1,3},{2,0},{3,1},{4,6},{5,7},{6,4},{7,5},{8,10},{9,11},{10,... | collective-permute-start | bytes 2359304 | tf_op jit(solution)/shard_map/ppermute | solution.py:467
  130.8 36.5 %collective-permute-start.4 = (bf16[256,768]{1,0:T(8,128)(2,1)}, bf16[256,768]{1,0:T(8,128)(2,1)}, u32[]{:S(2)}, u32[]{:S(2)}) collective-permute-start(bf16[256,768]{1,0:T(8,128)(2,1)} %dynamic-slice_bitcast_fusion.1), channel_id=1, source_target_pairs={{0,2},{1,3},{2,0},{3,1},{4,6},{5,7},{6,4},{7,5},{8,10},{9,11},{10,... | collective-permute-start | bytes 1179656 | tf_op jit(solution)/shard_map/ppermute | solution.py:467
  132.1 26.8 %collective-permute-start.32 = (bf16[1,96,768]{2,1,0:T(8,128)(2,1)}, bf16[1,96,768]{2,1,0:T(8,128)(2,1)}, u32[]{:S(2)}, u32[]{:S(2)}) collective-permute-start(bf16[1,96,768]{2,1,0:T(8,128)(2,1)} %dynamic-slice_convert_fusion.2), channel_id=1, source_target_pairs={{0,16},{4,20},{8,24},{12,28},{16,0},{20,4},{24,8},{28,12},{1,17},{... | collective-permute-start | bytes 442376 | tf_op jit(solution)/shard_map/ppermute | solution.py:467
  156.2 15.1 %collective-permute-start.7 = (bf16[512,768]{1,0:T(8,128)(2,1)}, bf16[512,768]{1,0:T(8,128)(2,1)S(1)}, u32[]{:S(2)}, u32[]{:S(2)}) collective-permute-start(bf16[512,768]{1,0:T(8,128)(2,1)} %get-tuple-element.65.own_ref), channel_id=1, source_target_pairs={{0,1},{1,0},{2,3},{3,2},{4,5},{5,4},{6,7},{7,6},{8,9},{9,8},{10,11... | collective-permute-start | bytes 2359304 | tf_op jit(solution)/shard_map/ppermute | solution.py:467
  156.2 10.4 %collective-permute-start.35 = (bf16[1,96,768]{2,1,0:T(8,128)(2,1)S(1)}, bf16[1,96,768]{2,1,0:T(8,128)(2,1)S(1)}, u32[]{:S(2)}, u32[]{:S(2)}) collective-permute-start(bf16[1,96,768]{2,1,0:T(8,128)(2,1)S(1)} %dynamic-slice_convert_fusion.1), channel_id=1, source_target_pairs={{0,16},{4,20},{8,24},{12,28},{16,0},{20,4},{24,8},{28,12},{1,17},{... | collective-permute-start | bytes 442376 | tf_op jit(solution)/shard_map/ppermute | solution.py:467
  185.5 23.5 %collective-permute-start.8 = (bf16[640,768]{1,0:T(8,128)(2,1)}, bf16[640,768]{1,0:T(8,128)(2,1)}, u32[]{:S(2)}, u32[]{:S(2)}) collective-permute-start(bf16[640,768]{1,0:T(8,128)(2,1)} %get-tuple-element.71), channel_id=1, source_target_pairs={{0,1},{1,0},{2,3},{3,2},{4,5},{5,4},{6,7},{7,6},{8,9},{9,8},{10,11... | collective-permute-start | bytes 2949128 | tf_op jit(solution)/shard_map/ppermute | solution.py:467
  189.4 19.1 %collective-permute-start.24 = (bf16[4,96,192]{2,1,0:T(8,128)(2,1)S(1)}, bf16[4,96,192]{2,1,0:T(8,128)(2,1)S(1)}, u32[]{:S(2)}, u32[]{:S(2)}) collective-permute-start(bf16[4,96,192]{2,1,0:T(8,128)(2,1)S(1)} %bitcast.111), channel_id=1, source_target_pairs={{0,4},{4,0},{8,12},{12,8},{16,20},{20,16},{24,28},{28,24},{1,5},{5... | collective-permute-start | bytes 442376 | tf_op jit(solution)/shard_map/ppermute | solution.py:467
  190.7 7.1 %collective-permute-start.27 = (f32[12,768]{1,0:T(8,128)S(1)}, f32[12,768]{1,0:T(8,128)S(1)}, u32[]{:S(2)}, u32[]{:S(2)}) collective-permute-start(f32[12,768]{1,0:T(8,128)S(1)} %pad_maximum_fusion.2), channel_id=1, source_target_pairs={{0,4},{4,0},{8,12},{12,8},{16,20},{20,16},{24,28},{28,24},{1,5},{5... | collective-permute-start | bytes 110600 | tf_op jit(solution)/shard_map/ppermute | solution.py:467
  198.3 33.8 %collective-permute-start.21 = (bf16[4,96,576]{2,1,0:T(8,128)(2,1)S(1)}, bf16[4,96,576]{2,1,0:T(8,128)(2,1)}, u32[]{:S(2)}, u32[]{:S(2)}) collective-permute-start(bf16[4,96,576]{2,1,0:T(8,128)(2,1)S(1)} %fusion.2), channel_id=1, source_target_pairs={{0,4},{4,0},{8,12},{12,8},{16,20},{20,16},{24,28},{28,24},{1,5},{5... | collective-permute-start | bytes 1327112 | tf_op jit(solution)/shard_map/ppermute | solution.py:467
  210.5 10.5 %collective-permute-start.9 = (bf16[320,768]{1,0:T(8,128)(2,1)S(1)}, bf16[320,768]{1,0:T(8,128)(2,1)S(1)}, u32[]{:S(2)}, u32[]{:S(2)}) collective-permute-start(bf16[320,768]{1,0:T(8,128)(2,1)S(1)} %dynamic-slice_bitcast_fusion), channel_id=1, source_target_pairs={{0,2},{1,3},{2,0},{3,1},{4,6},{5,7},{6,4},{7,5},{8,10},{9,11},{10,... | collective-permute-start | bytes 1474568 | tf_op jit(solution)/shard_map/ppermute | solution.py:467
  234.9 8.1 %collective-permute-start.22 = (bf16[2,96,576]{2,1,0:T(8,128)(2,1)S(1)}, bf16[2,96,576]{2,1,0:T(8,128)(2,1)S(1)}, u32[]{:S(2)}, u32[]{:S(2)}) collective-permute-start(bf16[2,96,576]{2,1,0:T(8,128)(2,1)S(1)} %fusion.5), channel_id=1, source_target_pairs={{0,8},{4,12},{8,0},{12,4},{16,24},{20,28},{24,16},{28,20},{1,9},{5... | collective-permute-start | bytes 663560 | tf_op jit(solution)/shard_map/ppermute | solution.py:467
  244.2 9.1 %collective-permute-start.23 = (bf16[1,96,576]{2,1,0:T(8,128)(2,1)S(1)}, bf16[1,96,576]{2,1,0:T(8,128)(2,1)S(1)}, u32[]{:S(2)}, u32[]{:S(2)}) collective-permute-start(bf16[1,96,576]{2,1,0:T(8,128)(2,1)S(1)} %dynamic-slice_convert_fusion.3), channel_id=1, source_target_pairs={{0,16},{4,20},{8,24},{12,28},{16,0},{20,4},{24,8},{28,12},{1,17},{... | collective-permute-start | bytes 331784 | tf_op jit(solution)/shard_map/ppermute | solution.py:467
  248.0 7.5 %collective-permute-start.17 = (bf16[4,4608]{1,0:T(4,128)(2,1)S(1)}, bf16[4,4608]{1,0:T(4,128)(2,1)S(1)}, u32[]{:S(2)}, u32[]{:S(2)}) collective-permute-start(bf16[4,4608]{1,0:T(4,128)(2,1)S(1)} %pad_maximum_fusion.3), channel_id=1, source_target_pairs={{0,16},{4,20},{8,24},{12,28},{16,0},{20,4},{24,8},{28,12},{1,17},{... | collective-permute-start | bytes 110600 | tf_op jit(solution)/shard_map/ppermute | solution.py:467
  254.7 10.6 %collective-permute-start.20 = (f32[9,768]{1,0:T(8,128)S(1)}, f32[9,768]{1,0:T(8,128)S(1)}, u32[]{:S(2)}, u32[]{:S(2)}) collective-permute-start(f32[9,768]{1,0:T(8,128)S(1)} %add.218), channel_id=1, source_target_pairs={{0,16},{4,20},{8,24},{12,28},{16,0},{20,4},{24,8},{28,12},{1,17},{... | collective-permute-start | bytes 82952 | tf_op jit(solution)/shard_map/ppermute | solution.py:467
  (47 other events, 275.3 us)

commit v3 on v1

v3 whole, which is shorter than its diff:
```python
import math

import jax
import jax.numpy as jnp
from jax import lax
from jax.experimental import pallas as pl
from jax.experimental.pallas import tpu as pltpu
from jax.sharding import PartitionSpec as P

f32 = jnp.float32
bf16 = jnp.bfloat16

WIDTH = 768
TILES = WIDTH // 128
SIDE = 32
ITEM = SIDE * SIDE
HALF = ITEM // 2
SHARE = ITEM // 4
HALO = SHARE + 2 * SIDE
HEADS_HERE = 3
HEAD_WIDTH = 192
PITCH = 40
GRID_ROWS = 34 * PITCH + 8
SHARE_GRID_ROWS = 10 * PITCH + 16

norm_eps = 1e-06
score_scale = 0.125
gelu_slope = math.sqrt(2.0 / math.pi)
gelu_cubic = 0.044715
COST = 1000
BLOCK = 96
TAIL = 16


def dot_nn(left, right):
    return lax.dot_general(left, right, (((1,), (0,)), ((), ())), preferred_element_type=f32)


def dot_nt(left, right):
    return lax.dot_general(left, right, (((1,), (1,)), ((), ())), preferred_element_type=f32)


def dot_tn(left, right):
    return lax.dot_general(left, right, (((0,), (0,)), ((), ())), preferred_element_type=f32)


def at(start, size):
    return pl.ds(pl.multiple_of(start, size), size)


def at16(start, size):
    return pl.ds(pl.multiple_of(start, 16), size)


def tile_cols(tile):
    return pl.ds(pl.multiple_of(tile * 128, 128), 128)


def spot(row, col):
    return (row + 1) * PITCH + 8 + col


def every_other(start):
    return pl.ds(start, 16, stride=2)


def window(grid, tile, i):
    return [
        [grid[tile, every_other(spot(2 * i + row, col)), :] for col in range(-1, 3)]
        for row in range(-1, 3)
    ]


def here_core():
    place = lax.axis_index("tensor")
    return lax.rem(place, 2), lax.div(place, 2), place


def normed_of(values):
    center = values - jnp.mean(values, axis=-1, keepdims=True)
    scale = lax.rsqrt(jnp.mean(center * center, axis=-1, keepdims=True) + norm_eps)
    return center * scale, scale


def norm_back(normed, scale, grad):
    spread = jnp.mean(grad * normed, axis=-1, keepdims=True)
    return scale * (grad - jnp.mean(grad, axis=-1, keepdims=True) - normed * spread)


def row_of(flat, start=0):
    return flat[pl.ds(start, WIDTH)].astype(f32).reshape(1, WIDTH)


def column_sum(values):
    return jnp.sum(values, axis=0, keepdims=True)


def head_masks():
    lane = lax.broadcasted_iota(jnp.int32, (SHARE, HEAD_WIDTH), 1)
    return [(lane >= 64 * h) & (lane < 64 * h + 64) for h in range(HEADS_HERE)]


def split_halves(values, core, group, keep, send):
    for x in range(2):
        rows = at(x * SHARE + group * 64, 64)
        keep[rows, :] = values[at((2 * x + core) * 64, 64), :].astype(bf16)
        send[rows, :] = values[at((2 * x + 1 - core) * 64, 64), :].astype(bf16)


def join_halves(own, other, core, full):
    for half, h in ((own, core), (other, 1 - core)):
        for x in range(2):
            for g in range(4):
                rows = at(g * SHARE + (8 * x + 4 * h) * 16, 64)
                full[rows, :] = half[x * SHARE + g * 64 : x * SHARE + g * 64 + 64, :]


def take_half(natural, core, tile, half, cols):
    for x in range(2):
        for g in range(4):
            for ii in range(4):
                i = 8 * x + 4 * core + ii
                row = x * SHARE + g * 64 + ii * 16
                seen = natural[tile, every_other((2 * i + g // 2) * SIDE + g % 2), :]
                half[row : row + 16, cols] = seen.astype(half.dtype)


def modulation(act, weights, bias, pieces, first):
    return [
        dot_nt(act, weights[(p - first) * WIDTH : (p - first + 1) * WIDTH, :])[:1]
        + row_of(bias, p * WIDTH)
        for p in pieces
    ]


def kernel_a(
    tokens, act, b_mod, k_att, w_qkv, w_out, w_mod,
    mods_out, source, keep, send, mixed_out, q_out, k_out, v_out, att_out, lse_out,
    grid, natural, temp, kernel, weights, mixed, q_all, k_all, v_all, att_all, lse_all, sems, mod_sem,
):
    core, _, _ = here_core()
    fetch = pltpu.make_async_copy(w_mod.at[pl.ds(0, 2 * WIDTH), :], weights, mod_sem)
    fetch.start()
    grid[...] = jnp.zeros_like(grid)
    kernel[0:9, :] = k_att[...].astype(f32)
    fetch.wait()
    shift, scale = modulation(act[...], weights, b_mod, (0, 1), 0)
    mods_out[0:1, :] = shift
    mods_out[1:2, :] = scale
    scale = 1.0 + scale

    def norm(i, carry):
        values = tokens[at(i * 64, 64), :].astype(f32)
        shaped = normed_of(values)[0] * scale + shift
        for tile in range(TILES):
            cols = slice(tile * 128, tile * 128 + 128)
            natural[tile, at(i * 64, 64), :] = values[:, cols]
            for r in range(2):
                rows = pl.ds(pl.multiple_of((2 * i + r + 1) * PITCH + 8, 8), SIDE)
                grid[tile, rows, :] = shaped[SIDE * r : SIDE * r + SIDE, cols]
        return carry

    lax.fori_loop(0, 16, norm, 0)

    def conv(tile, carry):
        cols = tile_cols(tile)
        taps = [kernel[t : t + 1, cols] for t in range(9)]

        def row(i, inner):
            seen = window(grid, tile, i)
            for a in range(2):
                for b in range(2):
                    total = taps[0] * seen[a][b]
                    for t in range(1, 9):
                        total = total + taps[t] * seen[a + t // 3][b + t % 3]
                    mixed[at16((2 * a + b) * SHARE + i * 16, 16), cols] = total.astype(bf16)
            return inner

        lax.fori_loop(0, 16, row, 0)
        take_half(natural, core, tile, source, cols)
        return carry

    lax.fori_loop(0, TILES, conv, 0)
    masks = head_masks()
    lane = lax.broadcasted_iota(jnp.int32, (SHARE, 128), 1)
    pairs = (
        (mixed, mixed_out), (q_all, q_out), (k_all, k_out),
        (v_all, v_out), (att_all, att_out), (lse_all, lse_out),
    )

    def copies(g):
        rows = at(g * SHARE, SHARE)
        return [
            pltpu.make_async_copy(left.at[rows, :], right.at[rows, :], sems.at[n, g])
            for n, (left, right) in enumerate(pairs)
        ]

    def attend(g, carry):
        rows = at(g * SHARE, SHARE)
        values = mixed[rows, :]
        query, keys, vals = (dot_nt(values, w_qkv[kind]).astype(bf16) for kind in range(3))
        q_all[rows, :] = query
        k_all[rows, :] = keys
        v_all[rows, :] = vals
        attended = jnp.zeros((SHARE, HEAD_WIDTH), f32)
        lse = jnp.zeros((SHARE, 128), f32)
        for h in range(HEADS_HERE):
            scores = dot_nt(jnp.where(masks[h], query, jnp.zeros_like(query)), keys) * score_scale
            top = jnp.max(scores, axis=-1, keepdims=True)
            grown = jnp.exp(scores - top)
            total = jnp.sum(grown, axis=-1, keepdims=True)
            probs = (grown * (1.0 / total)).astype(bf16)
            attended = jnp.where(masks[h], dot_nn(probs, vals), attended)
            lse = jnp.where(lane == h, top + jnp.log(total), lse)
        lse_all[rows, :] = lse
        attended = attended.astype(bf16)
        att_all[rows, :] = attended
        for copy in copies(g):
            copy.start()
        temp[...] = dot_nn(attended, w_out[...])
        split_halves(temp, core, g, keep, send)
        return carry

    lax.fori_loop(0, 4, attend, 0)

    def finish(g, carry):
        for copy in copies(g):
            copy.wait()
        return carry

    lax.fori_loop(0, 4, finish, 0)


def kernel_p(
    count, cotangent, act, b_mod, w_mod,
    mods_out, grad_branch, half, other,
    natural, weights, sem,
):
    core, _, _ = here_core()
    fetch = pltpu.make_async_copy(w_mod.at[pl.ds(2 * WIDTH, 4 * WIDTH), :], weights, sem)
    fetch.start()
    live = jnp.where(count[0] > 0, 1.0, 0.0)

    def spread(i, carry):
        values = cotangent[at(i * 64, 64), :].astype(f32) * live
        for tile in range(TILES):
            natural[tile, at(i * 64, 64), :] = values[:, tile * 128 : tile * 128 + 128]
        return carry

    lax.fori_loop(0, 16, spread, 0)
    fetch.wait()
    for p, row in zip(range(2, 6), modulation(act[...], weights, b_mod, range(2, 6), 2)):
        mods_out[p : p + 1, :] = row

    def group(tile, carry):
        cols = tile_cols(tile)
        gate = mods_out[5:6, cols]

        def row(i, inner):
            for g in range(4):
                seen = natural[tile, every_other((2 * i + g // 2) * SIDE + g % 2), :]
                grad_branch[at16(g * SHARE + i * 16, 16), cols] = (seen * gate).astype(bf16)
            return inner

        lax.fori_loop(0, 16, row, 0)
        take_half(natural, core, tile, half, cols)
        take_half(natural, 1 - core, tile, other, cols)
        return carry

    lax.fori_loop(0, TILES, group, 0)


def kernel_b(chip, far, source, mods, b_out, branch_out, middle_out, shaped_out):
    gate = mods[2:3, :]
    shift = mods[3:4, :]
    scale = 1.0 + mods[4:5, :]
    bias = row_of(b_out)

    def step(r, carry):
        rows = at(r * 64, 64)
        branch = chip[rows, :].astype(f32) + far[rows, :].astype(f32) + bias
        middle = source[rows, :] + gate * branch
        branch_out[rows, :] = branch
        middle_out[rows, :] = middle
        shaped_out[rows, :] = (normed_of(middle)[0] * scale + shift).astype(bf16)
        return carry

    lax.fori_loop(0, HALF // 64, step, 0)


def kernel_c(
    own, other, grad_branch, w_up, w_down, b_up, k_ffn,
    shaped, activated, grad_hidden, sums, b_keep, b_send, g_keep, g_send,
    hidden, grad_conv, grad_act, temp, kernel,
):
    core, _, _ = here_core()
    hidden[...] = jnp.zeros_like(hidden)
    grad_conv[...] = jnp.zeros_like(grad_conv)
    kernel[0:9, :] = k_ffn[...].astype(f32)
    bias = row_of(b_up)
    join_halves(own, other, core, shaped)

    def up(g, carry):
        rows = at(g * SHARE, SHARE)
        a = lax.div(g, 2)
        b = lax.rem(g, 2)
        grad_act[rows, :] = dot_nn(grad_branch[rows, :], w_down[...])
        temp[...] = dot_nn(shaped[rows, :], w_up[...]) + bias

        def place(i, inner):
            for tile in range(TILES):
                values = temp[at(i * 16, 16), tile * 128 : tile * 128 + 128]
                hidden[tile, every_other(spot(2 * i + a, b)), :] = values
            return inner

        lax.fori_loop(0, 16, place, 0)
        return carry

    lax.fori_loop(0, 4, up, 0)

    def conv(tile, carry):
        cols = tile_cols(tile)
        taps = [kernel[t : t + 1, cols] for t in range(9)]

        def row(i, inner):
            seen = window(hidden, tile, i)
            for a in range(2):
                for b in range(2):
                    rows = at16((2 * a + b) * SHARE + i * 16, 16)
                    u = taps[0] * seen[a][b]
                    for t in range(1, 9):
                        u = u + taps[t] * seen[a + t // 3][b + t % 3]
                    square = u * u
                    bent = jnp.tanh(gelu_slope * u * (1.0 + gelu_cubic * square))
                    part = 0.5 + 0.5 * bent
                    activated[rows, cols] = (u * part).astype(bf16)
                    bend = (1.0 - bent * bent) * (1.0 + (3.0 * gelu_cubic) * square)
                    slope = part + (0.5 * gelu_slope) * u * bend
                    back = grad_act[rows, cols] * slope
                    grad_conv[tile, every_other(spot(2 * i + a, b)), :] = back
            return inner

        lax.fori_loop(0, 16, row, 0)
        return carry

    lax.fori_loop(0, TILES, conv, 0)

    def back(tile, carry):
        cols = tile_cols(tile)
        taps = [kernel[t : t + 1, cols] for t in range(9)]

        def row(i, held):
            held = list(held)
            seen = window(grad_conv, tile, i)
            for a in range(2):
                for b in range(2):
                    here = hidden[tile, every_other(spot(2 * i + a, b)), :]
                    total = None
                    for t in range(9):
                        view = seen[a + 2 - t // 3][b + 2 - t % 3]
                        term = taps[t] * view
                        total = term if total is None else total + term
                        product = here * view
                        held[t] = held[t] + (product[:8] + product[8:])
                    low = total.astype(bf16)
                    grad_hidden[at16((2 * a + b) * SHARE + i * 16, 16), cols] = low
                    low = low.astype(f32)
                    held[9] = held[9] + (low[:8] + low[8:])
            return tuple(held)

        zeros = tuple(jnp.zeros((8, 128), f32) for _ in range(10))
        held = lax.fori_loop(0, 16, row, zeros)
        for t in range(10):
            sums[t : t + 1, cols] = column_sum(held[t])
        return carry

    lax.fori_loop(0, TILES, back, 0)

    def out(g, total):
        rows = at(g * SHARE, SHARE)
        temp[...] = dot_nt(grad_hidden[rows, :], w_up[...])
        split_halves(temp, core, g, g_keep, g_send)
        temp[...] = dot_nt(activated[rows, :], w_down[...])
        split_halves(temp, core, g, b_keep, b_send)
        return total + column_sum(grad_branch[rows, :].astype(f32))

    sums[10:11, :] = lax.fori_loop(0, 4, out, jnp.zeros((1, WIDTH), f32))
    sums[11:16, :] = jnp.zeros((5, WIDTH), f32)


def kernel_d(chip, far, branch, middle, half, mods, grad_middle, grad_attn, sums):
    gate = mods[2:3, :]
    scale = 1.0 + mods[4:5, :]

    def step(r, held):
        rows = at(r * 64, 64)
        grad = chip[rows, :].astype(f32) + far[rows, :].astype(f32)
        normed, size = normed_of(middle[rows, :])
        total = half[rows, :].astype(f32) + norm_back(normed, size, grad * scale)
        low = (total * gate).astype(bf16)
        grad_middle[rows, :] = total
        grad_attn[rows, :] = low
        terms = (total * branch[rows, :], grad, grad * normed, low.astype(f32))
        return tuple(h + column_sum(t) for h, t in zip(held, terms))

    zeros = tuple(jnp.zeros((1, WIDTH), f32) for _ in range(4))
    held = lax.fori_loop(0, HALF // 64, step, zeros)
    for t in range(4):
        sums[t : t + 1, :] = held[t]


def kernel_o(count, near, far, middle, mods, b_down, out, natural):
    _, side, _ = here_core()
    live = jnp.where(count[0] > 0, 1.0, 0.0)
    gate = mods[5:6, :]
    bias = row_of(b_down)
    for g in range(4):
        part = slice(g * 64, g * 64 + 64)
        rows = at(side * SHARE + g * 64, 64)
        branch = near[part, :].astype(f32) + far[part, :].astype(f32) + bias
        result = (middle[rows, :] + gate * branch) * live
        for ii in range(4):
            place = every_other((2 * ii + g // 2) * SIDE + g % 2)
            for tile in range(TILES):
                cols = slice(tile * 128, tile * 128 + 128)
                natural[tile, place, :] = result[ii * 16 : ii * 16 + 16, cols]
    for tile in range(TILES):
        out[:, tile * 128 : tile * 128 + 128] = natural[tile, :, :].astype(bf16)


def kernel_e(
    own, other, q_all, k_all, v_all, att_all, lse_all, w_qkv, w_out,
    grad_branch, right, mixed, keep, send,
    padded,
):
    core, _, _ = here_core()
    join_halves(own, other, core, grad_branch)
    masks = head_masks()
    for g in range(4):
        padded[g, 0:16, :] = jnp.zeros((16, WIDTH), bf16)
        padded[g, 272:288, :] = jnp.zeros((16, WIDTH), bf16)

    def attend(g, carry):
        rows = at(g * SHARE, SHARE)
        grad = dot_nt(grad_branch[rows, :], w_out[...]).astype(bf16)
        query = q_all[rows, :]
        keys = k_all[rows, :]
        vals = v_all[rows, :]
        zero = jnp.zeros_like(query)
        g_query = jnp.zeros((SHARE, HEAD_WIDTH), f32)
        g_keys = g_query
        g_vals = g_query
        for h in range(HEADS_HERE):
            scores = dot_nt(jnp.where(masks[h], query, zero), keys) * score_scale
            probs = jnp.exp(scores - lse_all[rows, h : h + 1])
            g_probs = dot_nt(jnp.where(masks[h], grad, zero), vals)
            spread = jnp.sum(probs * g_probs, axis=-1, keepdims=True)
            g_scores = (probs * (g_probs - spread)).astype(bf16)
            g_query = jnp.where(masks[h], dot_nn(g_scores, keys), g_query)
            g_keys = jnp.where(masks[h], dot_tn(g_scores, query), g_keys)
            g_vals = jnp.where(masks[h], dot_tn(probs.astype(bf16), grad), g_vals)
        g_query = (g_query * score_scale).astype(bf16)
        g_keys = (g_keys * score_scale).astype(bf16)
        g_vals = g_vals.astype(bf16)
        right[rows, :] = jnp.concatenate([g_query, g_keys, g_vals, att_all[rows, :]], axis=1)
        total = dot_nn(g_query, w_qkv[0]) + dot_nn(g_keys, w_qkv[1]) + dot_nn(g_vals, w_qkv[2])
        low = total.astype(bf16)
        padded[g, 16:272, :] = low
        mixed[rows, :] = low
        return carry

    lax.fori_loop(0, 4, attend, 0)
    for out, h in ((keep, core), (send, 1 - core)):
        for x in range(2):
            share = 2 * x + h
            first = x * HALO
            for g in range(4):
                rows = at16((1 + 4 * share) * 16, 64)
                out[first + g * 64 : first + g * 64 + 64, :] = padded[g, rows, :]
            for b in range(2):
                row = first + SHARE + b * 16
                out[row : row + 16, :] = padded[2 + b, at16(4 * share * 16, 16), :]
                row = row + SIDE
                out[row : row + 16, :] = padded[b, at16((4 * share + 5) * 16, 16), :]


def kernel_n(tokens, natural):
    def step(i, carry):
        normed = normed_of(tokens[at(i * 64, 64), :].astype(f32))[0]
        for tile in range(TILES):
            natural[tile, at(i * 64, 64), :] = normed[:, tile * 128 : tile * 128 + 128]
        return carry

    lax.fori_loop(0, 16, step, 0)


def kernel_q(keep, send, own, other, b_down, sums):
    _, _, place = here_core()
    once = jnp.where(place == 0, 1.0, 0.0)
    bias = row_of(b_down) * once

    def step(r, total):
        rows = at(r * 64, 64)
        near = own[rows, :].astype(f32) * (keep[rows, :].astype(f32) + bias)
        away = other[rows, :].astype(f32) * (send[rows, :].astype(f32) + bias)
        return total + column_sum(near + away)

    sums[0:1, :] = lax.fori_loop(0, HALF // 64, step, jnp.zeros((1, WIDTH), f32))


def kernel_s(natural, mixed, mods, k_att, sums_d, sums_q, out, grid, kernel):
    _, side, _ = here_core()
    grid[...] = jnp.zeros_like(grid)
    kernel[0:9, :] = k_att[...].astype(f32)

    def norm(i, carry):
        for g in range(4):
            values = mixed[at16(g * SHARE + i * 16, 16), :].astype(f32)
            place = every_other(spot(2 * i + g // 2, g % 2))
            for tile in range(TILES):
                grid[tile, place, :] = values[:, tile * 128 : tile * 128 + 128]
        return carry

    lax.fori_loop(0, 16, norm, 0)

    def gather(tile, carry):
        cols = tile_cols(tile)
        taps = [kernel[t : t + 1, cols] for t in range(9)]

        def row(i, held):
            held = list(held)
            seen = window(grid, tile, i)
            for a in range(2):
                for b in range(2):
                    here = natural[tile, every_other((2 * i + a) * SIDE + b), :]
                    for t in range(9):
                        product = here * seen[a + 2 - t // 3][b + 2 - t % 3]
                        held[t] = held[t] + (product[:8] + product[8:])
                    center = seen[a + 1][b + 1]
                    held[9] = held[9] + (center[:8] + center[8:])
            return tuple(held)

        zeros = tuple(jnp.zeros((8, 128), f32) for _ in range(10))
        held = [column_sum(h) for h in lax.fori_loop(0, 16, row, zeros)]
        edge_row = [
            column_sum(grid[tile, pl.ds(spot(r, 0), SIDE), :]) if r is not None else 0.0
            for r in (0, None, SIDE - 1)
        ]
        edge_col = [
            column_sum(grid[tile, pl.ds(spot(0, c), SIDE, stride=PITCH), :])
            if c is not None
            else 0.0
            for c in (0, None, SIDE - 1)
        ]
        shift = mods[0:1, cols]
        scale = 1.0 + mods[1:2, cols]
        shift_sum = jnp.zeros((1, 128), f32)
        scale_sum = jnp.zeros((1, 128), f32)
        for t in range(9):
            a, b = t // 3, t % 3
            plain = held[9] - edge_row[a] - edge_col[b]
            if a != 1 and b != 1:
                corner = spot((SIDE - 1) * (a // 2), (SIDE - 1) * (b // 2))
                plain = plain + grid[tile, pl.ds(corner, 1), :]
            out[6 + t : 7 + t, cols] = scale * held[t] + shift * plain
            shift_sum = shift_sum + taps[t] * plain
            scale_sum = scale_sum + taps[t] * held[t]
        out[0:1, cols] = shift_sum
        out[1:2, cols] = scale_sum
        return carry

    lax.fori_loop(0, TILES, gather, 0)
    once = jnp.where(side == 0, 1.0, 0.0)
    out[2:5, :] = sums_d[0:3, :] * once
    out[5:6, :] = sums_q[0:1, :]
    out[15:16, :] = sums_d[3:4, :] * once


def kernel_f(tokens, near, far, grad_middle, mods, k_att, out, grid, grad_shaped, middle, kernel):
    _, side, place = here_core()
    grid[...] = jnp.zeros_like(grid)
    kernel[0:9, :] = k_att[...].astype(f32)
    scale = 1.0 + mods[1:2, :]

    def fetch(start, rows):
        part = slice(start, start + rows)
        total = near[part, :].astype(f32) + far[part, :].astype(f32)
        return total.astype(bf16).astype(f32)

    for g in range(4):
        a, b = g // 2, g % 2
        values = fetch(g * 64, 64)
        grads = grad_middle[at(side * SHARE + g * 64, 64), :]
        for ii in range(4):
            rows = slice(ii * 16, ii * 16 + 16)
            for tile in range(TILES):
                cols = slice(tile * 128, tile * 128 + 128)
                grid[tile, every_other(spot(2 * ii + a, b)), :] = values[rows, cols]
                middle[tile, every_other((2 * ii + a) * SIDE + b), :] = grads[rows, cols]
    for b in range(2):
        above = fetch(SHARE + b * 16, 16)
        below = fetch(SHARE + SIDE + b * 16, 16)
        for tile in range(TILES):
            cols = slice(tile * 128, tile * 128 + 128)
            grid[tile, every_other(spot(-1, b)), :] = above[:, cols]
            grid[tile, every_other(spot(8, b)), :] = below[:, cols]

    def conv(tile, carry):
        cols = tile_cols(tile)
        taps = [kernel[t : t + 1, cols] for t in range(9)]

        def row(i, inner):
            seen = window(grid, tile, i)
            for a in range(2):
                for b in range(2):
                    total = taps[0] * seen[a + 2][b + 2]
                    for t in range(1, 9):
                        total = total + taps[t] * seen[a + 2 - t // 3][b + 2 - t % 3]
                    grad_shaped[tile, every_other((2 * i + a) * SIDE + b), :] = total
            return inner

        lax.fori_loop(0, 4, row, 0)
        return carry

    lax.fori_loop(0, TILES, conv, 0)

    def finish(r, carry):
        rows = at(r * SIDE, SIDE)
        values = tokens[at(place * SHARE + r * SIDE, SIDE), :].astype(f32)
        normed, size = normed_of(values)
        grad = jnp.concatenate([grad_shaped[tile, rows, :] for tile in range(TILES)], axis=1)
        base = jnp.concatenate([middle[tile, rows, :] for tile in range(TILES)], axis=1)
        out[rows, :] = base + norm_back(normed, size, grad * scale)
        return carry

    lax.fori_loop(0, SHARE // SIDE, finish, 0)


def bit_here(bit):
    return lax.rem(lax.div(lax.axis_index("dp"), bit), 2)


def split_blocks(blocks, stride, bit, values, keep, send):
    mine = bit_here(bit)
    for j in range(blocks // 2):
        base = (j // stride) * 2 * stride + j % stride
        rows = slice(j * BLOCK, (j + 1) * BLOCK)
        keep[rows, :] = values(at16((base + mine * stride) * BLOCK, BLOCK))
        send[rows, :] = values(at16((base + (1 - mine) * stride) * BLOCK, BLOCK)).astype(bf16)


def summed(held, came):
    return lambda rows: held[rows, :] + came[rows, :].astype(f32)


def kernel_w(grad, activated, shaped, hidden, sums, d_keep, d_send, u_keep, u_send, total):
    for left, right, stride, keep, send in (
        (grad, activated, 1, d_keep, d_send),
        (shaped, hidden, 2, u_keep, u_send),
    ):

        def step(i, carry):
            total[at(i * 256, 256), :] = dot_tn(left[:, at(i * 256, 256)], right[...])
            return carry

        lax.fori_loop(0, 3, step, 0)
        split_blocks(8, stride, stride, lambda rows: total[rows, :], keep, send)
    d_keep[4 * BLOCK :, :] = sums[...].astype(bf16).astype(f32)
    d_send[4 * BLOCK :, :] = sums[...].astype(bf16)


def kernel_w_one(d_held, d_came, u_held, u_came, d_keep, d_send, u_keep, u_send):
    split_blocks(4, 1, 2, summed(d_held, d_came), d_keep, d_send)
    tail = summed(d_held, d_came)(slice(4 * BLOCK, 4 * BLOCK + TAIL)).astype(bf16)
    d_keep[2 * BLOCK :, :] = tail.astype(f32)
    d_send[2 * BLOCK :, :] = tail
    split_blocks(4, 2, 4, summed(u_held, u_came), u_keep, u_send)


def kernel_w_two(d_held, d_came, u_held, u_came, d_keep, d_send, u_keep, u_send):
    split_blocks(2, 1, 4, summed(d_held, d_came), d_keep, d_send)
    tail = summed(d_held, d_came)(slice(2 * BLOCK, 2 * BLOCK + TAIL)).astype(bf16)
    d_keep[BLOCK:, :] = tail.astype(f32)
    d_send[BLOCK:, :] = tail
    split_blocks(2, 1, 1, summed(u_held, u_came), u_keep, u_send)


def kernel_w_end(d_held, d_came, u_held, u_came, down, up, k_out, b_up, b_down):
    total = summed(d_held, d_came)
    down[...] = total(slice(0, BLOCK))
    up[...] = summed(u_held, u_came)(slice(0, BLOCK))
    tail = total(slice(BLOCK, BLOCK + TAIL))
    k_out[...] = tail[0:9, :]
    b_up[...] = tail[9:10, :].reshape(WIDTH)
    b_down[...] = tail[10:11, :].reshape(WIDTH)


def kernel_v(mixed, grad_branch, right, a_keep, a_send, b_keep, b_send, total):
    lane = lax.broadcasted_iota(jnp.int32, (256, 256), 1)

    def step(i, carry):
        cols = at(i * 256, 256)
        total[cols, 0:512] = dot_tn(mixed[:, cols], right[:, 0:512])
        last = right[:, 512:768]
        total[cols, 512:768] = jnp.where(
            lane < 64, dot_tn(mixed[:, cols], last), dot_tn(grad_branch[:, cols], last)
        )
        return carry

    lax.fori_loop(0, 3, step, 0)
    split_blocks(8, 1, 1, lambda rows: total[rows, 0:384], a_keep, a_send)
    split_blocks(8, 2, 2, lambda rows: total[rows, 384:768], b_keep, b_send)


def kernel_v_one(a_held, a_came, b_held, b_came, a_keep, a_send, b_keep, b_send):
    split_blocks(4, 1, 2, summed(a_held, a_came), a_keep, a_send)
    split_blocks(4, 2, 4, summed(b_held, b_came), b_keep, b_send)


def kernel_v_two(a_held, a_came, b_held, b_came, a_keep, a_send, b_keep, b_send):
    split_blocks(2, 1, 4, summed(a_held, a_came), a_keep, a_send)
    split_blocks(2, 1, 1, summed(b_held, b_came), b_keep, b_send)


def kernel_v_end(a_held, a_came, b_held, b_came, qkv, out):
    first = summed(a_held, a_came)(slice(0, BLOCK))
    last = summed(b_held, b_came)(slice(0, BLOCK))
    qkv[0] = first[:, :HEAD_WIDTH]
    qkv[1] = first[:, HEAD_WIDTH:]
    qkv[2] = last[:, :HEAD_WIDTH]
    out[...] = last[:, HEAD_WIDTH:]


def kernel_join(near, came, chip):
    chip[...] = (near[...].astype(f32) + came[...].astype(f32)).astype(bf16)


def kernel_join_split(near, came, own, send):
    _, side, _ = here_core()
    rows = own.shape[0]
    for out, x in ((own, side), (send, 1 - side)):
        part = at16(x * rows, rows)
        out[...] = (near[part, :].astype(f32) + came[part, :].astype(f32)).astype(bf16)


def kernel_slot(late, came, cond, out):
    total = late[...] + came[...]
    out[0, 0:6, :] = total[0:6, :].astype(bf16).astype(f32)
    out[0, 6:7, :] = cond[...]
    out[0, 7:8, :] = cond[...]
    out[1] = total[6:14, :]
    out[2, 0:2, :] = total[14:16, :]
    out[2, 2:8, :] = jnp.zeros((6, WIDTH), f32)


def kernel_gather(slots, held, came, out):
    out[0:slots] = held[0:slots]
    out[slots : 2 * slots] = came[0:slots]
    out[2 * slots : 2 * slots + 2] = held[slots : slots + 2] + came[slots : slots + 2]


def kernel_g(
    size, share, ids, near, came, w_mod,
    w_out, b_out, class_out, k_out, bias_out,
    held, lanes, grads, outer,
):
    here = lax.axis_index("dp")
    kernel_gather(size // 2, near, came, held)
    class_out[...] = jnp.zeros_like(class_out)
    conds = held[0:size, 6, :]
    sig = 1.0 / (1.0 + jnp.exp(-conds))
    act = (conds * sig).astype(bf16)
    total = jnp.zeros((size, WIDTH), f32)
    for p in range(6):
        piece = held[0:size, p, :].astype(bf16)
        lanes[:, p * WIDTH : (p + 1) * WIDTH] = piece
        total = total + dot_nn(piece, w_mod[p * WIDTH : (p + 1) * WIDTH, :])
    grads[...] = total * (sig * (1.0 + conds * (1.0 - sig)))
    reach = outer.shape[0]
    first = jnp.minimum(lax.div(here * share, 128) * 128, 6 * WIDTH - reach)
    outer[...] = dot_tn(lanes[:, pl.ds(pl.multiple_of(first, 128), reach)], act)
    w_out[...] = outer[pl.ds(pl.multiple_of(here * share - first, 8), share), :]

    def item(i, bias):
        slot = lax.bitwise_xor(here, i)
        row = pl.ds(ids[slot], 1)
        class_out[row, :] = class_out[row, :] + grads[pl.ds(slot, 1), :]
        return bias + held[slot]

    bias = lax.fori_loop(0, size, item, jnp.zeros((8, WIDTH), f32))
    for p in range(6):
        b_out[pl.ds(p * WIDTH, WIDTH)] = bias[p : p + 1, :].reshape(WIDTH)
    k_out[0:8, :] = held[size]
    k_out[8:9, :] = held[size + 1, 0:1, :]
    bias_out[...] = held[size + 1, 1:2, :].reshape(WIDTH)


def vmem(shape, dtype):
    return pltpu.VMEM(shape, dtype)


def hbm(shape, dtype):
    return pltpu.HBM(shape, dtype)


def plain(shape, dtype):
    return jax.ShapeDtypeStruct(shape, dtype)


def call(kernel, scalars, arrays, far_arrays, outs, scratch, mebibytes, flops, moved):
    spots = (
        [pl.BlockSpec(memory_space=pltpu.SMEM)] * len(scalars)
        + [pl.BlockSpec(memory_space=pltpu.VMEM)] * len(arrays)
        + [pl.BlockSpec(memory_space=pltpu.HBM)] * len(far_arrays)
    )
    spaces = [pltpu.VMEM if getattr(o, "memory_space", None) != pltpu.HBM else pltpu.HBM for o in outs]
    return pl.pallas_call(
        kernel,
        out_shape=tuple(outs),
        in_specs=spots,
        out_specs=tuple(pl.BlockSpec(memory_space=m) for m in spaces),
        scratch_shapes=scratch,
        compiler_params=pltpu.CompilerParams(vmem_limit_bytes=mebibytes << 20),
        cost_estimate=pl.CostEstimate(flops=flops // COST, bytes_accessed=moved // COST, transcendentals=0),
    )(
        *scalars,
        *(pltpu.with_memory_space_constraint(a, pltpu.VMEM) for a in arrays),
        *(pltpu.with_memory_space_constraint(a, pltpu.HBM) for a in far_arrays),
    )


def swap(values, axis, bit):
    size = lax.axis_size(axis)
    return lax.ppermute(values, axis, [(i, i ^ bit) for i in range(size)])


def bits_of(axis):
    return [1 << b for b in range(lax.axis_size(axis).bit_length() - 1)]


def butterfly(values, axis):
    for bit in bits_of(axis):
        values = values + swap(values, axis, bit)
    return values


def gather_xor(values):
    for bit in bits_of("dp"):
        values = jnp.concatenate([values, swap(values, "dp", bit)], axis=0)
    return values


def scatter_plain(total):
    size = lax.axis_size("dp")
    here = lax.axis_index("dp")
    held = total.reshape(total.shape[0], size, -1, total.shape[-1])
    for bit in bits_of("dp"):
        mine = (here // bit) % 2
        parts, blocks, rows, width = held.shape
        halves = held.reshape(parts, blocks // 2, 2, rows, width)
        keep = lax.dynamic_index_in_dim(halves, mine, 2, keepdims=False)
        send = lax.dynamic_index_in_dim(halves, 1 - mine, 2, keepdims=False).astype(bf16)
        held = keep + swap(send, "dp", bit).astype(f32)
    return held[:, 0]


def join(near, came):
    (chip,) = call(kernel_join, [], [near, came], [], [vmem(near.shape, bf16)], [], 4, 10**6, 3 * 10**6)
    return chip


def join_split(near, came):
    part = vmem((near.shape[0] // 2, WIDTH), bf16)
    return call(kernel_join_split, [], [near, came], [], [part, part], [], 4, 10**6, 3 * 10**6)


def weight_step(kernel, blocks, tail, width, *arrays):
    first = (blocks * BLOCK + tail, width)
    last = (blocks * BLOCK, width)
    outs = [vmem(first, f32), vmem(first, bf16), vmem(last, f32), vmem(last, bf16)]
    return call(kernel, [], list(arrays), [], outs, [], 4, 10**6, 4 * 10**6)


def time_features(timestep):
    half_width = WIDTH // 2
    freqs = jnp.exp(-math.log(10000.0) * jnp.arange(half_width, dtype=f32) / half_width)
    angles = timestep.astype(f32)[:, None] * freqs[None, :]
    return jnp.concatenate([jnp.cos(angles), jnp.sin(angles)], axis=1)


def together(*values):
    return lax.optimization_barrier(values)


def shards(
    tokens,
    cotangent,
    item_count,
    timestep,
    class_id,
    class_table,
    w_mod,
    b_mod,
    k_att,
    w_qkv,
    w_out,
    b_out,
    w_up,
    b_up,
    k_ffn,
    w_down,
    b_down,
):
    items = lax.axis_size("dp")
    bits = bits_of("dp")
    eight = items * BLOCK == WIDTH
    full = (ITEM, WIDTH)
    half = (HALF, WIDTH)
    head = (ITEM, HEAD_WIDTH)
    grid = pltpu.VMEM((TILES, GRID_ROWS, 128), f32)
    natural = pltpu.VMEM((TILES, ITEM, 128), f32)
    share_tiles = pltpu.VMEM((TILES, SHARE, 128), f32)
    temp = pltpu.VMEM((SHARE, WIDTH), f32)
    taps = pltpu.VMEM((16, WIDTH), f32)
    sem = pltpu.SemaphoreType.DMA

    row = lax.dynamic_slice(class_table, (class_id[0], 0), (1, WIDTH), allow_negative_indices=False)
    cond = time_features(timestep) + row.astype(f32)
    act = jnp.broadcast_to(jax.nn.silu(cond).astype(bf16), (16, WIDTH))
    w_three = jnp.transpose(w_qkv, (1, 2, 0))
    w_back = w_out.T

    mods_a, source, keep, send, mixed, query, keys, vals, attended, lse = call(
        kernel_a, [], [tokens, act, b_mod, k_att, w_three, w_back], [w_mod],
        [
            vmem((8, WIDTH), f32), vmem(half, f32), vmem(half, bf16), vmem(half, bf16),
            hbm(full, bf16), hbm(head, bf16), hbm(head, bf16), hbm(head, bf16), hbm(head, bf16),
            hbm((ITEM, 128), f32),
        ],
        [
            grid, natural, temp, taps, pltpu.VMEM((2 * WIDTH, WIDTH), bf16), pltpu.VMEM(full, bf16),
            pltpu.VMEM(head, bf16), pltpu.VMEM(head, bf16), pltpu.VMEM(head, bf16),
            pltpu.VMEM(head, bf16), pltpu.VMEM((ITEM, 128), f32), sem((6, 4)), sem,
        ],
        22, 3 * 10**9, 10**7,
    )
    chip = join(keep, swap(send, "tensor", 1))
    far = swap(chip, "tensor", 2)
    _, cotangent, class_id = together(chip, cotangent, class_id)
    mods_p, grad_ffn, cot_half, cot_other = call(
        kernel_p, [item_count], [cotangent, act, b_mod], [w_mod],
        [vmem((8, WIDTH), f32), vmem(full, bf16), vmem(half, bf16), vmem(half, bf16)],
        [natural, pltpu.VMEM((4 * WIDTH, WIDTH), bf16), sem], 12, 10**8, 8 * 10**6,
    )
    ids = gather_xor(class_id)
    far, mods_p, ids = together(far, mods_p, ids)
    branch, middle, shaped_own = call(
        kernel_b, [], [chip, far, source, mods_p, b_out], [],
        [vmem(half, f32), vmem(half, f32), vmem(half, bf16)], [], 6, 10**7, 7 * 10**6,
    )
    shaped_other = swap(shaped_own, "tensor", 1)

    shaped, activated, grad_hidden, sums_c, b_keep, b_send, g_keep, g_send = call(
        kernel_c, [], [shaped_own, shaped_other, grad_ffn, w_up, w_down, b_up, k_ffn], [],
        [vmem(full, bf16)] * 3 + [vmem((16, WIDTH), f32)] + [vmem(half, bf16)] * 4,
        [grid, grid, pltpu.VMEM(full, f32), temp, taps], 16, 5 * 10**9, 12 * 10**6,
    )
    chip = join(g_keep, swap(g_send, "tensor", 1))
    far = swap(chip, "tensor", 2)
    _, activated, b_send, sums_c = together(chip, activated, b_send, sums_c)
    b_own, b_part = join_split(b_keep, swap(b_send, "tensor", 1))
    b_far = swap(b_part, "tensor", 2)
    if eight:
        d_keep, d_send, u_keep, u_send = call(
            kernel_w, [], [grad_ffn, activated, shaped, grad_hidden, sums_c], [],
            [
                vmem((4 * BLOCK + TAIL, WIDTH), f32), vmem((4 * BLOCK + TAIL, WIDTH), bf16),
                vmem((4 * BLOCK, WIDTH), f32), vmem((4 * BLOCK, WIDTH), bf16),
            ],
            [pltpu.VMEM((WIDTH, WIDTH), f32)], 6, 24 * 10**8, 9 * 10**6,
        )
        d_came = swap(d_send, "dp", 1)
        u_came = swap(u_send, "dp", 2)
        tokens_n, b_keep, _, _ = together(tokens, b_keep, d_send, u_send)
    else:
        ffn_grads = scatter_plain(
            jnp.stack([dot_tn(grad_ffn, activated), dot_tn(shaped, grad_hidden)])
        )
        early = butterfly(sums_c, "dp")
        tokens_n = tokens
    (normed,) = call(
        kernel_n, [], [tokens_n], [], [vmem((TILES, ITEM, 128), f32)], [], 4, 10**7, 5 * 10**6
    )
    (sums_q,) = call(
        kernel_q, [], [b_keep, b_send, cot_half, cot_other, b_down], [], [vmem((8, WIDTH), f32)], [],
        4, 10**7, 4 * 10**6,
    )
    far, _, _ = together(far, normed, sums_q)
    if eight:
        far, d_came, u_came = together(far, d_came, u_came)
        d_keep, d_send, u_keep, u_send = weight_step(
            kernel_w_one, 2, TAIL, WIDTH, d_keep, d_came, u_keep, u_came
        )
        d_came = swap(d_send, "dp", 2)
        u_came = swap(u_send, "dp", 4)
    grad_middle, attn_own, sums_d = call(
        kernel_d, [], [chip, far, branch, middle, cot_half, mods_p], [],
        [vmem(half, f32), vmem(half, bf16), vmem((8, WIDTH), f32)], [], 6, 10**7, 8 * 10**6,
    )
    attn_other = swap(attn_own, "tensor", 1)

    grad_attn, right, mixed_grad, h_keep, h_send = call(
        kernel_e, [],
        [attn_own, attn_other, query, keys, vals, attended, lse, w_three, w_back], [],
        [vmem(full, bf16)] * 3 + [vmem((2 * HALO, WIDTH), bf16)] * 2,
        [pltpu.VMEM((4, 288, WIDTH), bf16)], 8, 3 * 10**9, 10**7,
    )
    h_came = swap(h_send, "tensor", 1)
    w_mod_late, _ = together(w_mod, mixed_grad)
    if eight:
        a_keep, a_send, e_keep, e_send = call(
            kernel_v, [], [mixed, grad_attn, right], [],
            [vmem((4 * BLOCK, 384), f32), vmem((4 * BLOCK, 384), bf16)] * 2,
            [pltpu.VMEM((WIDTH, WIDTH), f32)], 6, 16 * 10**8, 7 * 10**6,
        )
        h_came, d_came, u_came, mixed_grad, _, _ = together(
            h_came, d_came, u_came, mixed_grad, a_send, e_send
        )
        a_came = swap(a_send, "dp", 1)
        e_came = swap(e_send, "dp", 2)
        d_keep, d_send, u_keep, u_send = weight_step(
            kernel_w_two, 1, TAIL, WIDTH, d_keep, d_came, u_keep, u_came
        )
        d_came = swap(d_send, "dp", 4)
        u_came = swap(u_send, "dp", 1)
    else:
        last = dot_tn(grad_attn, right[:, 3 * HEAD_WIDTH :])
        total = jnp.concatenate([dot_tn(mixed, right[:, : 3 * HEAD_WIDTH]), last], axis=1)
        att_grads = scatter_plain(total[None])[0]
    h_own, h_part = join_split(h_keep, h_came)
    h_far = swap(h_part, "tensor", 2)
    (late,) = call(
        kernel_s, [], [normed, mixed_grad, mods_a, k_att, sums_d, sums_q], [],
        [vmem((16, WIDTH), f32)], [grid, taps], 8, 10**8, 4 * 10**6,
    )
    late = late + swap(late, "tensor", 1)
    late_came = swap(late, "tensor", 2)
    b_far, _ = together(b_far, late)
    (block_out,) = call(
        kernel_o, [item_count], [b_own, b_far, middle, mods_p, b_down], [],
        [plain((SHARE, WIDTH), bf16)], [share_tiles], 4, 10**7, 4 * 10**6,
    )
    late_came, _ = together(late_came, block_out)
    (held,) = call(
        kernel_slot, [], [late, late_came, cond], [], [vmem((3, 8, WIDTH), f32)], [], 2, 10**5, 10**5
    )
    came = swap(held, "dp", bits[0])
    if eight:
        a_came, e_came, _ = together(a_came, e_came, held)
        a_keep, a_send, e_keep, e_send = weight_step(
            kernel_v_one, 2, 0, 384, a_keep, a_came, e_keep, e_came
        )
        a_came = swap(a_send, "dp", 2)
        e_came = swap(e_send, "dp", 4)
        came, _ = together(came, a_send)
    for step, bit in enumerate(bits[1:], 1):
        slots = 1 << (step - 1)

        def kernel(*refs, slots=slots):
            kernel_gather(slots, *refs)

        (held,) = call(
            kernel, [], [held, came], [], [vmem((2 * slots + 2, 8, WIDTH), f32)], [], 4, 10**5, 10**5
        )
        came = swap(held, "dp", bit)
        if step == 1:
            h_far, _ = together(h_far, held)
            (grad_tokens,) = call(
                kernel_f, [], [tokens, h_own, h_far, grad_middle, mods_a, k_att], [],
                [plain((SHARE, WIDTH), f32)],
                [pltpu.VMEM((TILES, SHARE_GRID_ROWS, 128), f32), share_tiles, share_tiles, taps],
                6, 10**7, 6 * 10**6,
            )
            came, _ = together(came, grad_tokens)
    if eight:
        a_came, e_came, _ = together(a_came, e_came, held)
        a_keep, a_send, e_keep, e_send = weight_step(
            kernel_v_two, 1, 0, 384, a_keep, a_came, e_keep, e_came
        )
        a_came = swap(a_send, "dp", 4)
        e_came = swap(e_send, "dp", 1)
        came, _ = together(came, a_send)

    share = w_mod.shape[0] // items

    def kernel(*refs):
        kernel_g(items, share, *refs)

    grad_w_mod, grad_b_mod, grad_class, grad_k_att, grad_b_out = call(
        kernel, [ids], [held, came, w_mod_late], [],
        [
            plain((share, WIDTH), f32), plain(w_mod.shape[:1], f32), plain(class_table.shape, f32),
            plain((9, WIDTH), f32), plain((WIDTH,), f32),
        ],
        [
            pltpu.VMEM((items + 2, 8, WIDTH), f32), pltpu.VMEM((items, 6 * WIDTH), bf16),
            pltpu.VMEM((items, WIDTH), f32), pltpu.VMEM(((share + 254) // 128 * 128, WIDTH), f32),
        ],
        12, 10**8, 14 * 10**6,
    )

    if eight:
        rows = plain((BLOCK, WIDTH), f32)
        flat = plain((WIDTH,), f32)
        grad_down, grad_up, grad_k_ffn, grad_b_up, grad_b_down = call(
            kernel_w_end, [], [d_keep, d_came, u_keep, u_came], [],
            [rows, rows, plain((9, WIDTH), f32), flat, flat], [], 4, 10**6, 2 * 10**6,
        )
        a_came, e_came, _, _ = together(a_came, e_came, grad_b_mod, grad_b_up)
        grad_qkv, grad_out = call(
            kernel_v_end, [], [a_keep, a_came, e_keep, e_came], [],
            [plain((3, BLOCK, HEAD_WIDTH), f32), plain((BLOCK, HEAD_WIDTH), f32)], [], 4, 10**6, 10**6,
        )
        grad_qkv = jnp.transpose(grad_qkv, (1, 0, 2))
    else:
        grad_down, grad_up = ffn_grads[0], ffn_grads[1]
        grad_k_ffn, grad_b_up, grad_b_down = early[:9], early[9], early[10]
        grad_qkv = att_grads[:, : 3 * HEAD_WIDTH].reshape(-1, 3, HEAD_WIDTH)
        grad_out = att_grads[:, 3 * HEAD_WIDTH :]
    return (
        block_out,
        grad_tokens,
        grad_class,
        grad_w_mod,
        grad_b_mod,
        grad_k_att,
        grad_qkv,
        grad_out,
        grad_b_out,
        grad_up,
        grad_b_up,
        grad_k_ffn,
        grad_down,
        grad_b_down,
    )


def solution(mesh):
    placed = (
        P("dp", None),
        P("dp", None),
        P("dp"),
        P("dp"),
        P("dp"),
        P(),
        P(),
        P(),
        P(),
        P(None, None, "tensor"),
        P(None, "tensor"),
        P(),
        P(None, "tensor"),
        P("tensor"),
        P(None, "tensor"),
        P(None, "tensor"),
        P(),
    )
    return jax.shard_map(
        shards,
        mesh=mesh,
        in_specs=placed,
        out_specs=(
            P(("dp", "tensor"), None),
            P(("dp", "tensor"), None),
            P(),
            P("dp", None),
            P(),
            P(),
            P("dp", None, "tensor"),
            P("dp", "tensor"),
            P(),
            P("dp", "tensor"),
            P("tensor"),
            P(None, "tensor"),
            P("dp", "tensor"),
            P(),
        ),
        check_vma=False,
    )
```

time: 353 us -> 174 us (0.49); the launches traced: 348 us -> 174 us
  local copies, waits for them, and re-layouts: 113 us -> 5.06 us
  other arithmetic: 94.7 us -> 2.76 us
  Pallas kernels: 0 us -> 78.4 us
  matrix products: 45.9 us -> 0 us
  starting transfers between devices: 39.6 us -> 35.7 us
    pallas_call x0 -> x27, Pallas kernels: none -> 78.4 us  [call(): pl.pallas_call(kernel, out_shape=tuple(outs), in_specs=spots, out_specs=t...]
    dot_general x27 -> x0, matrix products: 45.9 us -> none  [the longest x7 14.6 us: dot_nn(): lax.dot_general(left, right, (((1,), (0,)), ((), ())), preferred_element_...]
    reduce_sum x18 -> x0, other arithmetic: 26.9 us -> none  [the longest x2 9.72 us: depthwise_back(): kernel_rows.append(jnp.sum(field * seen, axis=(0, 1)))]
    convert_element_type x18 -> x1, other arithmetic: 26.1 us -> 0.75 us  [shards(): act = jnp.broadcast_to(jax.nn.silu(cond).astype(bf16), (16, WIDTH))]
    convert_element_type x23 -> x0, local copies, waits for them, and re-layouts: 22.5 us -> none  [the longest x1 4.5 us: stage_c(): activated = to_groups(activated.reshape(ITEM, -1).astype(bf16), SIDE)]
    reshape x14 -> x0, local copies, waits for them, and re-layouts: 18.6 us -> none  [the longest x2 6.16 us: to_groups(): shaped = values.reshape((rows // 2, 2, HALF, 2, width))]
    another operation x26 -> x0, local copies, waits for them, and re-layouts: 18.5 us -> none  [the longest x18 5.34 us: depthwise_back(): return (total, jnp.stack(kernel_rows))]
    transpose x14 -> x0, local copies, waits for them, and re-layouts: 17 us -> none  [the longest x4 8.44 us: from_groups(): return shaped.transpose((2, 0, 3, 1, 4)).reshape((rows * SIDE, width))]
  transfers between devices with their start and end apart: 36 -> 30, of which waited for: 15 -> 17; matrix products, arithmetic and copies ran while one was open for 37% -> 1% of each run, Pallas kernels for 0% -> 18%
where the time goes in v3:
time: 174 us
  Pallas kernels  78.4 us (45%)
  waiting for transfers between devices  48.8 us (28%)
  starting transfers between devices  35.7 us (21%)
  local copies, waits for them, and re-layouts  5.06 us (3%)
  between operations  2.94 us (2%)
  other arithmetic  2.76 us (2%)
    pallas_call x27, Pallas kernels, call(): pl.pallas_call(kernel, out_shape=tuple(outs), in_specs=spots, out_specs=t...  78.4 us
    ppermute x30, waiting for transfers between devices, swap(): return lax.ppermute(values, axis, [(i, i ^ bit) for i in range(size)])  48.8 us
    ppermute x30, starting transfers between devices, swap(): return lax.ppermute(values, axis, [(i, i ^ bit) for i in range(size)])  35.7 us
    unnamed x48, local copies, waits for them, and re-layouts  5.06 us
  transfers between devices with their start and end apart: 30, of which 17 were waited for; matrix products, arithmetic and copies ran while one was open for 1% of the time, Pallas kernels for 18%

profile of v3, /device:TPU:0, one launch (start us, length us, event | category | flops | bytes accessed | tf_op | source)
XLA Modules:
  0.0 173.6 jit_solution(8199244573614501051)
XLA Ops:
  7.8 15.6 %shard_map.272 = (f32[8,768]{1,0:T(8,128)S(1)}, f32[512,768]{1,0:T(8,128)S(1)}, bf16[512,768]{1,0:T(8,128)(2,1)S(1)}, bf16[512,768]{1,0:T(8,128)(2,1)S(1)}, bf16...) custom-call(bf16[1024,768]{1,0:T(8,128)(2,1)S(1)} %copy-done, ...), custom_call_target="tpu_custom_call" | custom-call | flops 3000000 | bytes 10000 | tf_op jit(solution)/shard_map/pallas_call | solution.py:817
  26.1 2.9 %collective-permute-start.1 = (bf16[512,768]{1,0:T(8,128)(2,1)S(1)}, bf16[512,768]{1,0:T(8,128)(2,1)S(1)}, u32[]{:S(2)}, u32[]{:S(2)}) collective-permute-start(bf16[512,768]{1,0:T(8,128)(2,1)S(1)} %shard_map.273.chip), channel_id=1, source_target_pairs={{0,2},{1,3},{2,0},{3,1},{4,6},{5,7},{6,4},{7,5},{8,10},{9,11},{10,... | collective-permute-start | bytes 2359304 | tf_op jit(solution)/shard_map/ppermute | solution.py:834
  31.2 5.2 %shard_map.274 = (f32[8,768]{1,0:T(8,128)S(1)}, bf16[1024,768]{1,0:T(8,128)(2,1)S(1)}, bf16[512,768]{1,0:T(8,128)(2,1)S(1)}, bf16[512,768]{1,0:T(8,128)(2,1)S(1)}) custom-call(s32[1]{0:T(128)S(6)} %copy.31.count, bf16[1024,768]{1,0:T(8,128)(2,1)S(1)} %copy-done.4, bf16[16,768]{1,0:T(8,128)(2,1)S(1)} %broadcast_in_dim.10.act, bf16[4608]{0:T(1024)(128)(2,1)S(1)} %copy-done.17, ...), custom_call_target="tpu_custom_call" | custom-call | flops 100000 | bytes 8000 | tf_op jit(solution)/shard_map/pallas_call | solution.py:817
  41.2 2.6 %collective-permute-start.4 = (s32[4]{0:T(128)S(1)}, s32[4]{0:T(128)S(1)}, u32[]{:S(2)}, u32[]{:S(2)}) collective-permute-start(s32[4]{0:T(128)S(1)} %pad_add_fusion.1), channel_id=1, source_target_pairs={{0,16},{4,20},{8,24},{12,28},{16,0},{20,4},{24,8},{28,12},{1,17},{... | collective-permute-start | bytes 56 | tf_op jit(solution)/shard_map/ppermute | solution.py:834
  48.7 2.3 %collective-permute-done.5.other = bf16[512,768]{1,0:T(8,128)(2,1)S(1)} collective-permute-done((bf16[512,768]{1,0:T(8,128)(2,1)S(1)}, bf16[512,768]{1,0:T(8,128)(2,1)S(1)}, u32[]{:S(2)}, u32[]{:S(2)}) %collective-permute-start.5) | collective-permute-done | bytes 786464 | tf_op jit(solution)/shard_map/ppermute | solution.py:834
  51.0 17.9 %shard_map.276 = (bf16[1024,768]{1,0:T(8,128)(2,1)S(1)}, bf16[1024,768]{1,0:T(8,128)(2,1)S(1)}, bf16[1024,768]{1,0:T(8,128)(2,1)S(1)}, f32[16,768]{1,0:T(8,128)S...) custom-call(bf16[512,768]{1,0:T(8,128)(2,1)S(1)} %get-tuple-element., ...), custom_call_target="tpu_custom_call" | custom-call | flops 5000000 | bytes 12000 | tf_op jit(solution)/shard_map/pallas_call | solution.py:817
  73.3 4.1 %shard_map.279 = (f32[400,768]{1,0:T(8,128)S(1)}, bf16[400,768]{1,0:T(8,128)(2,1)S(1)}, f32[384,768]{1,0:T(8,128)S(1)}, bf16[384,768]{1,0:T(8,128)(2,1)S(1)}) custom-call(bf16[1024,768]{1,0:T(8,128)(2,1)S(1)} %get-tuple-element.127.grad_branch.grad, bf16[1024,768]{1,0:T(8,128)(2,1)S(1)} %get-tuple-element.137.activated, ...), custom_call_target="tpu_custom_call" | custom-call | flops 2400000 | bytes 9000 | tf_op jit(solution)/shard_map/pallas_call | solution.py:817
  80.6 3.1 %shard_map.280.natural = f32[6,1024,128]{2,1,0:T(8,128)S(1)} custom-call(bf16[1024,768]{1,0:T(8,128)(2,1)S(1)} %copy-done.1), custom_call_target="tpu_custom_call" | custom-call | flops 10000 | bytes 5000 | tf_op jit(solution)/shard_map/pallas_call | solution.py:817
  84.4 6.8 %collective-permute-done.9.far = bf16[512,768]{1,0:T(8,128)(2,1)S(1)} collective-permute-done((bf16[512,768]{1,0:T(8,128)(2,1)S(1)}, bf16[512,768]{1,0:T(8,128)(2,1)S(1)}, u32[]{:S(2)}, u32[]{:S(2)}) %collective-permute-start.9) | collective-permute-done | bytes 786464 | tf_op jit(solution)/shard_map/ppermute | solution.py:834
  91.2 2.6 %collective-permute-done.11.u_came = bf16[384,768]{1,0:T(8,128)(2,1)S(1)} collective-permute-done((bf16[384,768]{1,0:T(8,128)(2,1)S(1)}, bf16[384,768]{1,0:T(8,128)(2,1)S(1)}, u32[]{:S(2)}, u32[]{:S(2)}) %collective-permute-start.11) | collective-permute-done | bytes 589856 | tf_op jit(solution)/shard_map/ppermute | solution.py:834
  93.9 2.8 %shard_map.282 = (f32[512,768]{1,0:T(8,128)S(1)}, bf16[512,768]{1,0:T(8,128)(2,1)S(1)}, f32[8,768]{1,0:T(8,128)S(1)}) custom-call(bf16[512,768]{1,0:T(8,128)(2,1)S(1)} %shard_map.277.chip, bf16[512,768]{1,0:T(8,128)(2,1)S(1)} %collective-permute-done.9.far, f32[512,768]{1,0:T(8,128)S(1)} %get-tuple-element.149.branch, ...), custom_call_target="tpu_custom_call" | custom-call | flops 10000 | bytes 8000 | tf_op jit(solution)/shard_map/pallas_call | solution.py:817
  96.8 2.3 %collective-permute-done.12.other = bf16[512,768]{1,0:T(8,128)(2,1)S(1)} collective-permute-done((bf16[512,768]{1,0:T(8,128)(2,1)S(1)}, bf16[512,768]{1,0:T(8,128)(2,1)S(1)}, u32[]{:S(2)}, u32[]{:S(2)}) %collective-permute-start.12) | collective-permute-done | bytes 786464 | tf_op jit(solution)/shard_map/ppermute | solution.py:834
  99.1 8.5 %shard_map.283 = (bf16[1024,768]{1,0:T(8,128)(2,1)S(1)}, bf16[1024,768]{1,0:T(8,128)(2,1)S(1)}, bf16[1024,768]{1,0:T(8,128)(2,1)S(1)}, bf16[640,768]{1,0:T(8,128)(2,1)S(1)}, bf16[640,768]{1,0:T(8,128)(2,1)S(1)}) custom-call(bf16[512,768]{1,0:T(8,128)(2,1)S(1)} %get-tuple-element.151.own, bf16[512,768]{1,0:T(8,128)(2,1)S(1)} %collective-permute-done.12.other, ...), custom_call_target="tpu_custom_call" | custom-call | flops 3000000 | bytes 10000 | tf_op jit(solution)/shard_map/pallas_call | solution.py:817
  110.1 2.6 %collective-permute-start.15 = (bf16[192,768]{1,0:T(8,128)(2,1)S(1)}, bf16[192,768]{1,0:T(8,128)(2,1)S(1)}, u32[]{:S(2)}, u32[]{:S(2)}) collective-permute-start(bf16[192,768]{1,0:T(8,128)(2,1)S(1)} %get-tuple-element.163), channel_id=1, source_target_pairs={{0,16},{4,20},{8,24},{12,28},{16,0},{20,4},{24,8},{28,12},{1,17},{... | collective-permute-start | bytes 884744 | tf_op jit(solution)/shard_map/ppermute | solution.py:834
  113.5 2.4 %shard_map.285 = (f32[384,384]{1,0:T(8,128)S(1)}, bf16[384,384]{1,0:T(8,128)(2,1)S(1)}, f32[384,384]{1,0:T(8,128)S(1)}, bf16[384,384]{1,0:T(8,128)(2,1)S(1)}) custom-call(bf16[1024,768]{1,0:T(8,128)(2,1)S(1)} %copy-done.5, bf16[1024,768]{1,0:T(8,128)(2,1)S(1)} %get-tuple-element.166.grad_branch, bf16[1024,768]{1,0:T(8,128)(2,1)S(1)} %get-tuple-element.167.right), custom_call_target="tpu_custom_call" | custom-call | flops 1600000 | bytes 7000 | tf_op jit(solution)/shard_map/pallas_call | solution.py:817
  115.9 7.7 %collective-permute-done.15.u_came = bf16[192,768]{1,0:T(8,128)(2,1)S(1)} collective-permute-done((bf16[192,768]{1,0:T(8,128)(2,1)S(1)}, bf16[192,768]{1,0:T(8,128)(2,1)S(1)}, u32[]{:S(2)}, u32[]{:S(2)}) %collective-permute-start.15) | collective-permute-done | bytes 294944 | tf_op jit(solution)/shard_map/ppermute | solution.py:834
  126.1 2.6 %collective-permute-start.21 = (bf16[384,384]{1,0:T(8,128)(2,1)S(1)}, bf16[384,384]{1,0:T(8,128)(2,1)S(1)}, u32[]{:S(2)}, u32[]{:S(2)}) collective-permute-start(bf16[384,384]{1,0:T(8,128)(2,1)S(1)} %get-tuple-element.169), channel_id=1, source_target_pairs={{0,8},{4,12},{8,0},{12,4},{16,24},{20,28},{24,16},{28,20},{1,9},{5... | collective-permute-start | bytes 884744 | tf_op jit(solution)/shard_map/ppermute | solution.py:834
  128.6 3.5 %shard_map.286 = f32[16,768]{1,0:T(8,128)S(1)} custom-call(f32[6,1024,128]{2,1,0:T(8,128)S(1)} %shard_map.280.natural, bf16[1024,768]{1,0:T(8,128)(2,1)S(1)} %get-tuple-element.170.mixed, f32[8,768]{1,0:T(8,128)S(1)} %get-tuple-element.171.mods, bf16[9,768]{1,0:T(8,128)(2,1)S(1)} %copy-done.16, f32[8,768]{1,0:T(8,128)S(1)} %get-tuple-element.172.sums_d, ...), custom_call_target="tpu_custom_call" | custom-call | flops 100000 | bytes 4000 | tf_op jit(solution)/shard_map/pallas_call | solution.py:817
  139.2 3.4 %collective-permute-done.19.refs_1_ = f32[3,8,768]{2,1,0:T(8,128)S(1)} collective-permute-done((f32[3,8,768]{2,1,0:T(8,128)S(1)}, f32[3,8,768]{2,1,0:T(8,128)S(1)}, u32[]{:S(2)}, u32[]{:S(2)}) %collective-permute-start.19) | collective-permute-done | bytes 73760 | tf_op jit(solution)/shard_map/ppermute | solution.py:834
  142.7 2.7 %collective-permute-start.22 = (f32[4,8,768]{2,1,0:T(8,128)S(1)}, f32[4,8,768]{2,1,0:T(8,128)S(1)}, u32[]{:S(2)}, u32[]{:S(2)}) collective-permute-start(f32[4,8,768]{2,1,0:T(8,128)S(1)} %shard_map.291.refs_0_), channel_id=1, source_target_pairs={{0,8},{4,12},{8,0},{12,4},{16,24},{20,28},{24,16},{28,20},{1,9},{5... | collective-permute-start | bytes 294920 | tf_op jit(solution)/shard_map/ppermute | solution.py:834
  149.3 4.0 %shard_map.292 = f32[256,768]{1,0:T(8,128)} custom-call(bf16[1024,768]{1,0:T(8,128)(2,1)S(1)} %copy-done.1, bf16[320,768]{1,0:T(8,128)(2,1)S(1)} %get-tuple-element.176.near, bf16[320,768]{1,0:T(8,128)(2,1)S(1)} %collective-permute-done.17.far, f32[512,768]{1,0:T(8,128)S(1)} %get-tuple-element.186.grad_middle, f32[8,768]{1,0:T(8,128)S(1)} %get-tuple-element.171.mods, ...), custom_call_target="tpu_custom_call" | custom-call | flops 10000 | bytes 6000 | tf_op jit(solution)/shard_map/pallas_call | solution.py:817
  155.2 7.0 %collective-permute-done.25.b_came = bf16[192,384]{1,0:T(8,128)(2,1)S(1)} collective-permute-done((bf16[192,384]{1,0:T(8,128)(2,1)S(1)}, bf16[192,384]{1,0:T(8,128)(2,1)S(1)}, u32[]{:S(2)}, u32[]{:S(2)}) %collective-permute-start.25) | collective-permute-done | bytes 147488 | tf_op jit(solution)/shard_map/ppermute | solution.py:834
  163.1 2.7 %collective-permute-done.28.d_came = bf16[112,768]{1,0:T(8,128)(2,1)S(1)} collective-permute-done((bf16[112,768]{1,0:T(8,128)(2,1)S(1)}, bf16[112,768]{1,0:T(8,128)(2,1)S(1)}, u32[]{:S(2)}, u32[]{:S(2)}) %collective-permute-start.28) | collective-permute-done | bytes 172064 | tf_op jit(solution)/shard_map/ppermute | solution.py:834
  168.2 4.5 %shard_map.295 = (f32[576,768]{1,0:T(8,128)}, f32[4608]{0:T(1024)}, f32[1001,768]{1,0:T(8,128)}, f32[9,768]{1,0:T(8,128)}, f32[768]{0:T(1024)}) custom-call(s32[8]{0:T(128)S(1)} %pad_add_fusion.2.refs_0_, f32[6,8,768]{2,1,0:T(8,128)S(1)} %shard_map.293.refs_1_, f32[6,8,768]{2,1,0:T(8,128)S(1)} %collective-permute-done.23.refs_2_, bf16[4608,768]{1,0:T(8,128)(2,1)S(1)} %bitcast.7), custom_call_target="tpu_custom_call" | custom-call | flops 100000 | bytes 14000 | tf_op jit(solution)/shard_map/pallas_call | solution.py:817
  (119 shorter events, 51.0 us)
Async XLA Ops:
  26.1 20.7 %collective-permute-start.1 = (bf16[512,768]{1,0:T(8,128)(2,1)S(1)}, bf16[512,768]{1,0:T(8,128)(2,1)S(1)}, u32[]{:S(2)}, u32[]{:S(2)}) collective-permute-start(bf16[512,768]{1,0:T(8,128)(2,1)S(1)} %shard_map.273.chip), channel_id=1, source_target_pairs={{0,2},{1,3},{2,0},{3,1},{4,6},{5,7},{6,4},{7,5},{8,10},{9,11},{10,... | collective-permute-start | bytes 2359304 | tf_op jit(solution)/shard_map/ppermute | solution.py:834
  29.6 6.8 %collective-permute-start.2 = (s32[1]{0:T(128)}, s32[1]{0:T(128)}, u32[]{:S(2)}, u32[]{:S(2)}) collective-permute-start(s32[1]{0:T(128)} %param.21), channel_id=1, source_target_pairs={{0,4},{4,0},{8,12},{12,8},{16,20},{20,16},{24,28},{28,24},{1,5},{5... | collective-permute-start | bytes 20 | tf_op jit(solution)/shard_map/ppermute | solution.py:834
  41.2 4.4 %collective-permute-start.4 = (s32[4]{0:T(128)S(1)}, s32[4]{0:T(128)S(1)}, u32[]{:S(2)}, u32[]{:S(2)}) collective-permute-start(s32[4]{0:T(128)S(1)} %pad_add_fusion.1), channel_id=1, source_target_pairs={{0,16},{4,20},{8,24},{12,28},{16,0},{20,4},{24,8},{28,12},{1,17},{... | collective-permute-start | bytes 56 | tf_op jit(solution)/shard_map/ppermute | solution.py:834
  71.5 19.7 %collective-permute-start.9 = (bf16[512,768]{1,0:T(8,128)(2,1)S(1)}, bf16[512,768]{1,0:T(8,128)(2,1)S(1)}, u32[]{:S(2)}, u32[]{:S(2)}) collective-permute-start(bf16[512,768]{1,0:T(8,128)(2,1)S(1)} %shard_map.277.chip), channel_id=1, source_target_pairs={{0,2},{1,3},{2,0},{3,1},{4,6},{5,7},{6,4},{7,5},{8,10},{9,11},{10,... | collective-permute-start | bytes 2359304 | tf_op jit(solution)/shard_map/ppermute | solution.py:834
  77.4 16.4 %collective-permute-start.10 = (bf16[400,768]{1,0:T(8,128)(2,1)S(1)}, bf16[400,768]{1,0:T(8,128)(2,1)S(1)}, u32[]{:S(2)}, u32[]{:S(2)}) collective-permute-start(bf16[400,768]{1,0:T(8,128)(2,1)S(1)} %get-tuple-element.141), channel_id=1, source_target_pairs={{0,4},{4,0},{8,12},{12,8},{16,20},{20,16},{24,28},{28,24},{1,5},{5... | collective-permute-start | bytes 1843208 | tf_op jit(solution)/shard_map/ppermute | solution.py:834
  79.0 14.8 %collective-permute-start.11 = (bf16[384,768]{1,0:T(8,128)(2,1)S(1)}, bf16[384,768]{1,0:T(8,128)(2,1)S(1)}, u32[]{:S(2)}, u32[]{:S(2)}) collective-permute-start(bf16[384,768]{1,0:T(8,128)(2,1)S(1)} %get-tuple-element.142), channel_id=1, source_target_pairs={{0,8},{4,12},{8,0},{12,4},{16,24},{20,28},{24,16},{28,20},{1,9},{5... | collective-permute-start | bytes 1769480 | tf_op jit(solution)/shard_map/ppermute | solution.py:834
  107.6 16.8 %collective-permute-start.13 = (bf16[640,768]{1,0:T(8,128)(2,1)S(1)}, bf16[640,768]{1,0:T(8,128)(2,1)S(1)}, u32[]{:S(2)}, u32[]{:S(2)}) collective-permute-start(bf16[640,768]{1,0:T(8,128)(2,1)S(1)} %get-tuple-element.157), channel_id=1, source_target_pairs={{0,1},{1,0},{2,3},{3,2},{4,5},{5,4},{6,7},{7,6},{8,9},{9,8},{10,11... | collective-permute-start | bytes 2949128 | tf_op jit(solution)/shard_map/ppermute | solution.py:834
  107.8 4.9 %collective-permute-start.7 = (bf16[512,768]{1,0:T(8,128)(2,1)S(1)}, bf16[512,768]{1,0:T(8,128)(2,1)S(1)}, u32[]{:S(2)}, u32[]{:S(2)}) collective-permute-start(bf16[512,768]{1,0:T(8,128)(2,1)S(1)} %get-tuple-element.134.send), channel_id=1, source_target_pairs={{0,1},{1,0},{2,3},{3,2},{4,5},{5,4},{6,7},{7,6},{8,9},{9,8},{10,11... | collective-permute-start | bytes 2359304 | tf_op jit(solution)/shard_map/ppermute | solution.py:834
  108.4 16.0 %collective-permute-start.14 = (bf16[208,768]{1,0:T(8,128)(2,1)S(1)}, bf16[208,768]{1,0:T(8,128)(2,1)S(1)}, u32[]{:S(2)}, u32[]{:S(2)}) collective-permute-start(bf16[208,768]{1,0:T(8,128)(2,1)S(1)} %get-tuple-element.162), channel_id=1, source_target_pairs={{0,8},{4,12},{8,0},{12,4},{16,24},{20,28},{24,16},{28,20},{1,9},{5... | collective-permute-start | bytes 958472 | tf_op jit(solution)/shard_map/ppermute | solution.py:834
  110.1 13.5 %collective-permute-start.15 = (bf16[192,768]{1,0:T(8,128)(2,1)S(1)}, bf16[192,768]{1,0:T(8,128)(2,1)S(1)}, u32[]{:S(2)}, u32[]{:S(2)}) collective-permute-start(bf16[192,768]{1,0:T(8,128)(2,1)S(1)} %get-tuple-element.163), channel_id=1, source_target_pairs={{0,16},{4,20},{8,24},{12,28},{16,0},{20,4},{24,8},{28,12},{1,17},{... | collective-permute-start | bytes 884744 | tf_op jit(solution)/shard_map/ppermute | solution.py:834
  112.9 22.1 %collective-permute-start.8 = (bf16[256,768]{1,0:T(8,128)(2,1)S(1)}, bf16[256,768]{1,0:T(8,128)(2,1)S(1)}, u32[]{:S(2)}, u32[]{:S(2)}) collective-permute-start(bf16[256,768]{1,0:T(8,128)(2,1)S(1)} %get-tuple-element.136), channel_id=1, source_target_pairs={{0,2},{1,3},{2,0},{3,1},{4,6},{5,7},{6,4},{7,5},{8,10},{9,11},{10,... | collective-permute-start | bytes 1179656 | tf_op jit(solution)/shard_map/ppermute | solution.py:834
  124.7 23.9 %collective-permute-start.17 = (bf16[320,768]{1,0:T(8,128)(2,1)S(1)}, bf16[320,768]{1,0:T(8,128)(2,1)S(1)}, u32[]{:S(2)}, u32[]{:S(2)}) collective-permute-start(bf16[320,768]{1,0:T(8,128)(2,1)S(1)} %get-tuple-element.177), channel_id=1, source_target_pairs={{0,2},{1,3},{2,0},{3,1},{4,6},{5,7},{6,4},{7,5},{8,10},{9,11},{10,... | collective-permute-start | bytes 1474568 | tf_op jit(solution)/shard_map/ppermute | solution.py:834
  125.3 13.8 %collective-permute-start.20 = (bf16[384,384]{1,0:T(8,128)(2,1)S(1)}, bf16[384,384]{1,0:T(8,128)(2,1)S(1)}, u32[]{:S(2)}, u32[]{:S(2)}) collective-permute-start(bf16[384,384]{1,0:T(8,128)(2,1)S(1)} %get-tuple-element.168), channel_id=1, source_target_pairs={{0,4},{4,0},{8,12},{12,8},{16,20},{20,16},{24,28},{28,24},{1,5},{5... | collective-permute-start | bytes 884744 | tf_op jit(solution)/shard_map/ppermute | solution.py:834
  126.1 13.0 %collective-permute-start.21 = (bf16[384,384]{1,0:T(8,128)(2,1)S(1)}, bf16[384,384]{1,0:T(8,128)(2,1)S(1)}, u32[]{:S(2)}, u32[]{:S(2)}) collective-permute-start(bf16[384,384]{1,0:T(8,128)(2,1)S(1)} %get-tuple-element.169), channel_id=1, source_target_pairs={{0,8},{4,12},{8,0},{12,4},{16,24},{20,28},{24,16},{28,20},{1,9},{5... | collective-permute-start | bytes 884744 | tf_op jit(solution)/shard_map/ppermute | solution.py:834
  133.5 4.7 %collective-permute-start.18 = (f32[16,768]{1,0:T(8,128)S(1)}, f32[16,768]{1,0:T(8,128)S(1)}, u32[]{:S(2)}, u32[]{:S(2)}) collective-permute-start(f32[16,768]{1,0:T(8,128)S(1)} %add.12.late), channel_id=1, source_target_pairs={{0,2},{1,3},{2,0},{3,1},{4,6},{5,7},{6,4},{7,5},{8,10},{9,11},{10,... | collective-permute-start | bytes 147464 | tf_op jit(solution)/shard_map/ppermute | solution.py:834
  138.2 4.4 %collective-permute-start.19 = (f32[3,8,768]{2,1,0:T(8,128)S(1)}, f32[3,8,768]{2,1,0:T(8,128)S(1)}, u32[]{:S(2)}, u32[]{:S(2)}) collective-permute-start(f32[3,8,768]{2,1,0:T(8,128)S(1)} %shard_map.289.refs_0_), channel_id=1, source_target_pairs={{0,4},{4,0},{8,12},{12,8},{16,20},{20,16},{24,28},{28,24},{1,5},{5... | collective-permute-start | bytes 221192 | tf_op jit(solution)/shard_map/ppermute | solution.py:834
  142.7 10.6 %collective-permute-start.22 = (f32[4,8,768]{2,1,0:T(8,128)S(1)}, f32[4,8,768]{2,1,0:T(8,128)S(1)}, u32[]{:S(2)}, u32[]{:S(2)}) collective-permute-start(f32[4,8,768]{2,1,0:T(8,128)S(1)} %shard_map.291.refs_0_), channel_id=1, source_target_pairs={{0,8},{4,12},{8,0},{12,4},{16,24},{20,28},{24,16},{28,20},{1,9},{5... | collective-permute-start | bytes 294920 | tf_op jit(solution)/shard_map/ppermute | solution.py:834
  145.3 16.9 %collective-permute-start.25 = (bf16[192,384]{1,0:T(8,128)(2,1)S(1)}, bf16[192,384]{1,0:T(8,128)(2,1)S(1)}, u32[]{:S(2)}, u32[]{:S(2)}) collective-permute-start(bf16[192,384]{1,0:T(8,128)(2,1)S(1)} %get-tuple-element.190), channel_id=1, source_target_pairs={{0,16},{4,20},{8,24},{12,28},{16,0},{20,4},{24,8},{28,12},{1,17},{... | collective-permute-start | bytes 442376 | tf_op jit(solution)/shard_map/ppermute | solution.py:834
  146.2 16.1 %collective-permute-start.24 = (bf16[192,384]{1,0:T(8,128)(2,1)S(1)}, bf16[192,384]{1,0:T(8,128)(2,1)S(1)}, u32[]{:S(2)}, u32[]{:S(2)}) collective-permute-start(bf16[192,384]{1,0:T(8,128)(2,1)S(1)} %get-tuple-element.183), channel_id=1, source_target_pairs={{0,8},{4,12},{8,0},{12,4},{16,24},{20,28},{24,16},{28,20},{1,9},{5... | collective-permute-start | bytes 442376 | tf_op jit(solution)/shard_map/ppermute | solution.py:834
  147.4 18.4 %collective-permute-start.28 = (bf16[112,768]{1,0:T(8,128)(2,1)S(1)}, bf16[112,768]{1,0:T(8,128)(2,1)S(1)}, u32[]{:S(2)}, u32[]{:S(2)}) collective-permute-start(bf16[112,768]{1,0:T(8,128)(2,1)S(1)} %get-tuple-element.208), channel_id=1, source_target_pairs={{0,16},{4,20},{8,24},{12,28},{16,0},{20,4},{24,8},{28,12},{1,17},{... | collective-permute-start | bytes 516104 | tf_op jit(solution)/shard_map/ppermute | solution.py:834
  148.5 14.6 %collective-permute-start.29 = (bf16[96,768]{1,0:T(8,128)(2,1)S(1)}, bf16[96,768]{1,0:T(8,128)(2,1)S(1)}, u32[]{:S(2)}, u32[]{:S(2)}) collective-permute-start(bf16[96,768]{1,0:T(8,128)(2,1)S(1)} %get-tuple-element.210), channel_id=1, source_target_pairs={{0,4},{4,0},{8,12},{12,8},{16,20},{20,16},{24,28},{28,24},{1,5},{5... | collective-permute-start | bytes 442376 | tf_op jit(solution)/shard_map/ppermute | solution.py:834
  153.3 14.9 %collective-permute-start.23 = (f32[6,8,768]{2,1,0:T(8,128)S(1)}, f32[6,8,768]{2,1,0:T(8,128)S(1)}, u32[]{:S(2)}, u32[]{:S(2)}) collective-permute-start(f32[6,8,768]{2,1,0:T(8,128)S(1)} %shard_map.293.refs_1_), channel_id=1, source_target_pairs={{0,16},{4,20},{8,24},{12,28},{16,0},{20,4},{24,8},{28,12},{1,17},{... | collective-permute-start | bytes 442376 | tf_op jit(solution)/shard_map/ppermute | solution.py:834
  162.3 10.5 %collective-permute-start.27 = (bf16[96,384]{1,0:T(8,128)(2,1)S(1)}, bf16[96,384]{1,0:T(8,128)(2,1)S(1)}, u32[]{:S(2)}, u32[]{:S(2)}) collective-permute-start(bf16[96,384]{1,0:T(8,128)(2,1)S(1)} %get-tuple-element.202), channel_id=1, source_target_pairs={{0,4},{4,0},{8,12},{12,8},{16,20},{20,16},{24,28},{28,24},{1,5},{5... | collective-permute-start | bytes 221192 | tf_op jit(solution)/shard_map/ppermute | solution.py:834
  163.1 9.6 %collective-permute-start.26 = (bf16[96,384]{1,0:T(8,128)(2,1)S(1)}, bf16[96,384]{1,0:T(8,128)(2,1)S(1)}, u32[]{:S(2)}, u32[]{:S(2)}) collective-permute-start(bf16[96,384]{1,0:T(8,128)(2,1)S(1)} %get-tuple-element.194), channel_id=1, source_target_pairs={{0,16},{4,20},{8,24},{12,28},{16,0},{20,4},{24,8},{28,12},{1,17},{... | collective-permute-start | bytes 221192 | tf_op jit(solution)/shard_map/ppermute | solution.py:834
  (30 other events, 194.9 us)

commit v4 on v3

--- a/solution.py
+++ b/solution.py
@@ -27,7 +27,6 @@
 score_scale = 0.125
 gelu_slope = math.sqrt(2.0 / math.pi)
 gelu_cubic = 0.044715
-COST = 1000
 BLOCK = 96
 TAIL = 16
 
@@ -134,16 +133,31 @@
 
 
 def kernel_a(
-    tokens, act, b_mod, k_att, w_qkv, w_out, w_mod,
+    act, tokens_far, b_mod_far, k_att_far, w_qkv_far, w_out_far, w_mod,
     mods_out, source, keep, send, mixed_out, q_out, k_out, v_out, att_out, lse_out,
-    grid, natural, temp, kernel, weights, mixed, q_all, k_all, v_all, att_all, lse_all, sems, mod_sem,
+    grid, natural, temp, kernel, tokens, b_mod, k_att, w_qkv, w_out, weights,
+    mixed, q_all, k_all, v_all, att_all, lse_all, sems, in_sems,
 ):
     core, _, _ = here_core()
-    fetch = pltpu.make_async_copy(w_mod.at[pl.ds(0, 2 * WIDTH), :], weights, mod_sem)
-    fetch.start()
+    fetches = [
+        pltpu.make_async_copy(far, near, in_sems.at[n])
+        for n, (far, near) in enumerate(
+            (
+                (w_mod.at[pl.ds(0, 2 * WIDTH), :], weights),
+                (b_mod_far, b_mod),
+                (k_att_far, k_att),
+                (tokens_far, tokens),
+                (w_qkv_far, w_qkv),
+                (w_out_far, w_out),
+            )
+        )
+    ]
+    for fetch in fetches:
+        fetch.start()
     grid[...] = jnp.zeros_like(grid)
+    for fetch in fetches[:4]:
+        fetch.wait()
     kernel[0:9, :] = k_att[...].astype(f32)
-    fetch.wait()
     shift, scale = modulation(act[...], weights, b_mod, (0, 1), 0)
     mods_out[0:1, :] = shift
     mods_out[1:2, :] = scale
@@ -181,6 +195,8 @@
         return carry
 
     lax.fori_loop(0, TILES, conv, 0)
+    for fetch in fetches[4:]:
+        fetch.wait()
     masks = head_masks()
     lane = lax.broadcasted_iota(jnp.int32, (SHARE, 128), 1)
     pairs = (
@@ -270,6 +286,15 @@
     lax.fori_loop(0, TILES, group, 0)
 
 
+def kernel_ga(grad_branch, w_down, grad_act):
+    def step(g, carry):
+        rows = at(g * SHARE, SHARE)
+        grad_act[rows, :] = dot_nn(grad_branch[rows, :], w_down[...])
+        return carry
+
+    lax.fori_loop(0, 4, step, 0)
+
+
 def kernel_b(chip, far, source, mods, b_out, branch_out, middle_out, shaped_out):
     gate = mods[2:3, :]
     shift = mods[3:4, :]
@@ -289,9 +314,9 @@
 
 
 def kernel_c(
-    own, other, grad_branch, w_up, w_down, b_up, k_ffn,
+    own, other, grad_branch, grad_act, w_up, w_down, b_up, k_ffn,
     shaped, activated, grad_hidden, sums, b_keep, b_send, g_keep, g_send,
-    hidden, grad_conv, grad_act, temp, kernel,
+    hidden, grad_conv, temp, kernel,
 ):
     core, _, _ = here_core()
     hidden[...] = jnp.zeros_like(hidden)
@@ -304,7 +329,6 @@
         rows = at(g * SHARE, SHARE)
         a = lax.div(g, 2)
         b = lax.rem(g, 2)
-        grad_act[rows, :] = dot_nn(grad_branch[rows, :], w_down[...])
         temp[...] = dot_nn(shaped[rows, :], w_up[...]) + bias
 
         def place(i, inner):
@@ -428,12 +452,29 @@
         out[:, tile * 128 : tile * 128 + 128] = natural[tile, :, :].astype(bf16)
 
 
+def kernel_p_again(q_all, k_all, lse_all, probs_all):
+    masks = head_masks()
+
+    def step(g, carry):
+        rows = at(g * SHARE, SHARE)
+        query = q_all[rows, :]
+        keys = k_all[rows, :]
+        for h in range(HEADS_HERE):
+            scores = dot_nt(jnp.where(masks[h], query, jnp.zeros_like(query)), keys) * score_scale
+            probs_all[HEADS_HERE * g + h] = jnp.exp(scores - lse_all[rows, h : h + 1])
+        return carry
+
+    lax.fori_loop(0, 4, step, 0)
+
+
 def kernel_e(
-    own, other, q_all, k_all, v_all, att_all, lse_all, w_qkv, w_out,
-    grad_branch, right, mixed, keep, send,
-    padded,
+    own, other, q_all, k_all, v_all, att_all, probs_all, w_qkv, w_out, mixed_far,
+    grad_branch, right, mixed, mixed_near, keep, send,
+    padded, sem,
 ):
     core, _, _ = here_core()
+    fetch = pltpu.make_async_copy(mixed_far, mixed_near, sem)
+    fetch.start()
     join_halves(own, other, core, grad_branch)
     masks = head_masks()
     for g in range(4):
@@ -451,8 +492,7 @@
         g_keys = g_query
         g_vals = g_query
         for h in range(HEADS_HERE):
-            scores = dot_nt(jnp.where(masks[h], query, zero), keys) * score_scale
-            probs = jnp.exp(scores - lse_all[rows, h : h + 1])
+            probs = probs_all[HEADS_HERE * g + h]
             g_probs = dot_nt(jnp.where(masks[h], grad, zero), vals)
             spread = jnp.sum(probs * g_probs, axis=-1, keepdims=True)
             g_scores = (probs * (g_probs - spread)).astype(bf16)
@@ -482,6 +522,7 @@
                 out[row : row + 16, :] = padded[2 + b, at16(4 * share * 16, 16), :]
                 row = row + SIDE
                 out[row : row + 16, :] = padded[b, at16((4 * share + 5) * 16, 16), :]
+    fetch.wait()
 
 
 def kernel_n(tokens, natural):
@@ -508,7 +549,7 @@
     sums[0:1, :] = lax.fori_loop(0, HALF // 64, step, jnp.zeros((1, WIDTH), f32))
 
 
-def kernel_s(natural, mixed, mods, k_att, sums_d, sums_q, out, grid, kernel):
+def kernel_s(natural, mixed, mods, k_att, sums_d, sums_q, low, out, grid, kernel):
     _, side, _ = here_core()
     grid[...] = jnp.zeros_like(grid)
     kernel[0:9, :] = k_att[...].astype(f32)
@@ -574,6 +615,7 @@
     out[2:5, :] = sums_d[0:3, :] * once
     out[5:6, :] = sums_q[0:1, :]
     out[15:16, :] = sums_d[3:4, :] * once
+    low[...] = out[...].astype(bf16)
 
 
 def kernel_f(tokens, near, far, grad_middle, mods, k_att, out, grid, grad_shaped, middle, kernel):
@@ -653,20 +695,24 @@
     return lambda rows: held[rows, :] + came[rows, :].astype(f32)
 
 
-def kernel_w(grad, activated, shaped, hidden, sums, d_keep, d_send, u_keep, u_send, total):
-    for left, right, stride, keep, send in (
-        (grad, activated, 1, d_keep, d_send),
-        (shaped, hidden, 2, u_keep, u_send),
-    ):
-
-        def step(i, carry):
-            total[at(i * 256, 256), :] = dot_tn(left[:, at(i * 256, 256)], right[...])
-            return carry
-
-        lax.fori_loop(0, 3, step, 0)
-        split_blocks(8, stride, stride, lambda rows: total[rows, :], keep, send)
-    d_keep[4 * BLOCK :, :] = sums[...].astype(bf16).astype(f32)
-    d_send[4 * BLOCK :, :] = sums[...].astype(bf16)
+def product_tn(left, right, total):
+    def step(i, carry):
+        total[at(i * 256, 256), :] = dot_tn(left[:, at(i * 256, 256)], right[...])
+        return carry
+
+    lax.fori_loop(0, 3, step, 0)
+
+
+def kernel_w_down(grad, activated, sums, keep, send, total):
+    product_tn(grad, activated, total)
+    split_blocks(8, 1, 1, lambda rows: total[rows, :], keep, send)
+    keep[4 * BLOCK :, :] = sums[...].astype(bf16).astype(f32)
+    send[4 * BLOCK :, :] = sums[...].astype(bf16)
+
+
+def kernel_w_up(shaped, hidden, keep, send, total):
+    product_tn(shaped, hidden, total)
+    split_blocks(8, 2, 2, lambda rows: total[rows, :], keep, send)
 
 
 def kernel_w_one(d_held, d_came, u_held, u_came, d_keep, d_send, u_keep, u_send):
@@ -674,28 +720,32 @@
     tail = summed(d_held, d_came)(slice(4 * BLOCK, 4 * BLOCK + TAIL)).astype(bf16)
     d_keep[2 * BLOCK :, :] = tail.astype(f32)
     d_send[2 * BLOCK :, :] = tail
-    split_blocks(4, 2, 4, summed(u_held, u_came), u_keep, u_send)
-
-
-def kernel_w_two(d_held, d_came, u_held, u_came, d_keep, d_send, u_keep, u_send):
-    split_blocks(2, 1, 4, summed(d_held, d_came), d_keep, d_send)
+    split_blocks(4, 1, 1, summed(u_held, u_came), u_keep, u_send)
+
+
+def kernel_w_two(d_held, d_came, u_held, u_came, keep, send):
+    mine = bit_here(4)
+    for n, (held, came) in enumerate(((d_held, d_came), (u_held, u_came))):
+        total = summed(held, came)
+        rows = slice(n * BLOCK, (n + 1) * BLOCK)
+        keep[rows, :] = total(at16(mine * BLOCK, BLOCK))
+        send[rows, :] = total(at16((1 - mine) * BLOCK, BLOCK)).astype(bf16)
     tail = summed(d_held, d_came)(slice(2 * BLOCK, 2 * BLOCK + TAIL)).astype(bf16)
-    d_keep[BLOCK:, :] = tail.astype(f32)
-    d_send[BLOCK:, :] = tail
-    split_blocks(2, 1, 1, summed(u_held, u_came), u_keep, u_send)
-
-
-def kernel_w_end(d_held, d_came, u_held, u_came, down, up, k_out, b_up, b_down):
-    total = summed(d_held, d_came)
+    keep[2 * BLOCK :, :] = tail.astype(f32)
+    send[2 * BLOCK :, :] = tail
+
+
+def kernel_w_end(held, came, down, up, k_out, b_up, b_down):
+    total = summed(held, came)
     down[...] = total(slice(0, BLOCK))
-    up[...] = summed(u_held, u_came)(slice(0, BLOCK))
-    tail = total(slice(BLOCK, BLOCK + TAIL))
+    up[...] = total(slice(BLOCK, 2 * BLOCK))
+    tail = total(slice(2 * BLOCK, 2 * BLOCK + TAIL))
     k_out[...] = tail[0:9, :]
     b_up[...] = tail[9:10, :].reshape(WIDTH)
     b_down[...] = tail[10:11, :].reshape(WIDTH)
 
 
-def kernel_v(mixed, grad_branch, right, a_keep, a_send, b_keep, b_send, total):
+def kernel_v(mixed, grad_branch, right, keep, send, total):
     lane = lax.broadcasted_iota(jnp.int32, (256, 256), 1)
 
     def step(i, carry):
@@ -708,27 +758,22 @@
         return carry
 
     lax.fori_loop(0, 3, step, 0)
-    split_blocks(8, 1, 1, lambda rows: total[rows, 0:384], a_keep, a_send)
-    split_blocks(8, 2, 2, lambda rows: total[rows, 384:768], b_keep, b_send)
-
-
-def kernel_v_one(a_held, a_came, b_held, b_came, a_keep, a_send, b_keep, b_send):
-    split_blocks(4, 1, 2, summed(a_held, a_came), a_keep, a_send)
-    split_blocks(4, 2, 4, summed(b_held, b_came), b_keep, b_send)
-
-
-def kernel_v_two(a_held, a_came, b_held, b_came, a_keep, a_send, b_keep, b_send):
-    split_blocks(2, 1, 4, summed(a_held, a_came), a_keep, a_send)
-    split_blocks(2, 1, 1, summed(b_held, b_came), b_keep, b_send)
-
-
-def kernel_v_end(a_held, a_came, b_held, b_came, qkv, out):
-    first = summed(a_held, a_came)(slice(0, BLOCK))
-    last = summed(b_held, b_came)(slice(0, BLOCK))
-    qkv[0] = first[:, :HEAD_WIDTH]
-    qkv[1] = first[:, HEAD_WIDTH:]
-    qkv[2] = last[:, :HEAD_WIDTH]
-    out[...] = last[:, HEAD_WIDTH:]
+    split_blocks(8, 1, 1, lambda rows: total[rows, :], keep, send)
+
+
+def kernel_v_one(held, came, keep, send):
+    split_blocks(4, 1, 2, summed(held, came), keep, send)
+
+
+def kernel_v_two(held, came, keep, send):
+    split_blocks(2, 1, 4, summed(held, came), keep, send)
+
+
+def kernel_v_end(held, came, qkv, out):
+    total = summed(held, came)(slice(0, BLOCK))
+    for kind in range(3):
+        qkv[kind] = total[:, kind * HEAD_WIDTH : (kind + 1) * HEAD_WIDTH]
+    out[...] = total[:, 3 * HEAD_WIDTH :]
 
 
 def kernel_join(near, came, chip):
@@ -739,24 +784,24 @@
     _, side, _ = here_core()
     rows = own.shape[0]
     for out, x in ((own, side), (send, 1 - side)):
-        part = at16(x * rows, rows)
-        out[...] = (near[part, :].astype(f32) + came[part, :].astype(f32)).astype(bf16)
-
-
-def kernel_slot(late, came, cond, out):
-    total = late[...] + came[...]
-    out[0, 0:6, :] = total[0:6, :].astype(bf16).astype(f32)
-    out[0, 6:7, :] = cond[...]
-    out[0, 7:8, :] = cond[...]
-    out[1] = total[6:14, :]
-    out[2, 0:2, :] = total[14:16, :]
-    out[2, 2:8, :] = jnp.zeros((6, WIDTH), f32)
+        where = at16(x * rows, rows)
+        out[...] = (near[where, :].astype(f32) + came[where, :].astype(f32)).astype(bf16)
+
+
+def kernel_slot(late, cond, out):
+    parts = [late[n].astype(f32) for n in range(4)]
+    total = (parts[0] + parts[1]) + (parts[2] + parts[3])
+    high = cond[...].astype(bf16).astype(f32)
+    out[0] = jnp.concatenate([total[0:6, :], high, cond[...] - high]).astype(bf16)
+    out[1] = total[6:14, :].astype(bf16)
+    out[2] = jnp.concatenate([total[14:16, :], jnp.zeros((6, WIDTH), f32)]).astype(bf16)
 
 
 def kernel_gather(slots, held, came, out):
-    out[0:slots] = held[0:slots]
-    out[slots : 2 * slots] = came[0:slots]
-    out[2 * slots : 2 * slots + 2] = held[slots : slots + 2] + came[slots : slots + 2]
+    out[0:slots] = held[0:slots].astype(out.dtype)
+    out[slots : 2 * slots] = came[0:slots].astype(out.dtype)
+    total = held[slots : slots + 2].astype(f32) + came[slots : slots + 2].astype(f32)
+    out[2 * slots : 2 * slots + 2] = total.astype(out.dtype)
 
 
 def kernel_g(
@@ -767,7 +812,7 @@
     here = lax.axis_index("dp")
     kernel_gather(size // 2, near, came, held)
     class_out[...] = jnp.zeros_like(class_out)
-    conds = held[0:size, 6, :]
+    conds = held[0:size, 6, :] + held[0:size, 7, :]
     sig = 1.0 / (1.0 + jnp.exp(-conds))
     act = (conds * sig).astype(bf16)
     total = jnp.zeros((size, WIDTH), f32)
@@ -807,7 +852,7 @@
     return jax.ShapeDtypeStruct(shape, dtype)
 
 
-def call(kernel, scalars, arrays, far_arrays, outs, scratch, mebibytes, flops, moved):
+def call(kernel, scalars, arrays, far_arrays, outs, scratch, mebibytes, flops, moved, cost=0):
     spots = (
         [pl.BlockSpec(memory_space=pltpu.SMEM)] * len(scalars)
         + [pl.BlockSpec(memory_space=pltpu.VMEM)] * len(arrays)
@@ -821,7 +866,7 @@
         out_specs=tuple(pl.BlockSpec(memory_space=m) for m in spaces),
         scratch_shapes=scratch,
         compiler_params=pltpu.CompilerParams(vmem_limit_bytes=mebibytes << 20),
-        cost_estimate=pl.CostEstimate(flops=flops // COST, bytes_accessed=moved // COST, transcendentals=0),
+        cost_estimate=pl.CostEstimate(flops=0, bytes_accessed=cost, transcendentals=0),
     )(
         *scalars,
         *(pltpu.with_memory_space_constraint(a, pltpu.VMEM) for a in arrays),
@@ -874,10 +919,8 @@
     return call(kernel_join_split, [], [near, came], [], [part, part], [], 4, 10**6, 3 * 10**6)
 
 
-def weight_step(kernel, blocks, tail, width, *arrays):
-    first = (blocks * BLOCK + tail, width)
-    last = (blocks * BLOCK, width)
-    outs = [vmem(first, f32), vmem(first, bf16), vmem(last, f32), vmem(last, bf16)]
+def weight_step(kernel, shapes, *arrays):
+    outs = [vmem(shape, kind) for shape in shapes for kind in (f32, bf16)]
     return call(kernel, [], list(arrays), [], outs, [], 4, 10**6, 4 * 10**6)
 
 
@@ -931,18 +974,20 @@
     w_back = w_out.T
 
     mods_a, source, keep, send, mixed, query, keys, vals, attended, lse = call(
-        kernel_a, [], [tokens, act, b_mod, k_att, w_three, w_back], [w_mod],
+        kernel_a, [], [act], [tokens, b_mod, k_att, w_three, w_back, w_mod],
         [
             vmem((8, WIDTH), f32), vmem(half, f32), vmem(half, bf16), vmem(half, bf16),
             hbm(full, bf16), hbm(head, bf16), hbm(head, bf16), hbm(head, bf16), hbm(head, bf16),
             hbm((ITEM, 128), f32),
         ],
         [
-            grid, natural, temp, taps, pltpu.VMEM((2 * WIDTH, WIDTH), bf16), pltpu.VMEM(full, bf16),
+            grid, natural, temp, taps, pltpu.VMEM(full, bf16), pltpu.VMEM(b_mod.shape, bf16),
+            pltpu.VMEM(k_att.shape, bf16), pltpu.VMEM(w_three.shape, bf16),
+            pltpu.VMEM(w_back.shape, bf16), pltpu.VMEM((2 * WIDTH, WIDTH), bf16), pltpu.VMEM(full, bf16),
             pltpu.VMEM(head, bf16), pltpu.VMEM(head, bf16), pltpu.VMEM(head, bf16),
-            pltpu.VMEM(head, bf16), pltpu.VMEM((ITEM, 128), f32), sem((6, 4)), sem,
+            pltpu.VMEM(head, bf16), pltpu.VMEM((ITEM, 128), f32), sem((6, 4)), sem((6,)),
         ],
-        22, 3 * 10**9, 10**7,
+        24, 3 * 10**9, 10**7,
     )
     chip = join(keep, swap(send, "tensor", 1))
     far = swap(chip, "tensor", 2)
@@ -952,8 +997,11 @@
         [vmem((8, WIDTH), f32), vmem(full, bf16), vmem(half, bf16), vmem(half, bf16)],
         [natural, pltpu.VMEM((4 * WIDTH, WIDTH), bf16), sem], 12, 10**8, 8 * 10**6,
     )
+    (grad_act,) = call(
+        kernel_ga, [], [grad_ffn, w_down], [], [vmem(full, f32)], [], 6, 12 * 10**8, 6 * 10**6
+    )
     ids = gather_xor(class_id)
-    far, mods_p, ids = together(far, mods_p, ids)
+    far, mods_p, ids, _ = together(far, mods_p, ids, grad_act)
     branch, middle, shaped_own = call(
         kernel_b, [], [chip, far, source, mods_p, b_out], [],
         [vmem(half, f32), vmem(half, f32), vmem(half, bf16)], [], 6, 10**7, 7 * 10**6,
@@ -961,23 +1009,28 @@
     shaped_other = swap(shaped_own, "tensor", 1)
 
     shaped, activated, grad_hidden, sums_c, b_keep, b_send, g_keep, g_send = call(
-        kernel_c, [], [shaped_own, shaped_other, grad_ffn, w_up, w_down, b_up, k_ffn], [],
+        kernel_c, [], [shaped_own, shaped_other, grad_ffn, grad_act, w_up, w_down, b_up, k_ffn], [],
         [vmem(full, bf16)] * 3 + [vmem((16, WIDTH), f32)] + [vmem(half, bf16)] * 4,
-        [grid, grid, pltpu.VMEM(full, f32), temp, taps], 16, 5 * 10**9, 12 * 10**6,
-    )
-    chip = join(g_keep, swap(g_send, "tensor", 1))
+        [grid, grid, temp, taps], 13, 5 * 10**9, 12 * 10**6,
+    )
+    g_came = swap(g_send, "tensor", 1)
+    total_scratch = [pltpu.VMEM((WIDTH, WIDTH), f32)]
+    if eight:
+        d_keep, d_send = call(
+            kernel_w_down, [], [grad_ffn, activated, sums_c], [],
+            [vmem((4 * BLOCK + TAIL, WIDTH), f32), vmem((4 * BLOCK + TAIL, WIDTH), bf16)],
+            total_scratch, 6, 12 * 10**8, 5 * 10**6,
+        )
+        g_came, _ = together(g_came, d_send)
+    chip = join(g_keep, g_came)
     far = swap(chip, "tensor", 2)
-    _, activated, b_send, sums_c = together(chip, activated, b_send, sums_c)
-    b_own, b_part = join_split(b_keep, swap(b_send, "tensor", 1))
-    b_far = swap(b_part, "tensor", 2)
+    _, shaped, b_send = together(chip, shaped, b_send)
+    b_came = swap(b_send, "tensor", 1)
     if eight:
-        d_keep, d_send, u_keep, u_send = call(
-            kernel_w, [], [grad_ffn, activated, shaped, grad_hidden, sums_c], [],
-            [
-                vmem((4 * BLOCK + TAIL, WIDTH), f32), vmem((4 * BLOCK + TAIL, WIDTH), bf16),
-                vmem((4 * BLOCK, WIDTH), f32), vmem((4 * BLOCK, WIDTH), bf16),
-            ],
-            [pltpu.VMEM((WIDTH, WIDTH), f32)], 6, 24 * 10**8, 9 * 10**6,
+        u_keep, u_send = call(
+            kernel_w_up, [], [shaped, grad_hidden], [],
+            [vmem((4 * BLOCK, WIDTH), f32), vmem((4 * BLOCK, WIDTH), bf16)],
+            total_scratch, 6, 12 * 10**8, 5 * 10**6,
         )
         d_came = swap(d_send, "dp", 1)
         u_came = swap(u_send, "dp", 2)
@@ -995,100 +1048,100 @@
         kernel_q, [], [b_keep, b_send, cot_half, cot_other, b_down], [], [vmem((8, WIDTH), f32)], [],
         4, 10**7, 4 * 10**6,
     )
-    far, _, _ = together(far, normed, sums_q)
+    query, _ = together(query, sums_q)
+    (probs,) = call(
+        kernel_p_again, [], [query, keys, lse], [], [vmem((12, SHARE, SHARE), f32)], [],
+        6, 10**8, 4 * 10**6,
+    )
+    b_own, b_part = join_split(b_keep, b_came)
+    far, b_part, _, _ = together(far, b_part, normed, probs)
+    b_far = swap(b_part, "tensor", 2)
     if eight:
         far, d_came, u_came = together(far, d_came, u_came)
-        d_keep, d_send, u_keep, u_send = weight_step(
-            kernel_w_one, 2, TAIL, WIDTH, d_keep, d_came, u_keep, u_came
-        )
-        d_came = swap(d_send, "dp", 2)
-        u_came = swap(u_send, "dp", 4)
     grad_middle, attn_own, sums_d = call(
         kernel_d, [], [chip, far, branch, middle, cot_half, mods_p], [],
         [vmem(half, f32), vmem(half, bf16), vmem((8, WIDTH), f32)], [], 6, 10**7, 8 * 10**6,
     )
     attn_other = swap(attn_own, "tensor", 1)
-
-    grad_attn, right, mixed_grad, h_keep, h_send = call(
+    if eight:
+        d_came, u_came, _ = together(d_came, u_came, attn_own)
+        d_keep, d_send, u_keep, u_send = weight_step(
+            kernel_w_one, [(2 * BLOCK + TAIL, WIDTH), (2 * BLOCK, WIDTH)], d_keep, d_came, u_keep, u_came
+        )
+        attn_other, _, _ = together(attn_other, d_send, u_send)
+        d_came = swap(d_send, "dp", 2)
+        u_came = swap(u_send, "dp", 1)
+
+    grad_attn, right, mixed_grad, mixed, h_keep, h_send = call(
         kernel_e, [],
-        [attn_own, attn_other, query, keys, vals, attended, lse, w_three, w_back], [],
-        [vmem(full, bf16)] * 3 + [vmem((2 * HALO, WIDTH), bf16)] * 2,
-        [pltpu.VMEM((4, 288, WIDTH), bf16)], 8, 3 * 10**9, 10**7,
-    )
+        [attn_own, attn_other, query, keys, vals, attended, probs, w_three, w_back], [mixed],
+        [vmem(full, bf16)] * 4 + [vmem((2 * HALO, WIDTH), bf16)] * 2,
+        [pltpu.VMEM((4, 288, WIDTH), bf16), sem], 8, 3 * 10**9, 10**7,
+    )
+    if eight:
+        d_came, u_came, b_far, right, h_send = together(d_came, u_came, b_far, right, h_send)
     h_came = swap(h_send, "tensor", 1)
     w_mod_late, _ = together(w_mod, mixed_grad)
     if eight:
-        a_keep, a_send, e_keep, e_send = call(
+        ffn_keep, ffn_send = weight_step(
+            kernel_w_two, [(2 * BLOCK + TAIL, WIDTH)], d_keep, d_came, u_keep, u_came
+        )
+        a_keep, a_send = call(
             kernel_v, [], [mixed, grad_attn, right], [],
-            [vmem((4 * BLOCK, 384), f32), vmem((4 * BLOCK, 384), bf16)] * 2,
+            [vmem((4 * BLOCK, WIDTH), f32), vmem((4 * BLOCK, WIDTH), bf16)],
             [pltpu.VMEM((WIDTH, WIDTH), f32)], 6, 16 * 10**8, 7 * 10**6,
         )
-        h_came, d_came, u_came, mixed_grad, _, _ = together(
-            h_came, d_came, u_came, mixed_grad, a_send, e_send
-        )
+        h_came, _, _ = together(h_came, a_send, ffn_send)
         a_came = swap(a_send, "dp", 1)
-        e_came = swap(e_send, "dp", 2)
-        d_keep, d_send, u_keep, u_send = weight_step(
-            kernel_w_two, 1, TAIL, WIDTH, d_keep, d_came, u_keep, u_came
-        )
-        d_came = swap(d_send, "dp", 4)
-        u_came = swap(u_send, "dp", 1)
+        ffn_came = swap(ffn_send, "dp", 4)
     else:
         last = dot_tn(grad_attn, right[:, 3 * HEAD_WIDTH :])
         total = jnp.concatenate([dot_tn(mixed, right[:, : 3 * HEAD_WIDTH]), last], axis=1)
         att_grads = scatter_plain(total[None])[0]
-    h_own, h_part = join_split(h_keep, h_came)
-    h_far = swap(h_part, "tensor", 2)
+    h_own, part = join_split(h_keep, h_came)
+    mixed_grad, _ = together(mixed_grad, part)
     (late,) = call(
         kernel_s, [], [normed, mixed_grad, mods_a, k_att, sums_d, sums_q], [],
-        [vmem((16, WIDTH), f32)], [grid, taps], 8, 10**8, 4 * 10**6,
-    )
-    late = late + swap(late, "tensor", 1)
-    late_came = swap(late, "tensor", 2)
-    b_far, _ = together(b_far, late)
-    (block_out,) = call(
-        kernel_o, [item_count], [b_own, b_far, middle, mods_p, b_down], [],
-        [plain((SHARE, WIDTH), bf16)], [share_tiles], 4, 10**7, 4 * 10**6,
-    )
-    late_came, _ = together(late_came, block_out)
+        [vmem((16, WIDTH), bf16)], [taps, grid, taps], 8, 10**8, 4 * 10**6,
+    )
+    late = lax.all_gather(late, "tensor")
     (held,) = call(
-        kernel_slot, [], [late, late_came, cond], [], [vmem((3, 8, WIDTH), f32)], [], 2, 10**5, 10**5
-    )
-    came = swap(held, "dp", bits[0])
-    if eight:
-        a_came, e_came, _ = together(a_came, e_came, held)
-        a_keep, a_send, e_keep, e_send = weight_step(
-            kernel_v_one, 2, 0, 384, a_keep, a_came, e_keep, e_came
-        )
-        a_came = swap(a_send, "dp", 2)
-        e_came = swap(e_send, "dp", 4)
-        came, _ = together(came, a_send)
-    for step, bit in enumerate(bits[1:], 1):
-        slots = 1 << (step - 1)
+        kernel_slot, [], [late, cond], [], [vmem((3, 8, WIDTH), bf16)], [], 2, 10**5, 10**5
+    )
+    part, _ = together(part, held)
+    part_far = swap(part, "tensor", 2)
+    for step, bit in enumerate(bits):
+        came = swap(held, "dp", bit)
+        if step == len(bits) - 1:
+            part_far, _ = together(part_far, held)
+            (grad_tokens,) = call(
+                kernel_f, [], [tokens, h_own, part_far, grad_middle, mods_a, k_att], [],
+                [plain((SHARE, WIDTH), f32)],
+                [pltpu.VMEM((TILES, SHARE_GRID_ROWS, 128), f32), share_tiles, share_tiles, taps],
+                6, 10**7, 6 * 10**6, 0,
+            )
+            (block_out,) = call(
+                kernel_o, [item_count], [b_own, b_far, middle, mods_p, b_down], [],
+                [plain((SHARE, WIDTH), bf16)], [share_tiles], 4, 10**7, 4 * 10**6,
+            )
+            came, _, _ = together(came, grad_tokens, block_out)
+            break
+        slots = 1 << step
 
         def kernel(*refs, slots=slots):
             kernel_gather(slots, *refs)
 
         (held,) = call(
-            kernel, [], [held, came], [], [vmem((2 * slots + 2, 8, WIDTH), f32)], [], 4, 10**5, 10**5
+            kernel, [], [held, came], [], [vmem((2 * slots + 2, 8, WIDTH), bf16)], [], 4, 10**5, 10**5
         )
-        came = swap(held, "dp", bit)
-        if step == 1:
-            h_far, _ = together(h_far, held)
-            (grad_tokens,) = call(
-                kernel_f, [], [tokens, h_own, h_far, grad_middle, mods_a, k_att], [],
-                [plain((SHARE, WIDTH), f32)],
-                [pltpu.VMEM((TILES, SHARE_GRID_ROWS, 128), f32), share_tiles, share_tiles, taps],
-                6, 10**7, 6 * 10**6,
-            )
-            came, _ = together(came, grad_tokens)
+        if eight and step == 0:
+            a_came, ffn_came, _ = together(a_came, ffn_came, held)
+            a_keep, a_send = weight_step(kernel_v_one, [(2 * BLOCK, WIDTH)], a_keep, a_came)
+            a_came = swap(a_send, "dp", 2)
     if eight:
-        a_came, e_came, _ = together(a_came, e_came, held)
-        a_keep, a_send, e_keep, e_send = weight_step(
-            kernel_v_two, 1, 0, 384, a_keep, a_came, e_keep, e_came
-        )
+        a_came, _ = together(a_came, held)
+        a_keep, a_send = weight_step(kernel_v_two, [(BLOCK, WIDTH)], a_keep, a_came)
         a_came = swap(a_send, "dp", 4)
-        e_came = swap(e_send, "dp", 1)
         came, _ = together(came, a_send)
 
     share = w_mod.shape[0] // items
@@ -1113,12 +1166,12 @@
         rows = plain((BLOCK, WIDTH), f32)
         flat = plain((WIDTH,), f32)
         grad_down, grad_up, grad_k_ffn, grad_b_up, grad_b_down = call(
-            kernel_w_end, [], [d_keep, d_came, u_keep, u_came], [],
+            kernel_w_end, [], [ffn_keep, ffn_came], [],
             [rows, rows, plain((9, WIDTH), f32), flat, flat], [], 4, 10**6, 2 * 10**6,
         )
-        a_came, e_came, _, _ = together(a_came, e_came, grad_b_mod, grad_b_up)
+        a_came, _, _ = together(a_came, grad_b_mod, grad_b_up)
         grad_qkv, grad_out = call(
-            kernel_v_end, [], [a_keep, a_came, e_keep, e_came], [],
+            kernel_v_end, [], [a_keep, a_came], [],
             [plain((3, BLOCK, HEAD_WIDTH), f32), plain((BLOCK, HEAD_WIDTH), f32)], [], 4, 10**6, 10**6,
         )
         grad_qkv = jnp.transpose(grad_qkv, (1, 0, 2))

time: 174 us -> 151 us (0.87)
  waiting for transfers between devices: 48.8 us -> 30.9 us
  starting transfers between devices: 35.7 us -> 27.2 us
  blocking collectives: 0 us -> 5.52 us
  local copies, waits for them, and re-layouts: 5.06 us -> 0.78 us
  Pallas kernels: 78.4 us -> 80.4 us
    ppermute x30 -> x24, waiting for transfers between devices: 48.8 us -> 30.9 us  [swap(): return lax.ppermute(values, axis, [(i, i ^ bit) for i in range(size)])]
    ppermute x30 -> x24, starting transfers between devices: 35.7 us -> 27.2 us  [swap(): return lax.ppermute(values, axis, [(i, i ^ bit) for i in range(size)])]
    all_gather x0 -> x1, blocking collectives: none -> 5.52 us  [shards(): late = lax.all_gather(late, 'tensor')]
    unnamed x48 -> x38, local copies, waits for them, and re-layouts: 5.06 us -> 0.77 us
    pallas_call x27 -> x30, Pallas kernels: 78.4 us -> 80.4 us  [call(): pl.pallas_call(kernel, out_shape=tuple(outs), in_specs=spots, out_specs=t...]
  transfers between devices with their start and end apart: 30 -> 24, of which waited for: 17 -> 10; matrix products, arithmetic and copies ran while one was open for 1% -> 2% of each run, Pallas kernels for 18% -> 28%
where the time goes in v4:
time: 151 us
  Pallas kernels  80.4 us (53%)
  waiting for transfers between devices  30.9 us (20%)
  starting transfers between devices  27.2 us (18%)
  blocking collectives  5.52 us (4%)
  other arithmetic  3.11 us (2%)
  between operations  2.98 us (2%)
    pallas_call x30, Pallas kernels, call(): pl.pallas_call(kernel, out_shape=tuple(outs), in_specs=spots, out_specs=t...  80.4 us
    ppermute x24, waiting for transfers between devices, swap(): return lax.ppermute(values, axis, [(i, i ^ bit) for i in range(size)])  30.9 us
    ppermute x24, starting transfers between devices, swap(): return lax.ppermute(values, axis, [(i, i ^ bit) for i in range(size)])  27.2 us
    all_gather x1, blocking collectives, shards(): late = lax.all_gather(late, 'tensor')  5.52 us
  transfers between devices with their start and end apart: 24, of which 10 were waited for; matrix products, arithmetic and copies ran while one was open for 2% of the time, Pallas kernels for 28%

profile of v4, /device:TPU:0, one launch (start us, length us, event | category | flops | bytes accessed | tf_op | source)
XLA Modules:
  0.0 150.8 jit_solution(12738332854141555164)
XLA Ops:
  2.8 16.2 %shard_map.272 = (f32[8,768]{1,0:T(8,128)S(1)}, f32[512,768]{1,0:T(8,128)S(1)}, bf16[512,768]{1,0:T(8,128)(2,1)S(1)}, bf16[512,768]{1,0:T(8,128)(2,1)S(1)}, bf16...) custom-call(bf16[16,768]{1,0:T(8,128)(2,1)S(1)} %broadcast_in_dim.10, ...), custom_call_target="tpu_custom_call" | custom-call | tf_op jit(solution)/shard_map/pallas_call | solution.py:862
  19.6 1.9 %collective-permute-done.came = bf16[512,768]{1,0:T(8,128)(2,1)S(1)} collective-permute-done((bf16[512,768]{1,0:T(8,128)(2,1)S(1)}, bf16[512,768]{1,0:T(8,128)(2,1)S(1)}, u32[]{:S(2)}, u32[]{:S(2)}) %collective-permute-start) | collective-permute-done | bytes 786464 | tf_op jit(solution)/shard_map/ppermute | solution.py:879
  21.7 2.9 %collective-permute-start.1 = (bf16[512,768]{1,0:T(8,128)(2,1)S(1)}, bf16[512,768]{1,0:T(8,128)(2,1)S(1)}, u32[]{:S(2)}, u32[]{:S(2)}) collective-permute-start(bf16[512,768]{1,0:T(8,128)(2,1)S(1)} %shard_map.273.chip), channel_id=1, source_target_pairs={{0,2},{1,3},{2,0},{3,1},{4,6},{5,7},{6,4},{7,5},{8,10},{9,11},{10,... | collective-permute-start | bytes 2359304 | tf_op jit(solution)/shard_map/ppermute | solution.py:879
  26.8 5.2 %shard_map.274 = (f32[8,768]{1,0:T(8,128)S(1)}, bf16[1024,768]{1,0:T(8,128)(2,1)S(1)}, bf16[512,768]{1,0:T(8,128)(2,1)S(1)}, bf16[512,768]{1,0:T(8,128)(2,1)S(1)}) custom-call(s32[1]{0:T(128)S(6)} %copy.31.count, bf16[1024,768]{1,0:T(8,128)(2,1)S(1)} %copy-done.5, bf16[16,768]{1,0:T(8,128)(2,1)S(1)} %broadcast_in_dim.10.act, bf16[4608]{0:T(1024)(128)(2,1)S(1)} %copy-done.12, ...), custom_call_target="tpu_custom_call" | custom-call | tf_op jit(solution)/shard_map/pallas_call | solution.py:862
  32.0 1.9 %shard_map.275.grad_act = f32[1024,768]{1,0:T(8,128)S(1)} custom-call(bf16[1024,768]{1,0:T(8,128)(2,1)S(1)} %get-tuple-element.120.grad_branch.grad, bf16[768,768]{1,0:T(8,128)(2,1)S(1)} %copy-done.1), custom_call_target="tpu_custom_call" | custom-call | tf_op jit(solution)/shard_map/pallas_call | solution.py:862
  36.3 2.0 %collective-permute-done.3 = s32[2]{0:T(128)S(1)} collective-permute-done((s32[2]{0:T(128)S(1)}, s32[2]{0:T(128)S(1)}, u32[]{:S(2)}, u32[]{:S(2)}) %collective-permute-start.3) | collective-permute-done | bytes 40 | tf_op jit(solution)/shard_map/ppermute | solution.py:879
  39.0 2.6 %collective-permute-start.4 = (s32[4]{0:T(128)S(1)}, s32[4]{0:T(128)S(1)}, u32[]{:S(2)}, u32[]{:S(2)}) collective-permute-start(s32[4]{0:T(128)S(1)} %pad_add_fusion.1), channel_id=1, source_target_pairs={{0,16},{4,20},{8,24},{12,28},{16,0},{20,4},{24,8},{28,12},{1,17},{... | collective-permute-start | bytes 56 | tf_op jit(solution)/shard_map/ppermute | solution.py:879
  46.2 2.3 %collective-permute-done.5.other = bf16[512,768]{1,0:T(8,128)(2,1)S(1)} collective-permute-done((bf16[512,768]{1,0:T(8,128)(2,1)S(1)}, bf16[512,768]{1,0:T(8,128)(2,1)S(1)}, u32[]{:S(2)}, u32[]{:S(2)}) %collective-permute-start.5) | collective-permute-done | bytes 786464 | tf_op jit(solution)/shard_map/ppermute | solution.py:879
  48.5 16.7 %shard_map.277 = (bf16[1024,768]{1,0:T(8,128)(2,1)S(1)}, bf16[1024,768]{1,0:T(8,128)(2,1)S(1)}, bf16[1024,768]{1,0:T(8,128)(2,1)S(1)}, f32[16,768]{1,0:T(8,128)S...) custom-call(bf16[512,768]{1,0:T(8,128)(2,1)S(1)} %get-tuple-element., ...), custom_call_target="tpu_custom_call" | custom-call | tf_op jit(solution)/shard_map/pallas_call | solution.py:862
  65.4 2.0 %shard_map.278 = (f32[400,768]{1,0:T(8,128)S(1)}, bf16[400,768]{1,0:T(8,128)(2,1)S(1)}) custom-call(bf16[1024,768]{1,0:T(8,128)(2,1)S(1)} %get-tuple-element.120.grad_branch.grad, bf16[1024,768]{1,0:T(8,128)(2,1)S(1)} %get-tuple-element.126.activated, f32[16,768]{1,0:T(8,128)S(1)} %get-tuple-element.127.sums), custom_call_target="tpu_custom_call" | custom-call | tf_op jit(solution)/shard_map/pallas_call | solution.py:862
  69.4 2.0 %shard_map.280 = (f32[384,768]{1,0:T(8,128)S(1)}, bf16[384,768]{1,0:T(8,128)(2,1)S(1)}) custom-call(bf16[1024,768]{1,0:T(8,128)(2,1)S(1)} %get-tuple-element.134.shaped, bf16[1024,768]{1,0:T(8,128)(2,1)S(1)} %get-tuple-element.135.hidden), custom_call_target="tpu_custom_call" | custom-call | tf_op jit(solution)/shard_map/pallas_call | solution.py:862
  74.6 3.1 %shard_map.282.natural = f32[6,1024,128]{2,1,0:T(8,128)S(1)} custom-call(bf16[1024,768]{1,0:T(8,128)(2,1)S(1)} %copy-done), custom_call_target="tpu_custom_call" | custom-call | tf_op jit(solution)/shard_map/pallas_call | solution.py:862
  79.2 8.5 %collective-permute-done.8.far = bf16[512,768]{1,0:T(8,128)(2,1)S(1)} collective-permute-done((bf16[512,768]{1,0:T(8,128)(2,1)S(1)}, bf16[512,768]{1,0:T(8,128)(2,1)S(1)}, u32[]{:S(2)}, u32[]{:S(2)}) %collective-permute-start.8) | collective-permute-done | bytes 786464 | tf_op jit(solution)/shard_map/ppermute | solution.py:879
  87.7 2.8 %shard_map.285 = (f32[512,768]{1,0:T(8,128)S(1)}, bf16[512,768]{1,0:T(8,128)(2,1)S(1)}, f32[8,768]{1,0:T(8,128)S(1)}) custom-call(bf16[512,768]{1,0:T(8,128)(2,1)S(1)} %shard_map.279.chip, bf16[512,768]{1,0:T(8,128)(2,1)S(1)} %collective-permute-done.8.far, f32[512,768]{1,0:T(8,128)S(1)} %get-tuple-element.153.branch, ...), custom_call_target="tpu_custom_call" | custom-call | tf_op jit(solution)/shard_map/pallas_call | solution.py:862
  94.0 8.3 %shard_map.287 = (bf16[1024,768]{1,0:T(8,128)(2,1)S(1)}, bf16[1024,768]{1,0:T(8,128)(2,1)S(1)}, bf16[1024,768]{1,0:T(8,128)(2,1)S(1)}, bf16[1024,768]{1,0:T(8,12...) custom-call(bf16[512,768]{1,0:T(8,128)(2,1)S(1)} %get-tuple-element.155.own, ...), custom_call_target="tpu_custom_call" | custom-call | tf_op jit(solution)/shard_map/pallas_call | solution.py:862
  102.4 2.4 %shard_map.289 = (f32[384,768]{1,0:T(8,128)S(1)}, bf16[384,768]{1,0:T(8,128)(2,1)S(1)}) custom-call(bf16[1024,768]{1,0:T(8,128)(2,1)S(1)} %get-tuple-element.171.mixed, bf16[1024,768]{1,0:T(8,128)(2,1)S(1)} %get-tuple-element.172.grad_branch, bf16[1024,768]{1,0:T(8,128)(2,1)S(1)} %get-tuple-element.173.right), custom_call_target="tpu_custom_call" | custom-call | tf_op jit(solution)/shard_map/pallas_call | solution.py:862
  106.1 2.7 %collective-permute-start.21 = (bf16[208,768]{1,0:T(8,128)(2,1)S(1)}, bf16[208,768]{1,0:T(8,128)(2,1)S(1)}, u32[]{:S(2)}, u32[]{:S(2)}) collective-permute-start(bf16[208,768]{1,0:T(8,128)(2,1)S(1)} %get-tuple-element.179), channel_id=1, source_target_pairs={{0,16},{4,20},{8,24},{12,28},{16,0},{20,4},{24,8},{28,12},{1,17},{... | collective-permute-start | bytes 958472 | tf_op jit(solution)/shard_map/ppermute | solution.py:879
  109.0 3.3 %shard_map.292 = bf16[16,768]{1,0:T(8,128)(2,1)S(1)} custom-call(f32[6,1024,128]{2,1,0:T(8,128)S(1)} %shard_map.282.natural, bf16[1024,768]{1,0:T(8,128)(2,1)S(1)} %get-tuple-element.184.mixed, f32[8,768]{1,0:T(8,128)S(1)} %get-tuple-element.185.mods, bf16[9,768]{1,0:T(8,128)(2,1)S(1)} %copy-done.11, f32[8,768]{1,0:T(8,128)S(1)} %get-tuple-element.186.sums_d, ...), custom_call_target="tpu_custom_call" | custom-call | tf_op jit(solution)/shard_map/pallas_call | solution.py:862
  112.4 5.5 %all-gather = bf16[64,768]{1,0:T(8,128)(2,1)S(1)} all-gather(bf16[16,768]{1,0:T(8,128)(2,1)S(1)} %shard_map.292), channel_id=2, replica_groups=mesh['dp'=8,'tensor'=4] {'tensor'}, dimensions={0}, use_global_device_ids=true | all-gather | bytes 122880 | tf_op jit(solution)/shard_map/all_gather | solution.py:1107
  120.0 3.5 %collective-permute-done.17.refs_1_ = bf16[3,8,768]{2,1,0:T(8,128)(2,1)S(1)} collective-permute-done((bf16[3,8,768]{2,1,0:T(8,128)(2,1)S(1)}, bf16[3,8,768]{2,1,0:T(8,128)(2,1)S(1)}, u32[]{:S(2)}, u32[]{:S(2)}) %collective-permute-start.17) | collective-permute-done | bytes 36896 | tf_op jit(solution)/shard_map/ppermute | solution.py:879
  125.8 7.8 %collective-permute-done.18.refs_1_ = bf16[4,8,768]{2,1,0:T(8,128)(2,1)S(1)} collective-permute-done((bf16[4,8,768]{2,1,0:T(8,128)(2,1)S(1)}, bf16[4,8,768]{2,1,0:T(8,128)(2,1)S(1)}, u32[]{:S(2)}, u32[]{:S(2)}) %collective-permute-start.18) | collective-permute-done | bytes 49184 | tf_op jit(solution)/shard_map/ppermute | solution.py:879
  138.6 4.0 %shard_map.296 = f32[256,768]{1,0:T(8,128)} custom-call(bf16[1024,768]{1,0:T(8,128)(2,1)S(1)} %copy-done, bf16[320,768]{1,0:T(8,128)(2,1)S(1)} %get-tuple-element.181.near, bf16[320,768]{1,0:T(8,128)(2,1)S(1)} %collective-permute-done.16.far, f32[512,768]{1,0:T(8,128)S(1)} %get-tuple-element.189.grad_middle, f32[8,768]{1,0:T(8,128)S(1)} %get-tuple-element.185.mods, ...), custom_call_target="tpu_custom_call" | custom-call | tf_op jit(solution)/shard_map/pallas_call | solution.py:862
  142.6 2.8 %collective-permute-done.19.refs_2_ = bf16[6,8,768]{2,1,0:T(8,128)(2,1)S(1)} collective-permute-done((bf16[6,8,768]{2,1,0:T(8,128)(2,1)S(1)}, bf16[6,8,768]{2,1,0:T(8,128)(2,1)S(1)}, u32[]{:S(2)}, u32[]{:S(2)}) %collective-permute-start.19) | collective-permute-done | bytes 73760 | tf_op jit(solution)/shard_map/ppermute | solution.py:879
  145.4 4.5 %shard_map.299 = (f32[576,768]{1,0:T(8,128)}, f32[4608]{0:T(1024)}, f32[1001,768]{1,0:T(8,128)}, f32[9,768]{1,0:T(8,128)}, f32[768]{0:T(1024)}) custom-call(s32[8]{0:T(128)S(1)} %pad_add_fusion.2.refs_0_, bf16[6,8,768]{2,1,0:T(8,128)(2,1)S(1)} %shard_map.295.refs_1_, bf16[6,8,768]{2,1,0:T(8,128)(2,1)S(1)} %collective-permute-done.19.refs_2_, ...), custom_call_target="tpu_custom_call" | custom-call | tf_op jit(solution)/shard_map/pallas_call | solution.py:862
  (100 shorter events, 32.9 us)
Async XLA Ops:
  19.0 2.5 %collective-permute-start = (bf16[512,768]{1,0:T(8,128)(2,1)S(1)}, bf16[512,768]{1,0:T(8,128)(2,1)S(1)}, u32[]{:S(2)}, u32[]{:S(2)}) collective-permute-start(bf16[512,768]{1,0:T(8,128)(2,1)S(1)} %get-tuple-element.116), channel_id=1, source_target_pairs={{0,1},{1,0},{2,3},{3,2},{4,5},{5,4},{6,7},{7,6},{8,9},{9,8},{10,11... | collective-permute-start | bytes 2359304 | tf_op jit(solution)/shard_map/ppermute | solution.py:879
  21.7 22.6 %collective-permute-start.1 = (bf16[512,768]{1,0:T(8,128)(2,1)S(1)}, bf16[512,768]{1,0:T(8,128)(2,1)S(1)}, u32[]{:S(2)}, u32[]{:S(2)}) collective-permute-start(bf16[512,768]{1,0:T(8,128)(2,1)S(1)} %shard_map.273.chip), channel_id=1, source_target_pairs={{0,2},{1,3},{2,0},{3,1},{4,6},{5,7},{6,4},{7,5},{8,10},{9,11},{10,... | collective-permute-start | bytes 2359304 | tf_op jit(solution)/shard_map/ppermute | solution.py:879
  25.2 8.7 %collective-permute-start.2 = (s32[1]{0:T(128)}, s32[1]{0:T(128)}, u32[]{:S(2)}, u32[]{:S(2)}) collective-permute-start(s32[1]{0:T(128)} %param.21), channel_id=1, source_target_pairs={{0,4},{4,0},{8,12},{12,8},{16,20},{20,16},{24,28},{28,24},{1,5},{5... | collective-permute-start | bytes 20 | tf_op jit(solution)/shard_map/ppermute | solution.py:879
  34.7 3.5 %collective-permute-start.3 = (s32[2]{0:T(128)S(1)}, s32[2]{0:T(128)S(1)}, u32[]{:S(2)}, u32[]{:S(2)}) collective-permute-start(s32[2]{0:T(128)S(1)} %pad_add_fusion), channel_id=1, source_target_pairs={{0,8},{4,12},{8,0},{12,4},{16,24},{20,28},{24,16},{28,20},{1,9},{5... | collective-permute-start | bytes 32 | tf_op jit(solution)/shard_map/ppermute | solution.py:879
  39.0 4.4 %collective-permute-start.4 = (s32[4]{0:T(128)S(1)}, s32[4]{0:T(128)S(1)}, u32[]{:S(2)}, u32[]{:S(2)}) collective-permute-start(s32[4]{0:T(128)S(1)} %pad_add_fusion.1), channel_id=1, source_target_pairs={{0,16},{4,20},{8,24},{12,28},{16,0},{20,4},{24,8},{28,12},{1,17},{... | collective-permute-start | bytes 56 | tf_op jit(solution)/shard_map/ppermute | solution.py:879
  46.1 2.4 %collective-permute-start.5 = (bf16[512,768]{1,0:T(8,128)(2,1)S(1)}, bf16[512,768]{1,0:T(8,128)(2,1)S(1)}, u32[]{:S(2)}, u32[]{:S(2)}) collective-permute-start(bf16[512,768]{1,0:T(8,128)(2,1)S(1)} %get-tuple-element.124.own), channel_id=1, source_target_pairs={{0,1},{1,0},{2,3},{3,2},{4,5},{5,4},{6,7},{7,6},{8,9},{9,8},{10,11... | collective-permute-start | bytes 2359304 | tf_op jit(solution)/shard_map/ppermute | solution.py:879
  65.2 2.4 %collective-permute-start.6 = (bf16[512,768]{1,0:T(8,128)(2,1)S(1)}, bf16[512,768]{1,0:T(8,128)(2,1)S(1)}, u32[]{:S(2)}, u32[]{:S(2)}) collective-permute-start(bf16[512,768]{1,0:T(8,128)(2,1)S(1)} %get-tuple-element.130), channel_id=1, source_target_pairs={{0,1},{1,0},{2,3},{3,2},{4,5},{5,4},{6,7},{7,6},{8,9},{9,8},{10,11... | collective-permute-start | bytes 2359304 | tf_op jit(solution)/shard_map/ppermute | solution.py:879
  67.7 11.3 %collective-permute-start.7 = (bf16[512,768]{1,0:T(8,128)(2,1)S(1)}, bf16[512,768]{1,0:T(8,128)(2,1)S(1)}, u32[]{:S(2)}, u32[]{:S(2)}) collective-permute-start(bf16[512,768]{1,0:T(8,128)(2,1)S(1)} %get-tuple-element.138.send), channel_id=1, source_target_pairs={{0,1},{1,0},{2,3},{3,2},{4,5},{5,4},{6,7},{7,6},{8,9},{9,8},{10,11... | collective-permute-start | bytes 2359304 | tf_op jit(solution)/shard_map/ppermute | solution.py:879
  68.0 19.7 %collective-permute-start.8 = (bf16[512,768]{1,0:T(8,128)(2,1)S(1)}, bf16[512,768]{1,0:T(8,128)(2,1)S(1)}, u32[]{:S(2)}, u32[]{:S(2)}) collective-permute-start(bf16[512,768]{1,0:T(8,128)(2,1)S(1)} %shard_map.279.chip), channel_id=1, source_target_pairs={{0,2},{1,3},{2,0},{3,1},{4,6},{5,7},{6,4},{7,5},{8,10},{9,11},{10,... | collective-permute-start | bytes 2359304 | tf_op jit(solution)/shard_map/ppermute | solution.py:879
  68.6 19.1 %collective-permute-start.9 = (bf16[400,768]{1,0:T(8,128)(2,1)S(1)}, bf16[400,768]{1,0:T(8,128)(2,1)S(1)}, u32[]{:S(2)}, u32[]{:S(2)}) collective-permute-start(bf16[400,768]{1,0:T(8,128)(2,1)S(1)} %get-tuple-element.128), channel_id=1, source_target_pairs={{0,4},{4,0},{8,12},{12,8},{16,20},{20,16},{24,28},{28,24},{1,5},{5... | collective-permute-start | bytes 1843208 | tf_op jit(solution)/shard_map/ppermute | solution.py:879
  71.5 16.2 %collective-permute-start.10 = (bf16[384,768]{1,0:T(8,128)(2,1)S(1)}, bf16[384,768]{1,0:T(8,128)(2,1)S(1)}, u32[]{:S(2)}, u32[]{:S(2)}) collective-permute-start(bf16[384,768]{1,0:T(8,128)(2,1)S(1)} %get-tuple-element.136), channel_id=1, source_target_pairs={{0,8},{4,12},{8,0},{12,4},{16,24},{20,28},{24,16},{28,20},{1,9},{5... | collective-permute-start | bytes 1769480 | tf_op jit(solution)/shard_map/ppermute | solution.py:879
  90.6 3.4 %collective-permute-start.14 = (bf16[512,768]{1,0:T(8,128)(2,1)S(1)}, bf16[512,768]{1,0:T(8,128)(2,1)S(1)}, u32[]{:S(2)}, u32[]{:S(2)}) collective-permute-start(bf16[512,768]{1,0:T(8,128)(2,1)S(1)} %get-tuple-element.155.own), channel_id=1, source_target_pairs={{0,1},{1,0},{2,3},{3,2},{4,5},{5,4},{6,7},{7,6},{8,9},{9,8},{10,11... | collective-permute-start | bytes 2359304 | tf_op jit(solution)/shard_map/ppermute | solution.py:879
  90.6 11.7 %collective-permute-start.13 = (bf16[256,768]{1,0:T(8,128)(2,1)S(1)}, bf16[256,768]{1,0:T(8,128)(2,1)S(1)}, u32[]{:S(2)}, u32[]{:S(2)}) collective-permute-start(bf16[256,768]{1,0:T(8,128)(2,1)S(1)} %get-tuple-element.161), channel_id=1, source_target_pairs={{0,2},{1,3},{2,0},{3,1},{4,6},{5,7},{6,4},{7,5},{8,10},{9,11},{10,... | collective-permute-start | bytes 1179656 | tf_op jit(solution)/shard_map/ppermute | solution.py:879
  91.5 10.8 %collective-permute-start.11 = (bf16[208,768]{1,0:T(8,128)(2,1)S(1)}, bf16[208,768]{1,0:T(8,128)(2,1)S(1)}, u32[]{:S(2)}, u32[]{:S(2)}) collective-permute-start(bf16[208,768]{1,0:T(8,128)(2,1)S(1)} %get-tuple-element.159), channel_id=1, source_target_pairs={{0,8},{4,12},{8,0},{12,4},{16,24},{20,28},{24,16},{28,20},{1,9},{5... | collective-permute-start | bytes 958472 | tf_op jit(solution)/shard_map/ppermute | solution.py:879
  93.1 9.2 %collective-permute-start.12 = (bf16[192,768]{1,0:T(8,128)(2,1)S(1)}, bf16[192,768]{1,0:T(8,128)(2,1)S(1)}, u32[]{:S(2)}, u32[]{:S(2)}) collective-permute-start(bf16[192,768]{1,0:T(8,128)(2,1)S(1)} %get-tuple-element.160), channel_id=1, source_target_pairs={{0,4},{4,0},{8,12},{12,8},{16,20},{20,16},{24,28},{28,24},{1,5},{5... | collective-permute-start | bytes 884744 | tf_op jit(solution)/shard_map/ppermute | solution.py:879
  102.3 6.5 %collective-permute-start.15 = (bf16[640,768]{1,0:T(8,128)(2,1)S(1)}, bf16[640,768]{1,0:T(8,128)(2,1)S(1)}, u32[]{:S(2)}, u32[]{:S(2)}) collective-permute-start(bf16[640,768]{1,0:T(8,128)(2,1)S(1)} %get-tuple-element.170), channel_id=1, source_target_pairs={{0,1},{1,0},{2,3},{3,2},{4,5},{5,4},{6,7},{7,6},{8,9},{9,8},{10,11... | collective-permute-start | bytes 2949128 | tf_op jit(solution)/shard_map/ppermute | solution.py:879
  104.8 18.8 %collective-permute-start.20 = (bf16[384,768]{1,0:T(8,128)(2,1)S(1)}, bf16[384,768]{1,0:T(8,128)(2,1)S(1)}, u32[]{:S(2)}, u32[]{:S(2)}) collective-permute-start(bf16[384,768]{1,0:T(8,128)(2,1)S(1)} %get-tuple-element.174), channel_id=1, source_target_pairs={{0,4},{4,0},{8,12},{12,8},{16,20},{20,16},{24,28},{28,24},{1,5},{5... | collective-permute-start | bytes 1769480 | tf_op jit(solution)/shard_map/ppermute | solution.py:879
  106.1 17.5 %collective-permute-start.21 = (bf16[208,768]{1,0:T(8,128)(2,1)S(1)}, bf16[208,768]{1,0:T(8,128)(2,1)S(1)}, u32[]{:S(2)}, u32[]{:S(2)}) collective-permute-start(bf16[208,768]{1,0:T(8,128)(2,1)S(1)} %get-tuple-element.179), channel_id=1, source_target_pairs={{0,16},{4,20},{8,24},{12,28},{16,0},{20,4},{24,8},{28,12},{1,17},{... | collective-permute-start | bytes 958472 | tf_op jit(solution)/shard_map/ppermute | solution.py:879
  117.9 20.7 %collective-permute-start.16 = (bf16[320,768]{1,0:T(8,128)(2,1)S(1)}, bf16[320,768]{1,0:T(8,128)(2,1)S(1)}, u32[]{:S(2)}, u32[]{:S(2)}) collective-permute-start(bf16[320,768]{1,0:T(8,128)(2,1)S(1)} %get-tuple-element.187), channel_id=1, source_target_pairs={{0,2},{1,3},{2,0},{3,1},{4,6},{5,7},{6,4},{7,5},{8,10},{9,11},{10,... | collective-permute-start | bytes 1474568 | tf_op jit(solution)/shard_map/ppermute | solution.py:879
  119.5 4.0 %collective-permute-start.17 = (bf16[3,8,768]{2,1,0:T(8,128)(2,1)S(1)}, bf16[3,8,768]{2,1,0:T(8,128)(2,1)S(1)}, u32[]{:S(2)}, u32[]{:S(2)}) collective-permute-start(bf16[3,8,768]{2,1,0:T(8,128)(2,1)S(1)} %shard_map.293.refs_0_), channel_id=1, source_target_pairs={{0,4},{4,0},{8,12},{12,8},{16,20},{20,16},{24,28},{28,24},{1,5},{5... | collective-permute-start | bytes 110600 | tf_op jit(solution)/shard_map/ppermute | solution.py:879
  123.7 9.9 %collective-permute-start.22 = (bf16[192,768]{1,0:T(8,128)(2,1)S(1)}, bf16[192,768]{1,0:T(8,128)(2,1)S(1)}, u32[]{:S(2)}, u32[]{:S(2)}) collective-permute-start(bf16[192,768]{1,0:T(8,128)(2,1)S(1)} %get-tuple-element.195), channel_id=1, source_target_pairs={{0,8},{4,12},{8,0},{12,4},{16,24},{20,28},{24,16},{28,20},{1,9},{5... | collective-permute-start | bytes 884744 | tf_op jit(solution)/shard_map/ppermute | solution.py:879
  124.1 9.5 %collective-permute-start.18 = (bf16[4,8,768]{2,1,0:T(8,128)(2,1)S(1)}, bf16[4,8,768]{2,1,0:T(8,128)(2,1)S(1)}, u32[]{:S(2)}, u32[]{:S(2)}) collective-permute-start(bf16[4,8,768]{2,1,0:T(8,128)(2,1)S(1)} %shard_map.294.refs_0_), channel_id=1, source_target_pairs={{0,8},{4,12},{8,0},{12,4},{16,24},{20,28},{24,16},{28,20},{1,9},{5... | collective-permute-start | bytes 147464 | tf_op jit(solution)/shard_map/ppermute | solution.py:879
  133.7 16.3 %collective-permute-start.23 = (bf16[96,768]{1,0:T(8,128)(2,1)S(1)}, bf16[96,768]{1,0:T(8,128)(2,1)S(1)}, u32[]{:S(2)}, u32[]{:S(2)}) collective-permute-start(bf16[96,768]{1,0:T(8,128)(2,1)S(1)} %get-tuple-element.197), channel_id=1, source_target_pairs={{0,16},{4,20},{8,24},{12,28},{16,0},{20,4},{24,8},{28,12},{1,17},{... | collective-permute-start | bytes 442376 | tf_op jit(solution)/shard_map/ppermute | solution.py:879
  134.8 10.6 %collective-permute-start.19 = (bf16[6,8,768]{2,1,0:T(8,128)(2,1)S(1)}, bf16[6,8,768]{2,1,0:T(8,128)(2,1)S(1)}, u32[]{:S(2)}, u32[]{:S(2)}) collective-permute-start(bf16[6,8,768]{2,1,0:T(8,128)(2,1)S(1)} %shard_map.295.refs_1_), channel_id=1, source_target_pairs={{0,16},{4,20},{8,24},{12,28},{16,0},{20,4},{24,8},{28,12},{1,17},{... | collective-permute-start | bytes 221192 | tf_op jit(solution)/shard_map/ppermute | solution.py:879
  (19 other events, 120.9 us)

commit v5 on v4

--- a/solution.py
+++ b/solution.py
@@ -44,7 +44,7 @@
 
 
 def at(start, size):
-    return pl.ds(pl.multiple_of(start, size), size)
+    return pl.ds(start if isinstance(start, int) else pl.multiple_of(start, size), size)
 
 
 def at16(start, size):
@@ -134,9 +134,9 @@
 
 def kernel_a(
     act, tokens_far, b_mod_far, k_att_far, w_qkv_far, w_out_far, w_mod,
-    mods_out, source, keep, send, mixed_out, q_out, k_out, v_out, att_out, lse_out,
-    grid, natural, temp, kernel, tokens, b_mod, k_att, w_qkv, w_out, weights,
-    mixed, q_all, k_all, v_all, att_all, lse_all, sems, in_sems,
+    mods_out, keep, send, lse_all, mixed_out, q_out, k_out, v_out, att_out,
+    grid, temp, kernel, tokens, b_mod, k_att, w_qkv, w_out, weights,
+    mixed, q_all, k_all, v_all, att_all, sems, in_sems,
 ):
     core, _, _ = here_core()
     fetches = [
@@ -168,13 +168,12 @@
         shaped = normed_of(values)[0] * scale + shift
         for tile in range(TILES):
             cols = slice(tile * 128, tile * 128 + 128)
-            natural[tile, at(i * 64, 64), :] = values[:, cols]
             for r in range(2):
                 rows = pl.ds(pl.multiple_of((2 * i + r + 1) * PITCH + 8, 8), SIDE)
                 grid[tile, rows, :] = shaped[SIDE * r : SIDE * r + SIDE, cols]
         return carry
 
-    lax.fori_loop(0, 16, norm, 0)
+    lax.fori_loop(0, 16, norm, 0, unroll=4)
 
     def conv(tile, carry):
         cols = tile_cols(tile)
@@ -190,18 +189,15 @@
                     mixed[at16((2 * a + b) * SHARE + i * 16, 16), cols] = total.astype(bf16)
             return inner
 
-        lax.fori_loop(0, 16, row, 0)
-        take_half(natural, core, tile, source, cols)
+        lax.fori_loop(0, 16, row, 0, unroll=2)
         return carry
 
     lax.fori_loop(0, TILES, conv, 0)
     for fetch in fetches[4:]:
         fetch.wait()
     masks = head_masks()
-    lane = lax.broadcasted_iota(jnp.int32, (SHARE, 128), 1)
     pairs = (
-        (mixed, mixed_out), (q_all, q_out), (k_all, k_out),
-        (v_all, v_out), (att_all, att_out), (lse_all, lse_out),
+        (mixed, mixed_out), (q_all, q_out), (k_all, k_out), (v_all, v_out), (att_all, att_out),
     )
 
     def copies(g):
@@ -219,25 +215,24 @@
         k_all[rows, :] = keys
         v_all[rows, :] = vals
         attended = jnp.zeros((SHARE, HEAD_WIDTH), f32)
-        lse = jnp.zeros((SHARE, 128), f32)
         for h in range(HEADS_HERE):
-            scores = dot_nt(jnp.where(masks[h], query, jnp.zeros_like(query)), keys) * score_scale
-            top = jnp.max(scores, axis=-1, keepdims=True)
+            scores = dot_nt(jnp.where(masks[h], keys, jnp.zeros_like(keys)), query) * score_scale
+            top = jnp.max(scores, axis=0, keepdims=True)
             grown = jnp.exp(scores - top)
-            total = jnp.sum(grown, axis=-1, keepdims=True)
+            total = jnp.sum(grown, axis=0, keepdims=True)
             probs = (grown * (1.0 / total)).astype(bf16)
-            attended = jnp.where(masks[h], dot_nn(probs, vals), attended)
-            lse = jnp.where(lane == h, top + jnp.log(total), lse)
-        lse_all[rows, :] = lse
+            attended = jnp.where(masks[h], dot_tn(probs, vals), attended)
+            lse_all[pl.ds(g, 1), h * SHARE : (h + 1) * SHARE] = top + jnp.log(total)
         attended = attended.astype(bf16)
         att_all[rows, :] = attended
         for copy in copies(g):
             copy.start()
-        temp[...] = dot_nn(attended, w_out[...])
-        split_halves(temp, core, g, keep, send)
-        return carry
-
-    lax.fori_loop(0, 4, attend, 0)
+        temp[g % 2] = dot_nn(attended, w_out[...])
+        split_halves(temp.at[g % 2], core, g, keep, send)
+        return carry
+
+    for g in range(4):
+        attend(g, 0)
 
     def finish(g, carry):
         for copy in copies(g):
@@ -263,7 +258,7 @@
             natural[tile, at(i * 64, 64), :] = values[:, tile * 128 : tile * 128 + 128]
         return carry
 
-    lax.fori_loop(0, 16, spread, 0)
+    lax.fori_loop(0, 16, spread, 0, unroll=2)
     fetch.wait()
     for p, row in zip(range(2, 6), modulation(act[...], weights, b_mod, range(2, 6), 2)):
         mods_out[p : p + 1, :] = row
@@ -278,9 +273,27 @@
                 grad_branch[at16(g * SHARE + i * 16, 16), cols] = (seen * gate).astype(bf16)
             return inner
 
-        lax.fori_loop(0, 16, row, 0)
+        lax.fori_loop(0, 16, row, 0, unroll=2)
         take_half(natural, core, tile, half, cols)
         take_half(natural, 1 - core, tile, other, cols)
+        return carry
+
+    lax.fori_loop(0, TILES, group, 0)
+
+
+def kernel_source(tokens, source, natural):
+    core, _, _ = here_core()
+
+    def spread(i, carry):
+        values = tokens[at(i * 64, 64), :].astype(f32)
+        for tile in range(TILES):
+            natural[tile, at(i * 64, 64), :] = values[:, tile * 128 : tile * 128 + 128]
+        return carry
+
+    lax.fori_loop(0, 16, spread, 0, unroll=2)
+
+    def group(tile, carry):
+        take_half(natural, core, tile, source, tile_cols(tile))
         return carry
 
     lax.fori_loop(0, TILES, group, 0)
@@ -310,12 +323,12 @@
         shaped_out[rows, :] = (normed_of(middle)[0] * scale + shift).astype(bf16)
         return carry
 
-    lax.fori_loop(0, HALF // 64, step, 0)
+    lax.fori_loop(0, HALF // 64, step, 0, unroll=2)
 
 
 def kernel_c(
-    own, other, grad_branch, grad_act, w_up, w_down, b_up, k_ffn,
-    shaped, activated, grad_hidden, sums, b_keep, b_send, g_keep, g_send,
+    class_id, own, other, grad_branch, grad_act, w_up, b_up, k_ffn,
+    shaped, activated, grad_hidden, sums, g_keep, g_send,
     hidden, grad_conv, temp, kernel,
 ):
     core, _, _ = here_core()
@@ -337,7 +350,7 @@
                 hidden[tile, every_other(spot(2 * i + a, b)), :] = values
             return inner
 
-        lax.fori_loop(0, 16, place, 0)
+        lax.fori_loop(0, 16, place, 0, unroll=4)
         return carry
 
     lax.fori_loop(0, 4, up, 0)
@@ -355,16 +368,17 @@
                     for t in range(1, 9):
                         u = u + taps[t] * seen[a + t // 3][b + t % 3]
                     square = u * u
-                    bent = jnp.tanh(gelu_slope * u * (1.0 + gelu_cubic * square))
+                    bent = jnp.tanh(u * (gelu_slope + (gelu_slope * gelu_cubic) * square))
                     part = 0.5 + 0.5 * bent
-                    activated[rows, cols] = (u * part).astype(bf16)
-                    bend = (1.0 - bent * bent) * (1.0 + (3.0 * gelu_cubic) * square)
-                    slope = part + (0.5 * gelu_slope) * u * bend
+                    value = u * part
+                    activated[rows, cols] = value.astype(bf16)
+                    bend = 2.0 * gelu_slope + (6.0 * gelu_slope * gelu_cubic) * square
+                    slope = part + value * ((1.0 - part) * bend)
                     back = grad_act[rows, cols] * slope
                     grad_conv[tile, every_other(spot(2 * i + a, b)), :] = back
             return inner
 
-        lax.fori_loop(0, 16, row, 0)
+        lax.fori_loop(0, 16, row, 0, unroll=2)
         return carry
 
     lax.fori_loop(0, TILES, conv, 0)
@@ -393,7 +407,7 @@
             return tuple(held)
 
         zeros = tuple(jnp.zeros((8, 128), f32) for _ in range(10))
-        held = lax.fori_loop(0, 16, row, zeros)
+        held = lax.fori_loop(0, 16, row, zeros, unroll=2)
         for t in range(10):
             sums[t : t + 1, cols] = column_sum(held[t])
         return carry
@@ -404,12 +418,26 @@
         rows = at(g * SHARE, SHARE)
         temp[...] = dot_nt(grad_hidden[rows, :], w_up[...])
         split_halves(temp, core, g, g_keep, g_send)
-        temp[...] = dot_nt(activated[rows, :], w_down[...])
+        return total + column_sum(grad_branch[rows, :].astype(f32))
+
+    sums[10:11, :] = lax.fori_loop(0, 4, out, jnp.zeros((1, WIDTH), f32), unroll=True)
+    lane = lax.broadcasted_iota(jnp.int32, (1, WIDTH), 1)
+    mine = lane == lax.axis_index("dp")
+    high = lax.div(class_id[0], 32)
+    for row, digit in ((11, high), (12, class_id[0] - 32 * high)):
+        sums[row : row + 1, :] = jnp.where(mine, digit.astype(f32), 0.0)
+    sums[13:16, :] = jnp.zeros((3, WIDTH), f32)
+
+
+def kernel_branch(activated, w_down, b_keep, b_send, temp):
+    core, _, _ = here_core()
+
+    def out(g, carry):
+        temp[...] = dot_nt(activated[at(g * SHARE, SHARE), :], w_down[...])
         split_halves(temp, core, g, b_keep, b_send)
-        return total + column_sum(grad_branch[rows, :].astype(f32))
-
-    sums[10:11, :] = lax.fori_loop(0, 4, out, jnp.zeros((1, WIDTH), f32))
-    sums[11:16, :] = jnp.zeros((5, WIDTH), f32)
+        return carry
+
+    lax.fori_loop(0, 4, out, 0, unroll=True)
 
 
 def kernel_d(chip, far, branch, middle, half, mods, grad_middle, grad_attn, sums):
@@ -428,7 +456,7 @@
         return tuple(h + column_sum(t) for h, t in zip(held, terms))
 
     zeros = tuple(jnp.zeros((1, WIDTH), f32) for _ in range(4))
-    held = lax.fori_loop(0, HALF // 64, step, zeros)
+    held = lax.fori_loop(0, HALF // 64, step, zeros, unroll=2)
     for t in range(4):
         sums[t : t + 1, :] = held[t]
 
@@ -460,8 +488,9 @@
         query = q_all[rows, :]
         keys = k_all[rows, :]
         for h in range(HEADS_HERE):
-            scores = dot_nt(jnp.where(masks[h], query, jnp.zeros_like(query)), keys) * score_scale
-            probs_all[HEADS_HERE * g + h] = jnp.exp(scores - lse_all[rows, h : h + 1])
+            scores = dot_nt(jnp.where(masks[h], keys, jnp.zeros_like(keys)), query) * score_scale
+            lse = lse_all[pl.ds(g, 1), h * SHARE : (h + 1) * SHARE]
+            probs_all[HEADS_HERE * g + h] = jnp.exp(scores - lse)
         return carry
 
     lax.fori_loop(0, 4, step, 0)
@@ -493,12 +522,12 @@
         g_vals = g_query
         for h in range(HEADS_HERE):
             probs = probs_all[HEADS_HERE * g + h]
-            g_probs = dot_nt(jnp.where(masks[h], grad, zero), vals)
-            spread = jnp.sum(probs * g_probs, axis=-1, keepdims=True)
+            g_probs = dot_nt(jnp.where(masks[h], vals, zero), grad)
+            spread = jnp.sum(probs * g_probs, axis=0, keepdims=True)
             g_scores = (probs * (g_probs - spread)).astype(bf16)
-            g_query = jnp.where(masks[h], dot_nn(g_scores, keys), g_query)
-            g_keys = jnp.where(masks[h], dot_tn(g_scores, query), g_keys)
-            g_vals = jnp.where(masks[h], dot_tn(probs.astype(bf16), grad), g_vals)
+            g_query = jnp.where(masks[h], dot_tn(g_scores, keys), g_query)
+            g_keys = jnp.where(masks[h], dot_nn(g_scores, query), g_keys)
+            g_vals = jnp.where(masks[h], dot_nn(probs.astype(bf16), grad), g_vals)
         g_query = (g_query * score_scale).astype(bf16)
         g_keys = (g_keys * score_scale).astype(bf16)
         g_vals = g_vals.astype(bf16)
@@ -509,7 +538,8 @@
         mixed[rows, :] = low
         return carry
 
-    lax.fori_loop(0, 4, attend, 0)
+    for g in range(4):
+        attend(g, 0)
     for out, h in ((keep, core), (send, 1 - core)):
         for x in range(2):
             share = 2 * x + h
@@ -532,7 +562,7 @@
             natural[tile, at(i * 64, 64), :] = normed[:, tile * 128 : tile * 128 + 128]
         return carry
 
-    lax.fori_loop(0, 16, step, 0)
+    lax.fori_loop(0, 16, step, 0, unroll=2)
 
 
 def kernel_q(keep, send, own, other, b_down, sums):
@@ -562,7 +592,7 @@
                 grid[tile, place, :] = values[:, tile * 128 : tile * 128 + 128]
         return carry
 
-    lax.fori_loop(0, 16, norm, 0)
+    lax.fori_loop(0, 16, norm, 0, unroll=4)
 
     def gather(tile, carry):
         cols = tile_cols(tile)
@@ -582,7 +612,7 @@
             return tuple(held)
 
         zeros = tuple(jnp.zeros((8, 128), f32) for _ in range(10))
-        held = [column_sum(h) for h in lax.fori_loop(0, 16, row, zeros)]
+        held = [column_sum(h) for h in lax.fori_loop(0, 16, row, zeros, unroll=2)]
         edge_row = [
             column_sum(grid[tile, pl.ds(spot(r, 0), SIDE), :]) if r is not None else 0.0
             for r in (0, None, SIDE - 1)
@@ -661,7 +691,7 @@
                     grad_shaped[tile, every_other((2 * i + a) * SIDE + b), :] = total
             return inner
 
-        lax.fori_loop(0, 4, row, 0)
+        lax.fori_loop(0, 4, row, 0, unroll=2)
         return carry
 
     lax.fori_loop(0, TILES, conv, 0)
@@ -675,7 +705,7 @@
         out[rows, :] = base + norm_back(normed, size, grad * scale)
         return carry
 
-    lax.fori_loop(0, SHARE // SIDE, finish, 0)
+    lax.fori_loop(0, SHARE // SIDE, finish, 0, unroll=2)
 
 
 def bit_here(bit):
@@ -735,7 +765,7 @@
     send[2 * BLOCK :, :] = tail
 
 
-def kernel_w_end(held, came, down, up, k_out, b_up, b_down):
+def kernel_w_end(held, came, down, up, k_out, b_up, b_down, ids):
     total = summed(held, came)
     down[...] = total(slice(0, BLOCK))
     up[...] = total(slice(BLOCK, 2 * BLOCK))
@@ -743,6 +773,7 @@
     k_out[...] = tail[0:9, :]
     b_up[...] = tail[9:10, :].reshape(WIDTH)
     b_down[...] = tail[10:11, :].reshape(WIDTH)
+    ids[...] = (32.0 * tail[11:12, 0:128] + tail[12:13, 0:128]).astype(jnp.int32)
 
 
 def kernel_v(mixed, grad_branch, right, keep, send, total):
@@ -828,7 +859,7 @@
 
     def item(i, bias):
         slot = lax.bitwise_xor(here, i)
-        row = pl.ds(ids[slot], 1)
+        row = pl.ds(ids[i], 1)
         class_out[row, :] = class_out[row, :] + grads[pl.ds(slot, 1), :]
         return bias + held[slot]
 
@@ -886,12 +917,6 @@
 def butterfly(values, axis):
     for bit in bits_of(axis):
         values = values + swap(values, axis, bit)
-    return values
-
-
-def gather_xor(values):
-    for bit in bits_of("dp"):
-        values = jnp.concatenate([values, swap(values, "dp", bit)], axis=0)
     return values
 
 
@@ -973,25 +998,27 @@
     w_three = jnp.transpose(w_qkv, (1, 2, 0))
     w_back = w_out.T
 
-    mods_a, source, keep, send, mixed, query, keys, vals, attended, lse = call(
+    mods_a, keep, send, lse, mixed, query, keys, vals, attended = call(
         kernel_a, [], [act], [tokens, b_mod, k_att, w_three, w_back, w_mod],
         [
-            vmem((8, WIDTH), f32), vmem(half, f32), vmem(half, bf16), vmem(half, bf16),
+            vmem((8, WIDTH), f32), vmem(half, bf16), vmem(half, bf16),
+            vmem((8, HEADS_HERE * SHARE), f32),
             hbm(full, bf16), hbm(head, bf16), hbm(head, bf16), hbm(head, bf16), hbm(head, bf16),
-            hbm((ITEM, 128), f32),
         ],
         [
-            grid, natural, temp, taps, pltpu.VMEM(full, bf16), pltpu.VMEM(b_mod.shape, bf16),
+            grid, pltpu.VMEM((2, SHARE, WIDTH), f32), taps, pltpu.VMEM(full, bf16),
+            pltpu.VMEM(b_mod.shape, bf16),
             pltpu.VMEM(k_att.shape, bf16), pltpu.VMEM(w_three.shape, bf16),
             pltpu.VMEM(w_back.shape, bf16), pltpu.VMEM((2 * WIDTH, WIDTH), bf16), pltpu.VMEM(full, bf16),
             pltpu.VMEM(head, bf16), pltpu.VMEM(head, bf16), pltpu.VMEM(head, bf16),
-            pltpu.VMEM(head, bf16), pltpu.VMEM((ITEM, 128), f32), sem((6, 4)), sem((6,)),
+            pltpu.VMEM(head, bf16), sem((5, 4)), sem((6,)),
         ],
-        24, 3 * 10**9, 10**7,
+        21, 3 * 10**9, 10**7,
     )
     chip = join(keep, swap(send, "tensor", 1))
     far = swap(chip, "tensor", 2)
-    _, cotangent, class_id = together(chip, cotangent, class_id)
+    _, cotangent, tokens_b = together(chip, cotangent, tokens)
+    (source,) = call(kernel_source, [], [tokens_b], [], [vmem(half, f32)], [natural], 6, 0, 0)
     mods_p, grad_ffn, cot_half, cot_other = call(
         kernel_p, [item_count], [cotangent, act, b_mod], [w_mod],
         [vmem((8, WIDTH), f32), vmem(full, bf16), vmem(half, bf16), vmem(half, bf16)],
@@ -1000,17 +1027,16 @@
     (grad_act,) = call(
         kernel_ga, [], [grad_ffn, w_down], [], [vmem(full, f32)], [], 6, 12 * 10**8, 6 * 10**6
     )
-    ids = gather_xor(class_id)
-    far, mods_p, ids, _ = together(far, mods_p, ids, grad_act)
+    far, mods_p, source, _ = together(far, mods_p, source, grad_act)
     branch, middle, shaped_own = call(
         kernel_b, [], [chip, far, source, mods_p, b_out], [],
         [vmem(half, f32), vmem(half, f32), vmem(half, bf16)], [], 6, 10**7, 7 * 10**6,
     )
     shaped_other = swap(shaped_own, "tensor", 1)
 
-    shaped, activated, grad_hidden, sums_c, b_keep, b_send, g_keep, g_send = call(
-        kernel_c, [], [shaped_own, shaped_other, grad_ffn, grad_act, w_up, w_down, b_up, k_ffn], [],
-        [vmem(full, bf16)] * 3 + [vmem((16, WIDTH), f32)] + [vmem(half, bf16)] * 4,
+    shaped, activated, grad_hidden, sums_c, g_keep, g_send = call(
+        kernel_c, [class_id], [shaped_own, shaped_other, grad_ffn, grad_act, w_up, b_up, k_ffn], [],
+        [vmem(full, bf16)] * 3 + [vmem((16, WIDTH), f32)] + [vmem(half, bf16)] * 2,
         [grid, grid, temp, taps], 13, 5 * 10**9, 12 * 10**6,
     )
     g_came = swap(g_send, "tensor", 1)
@@ -1024,8 +1050,7 @@
         g_came, _ = together(g_came, d_send)
     chip = join(g_keep, g_came)
     far = swap(chip, "tensor", 2)
-    _, shaped, b_send = together(chip, shaped, b_send)
-    b_came = swap(b_send, "tensor", 1)
+    _, shaped = together(chip, shaped)
     if eight:
         u_keep, u_send = call(
             kernel_w_up, [], [shaped, grad_hidden], [],
@@ -1034,13 +1059,16 @@
         )
         d_came = swap(d_send, "dp", 1)
         u_came = swap(u_send, "dp", 2)
-        tokens_n, b_keep, _, _ = together(tokens, b_keep, d_send, u_send)
+        tokens_n, activated, _, _ = together(tokens, activated, d_send, u_send)
     else:
         ffn_grads = scatter_plain(
             jnp.stack([dot_tn(grad_ffn, activated), dot_tn(shaped, grad_hidden)])
         )
         early = butterfly(sums_c, "dp")
         tokens_n = tokens
+    b_keep, b_send = call(
+        kernel_branch, [], [activated, w_down], [], [vmem(half, bf16)] * 2, [temp], 6, 0, 0
+    )
     (normed,) = call(
         kernel_n, [], [tokens_n], [], [vmem((TILES, ITEM, 128), f32)], [], 4, 10**7, 5 * 10**6
     )
@@ -1053,9 +1081,7 @@
         kernel_p_again, [], [query, keys, lse], [], [vmem((12, SHARE, SHARE), f32)], [],
         6, 10**8, 4 * 10**6,
     )
-    b_own, b_part = join_split(b_keep, b_came)
-    far, b_part, _, _ = together(far, b_part, normed, probs)
-    b_far = swap(b_part, "tensor", 2)
+    far, b_send, _, _ = together(far, b_send, normed, probs)
     if eight:
         far, d_came, u_came = together(far, d_came, u_came)
     grad_middle, attn_own, sums_d = call(
@@ -1079,8 +1105,10 @@
         [pltpu.VMEM((4, 288, WIDTH), bf16), sem], 8, 3 * 10**9, 10**7,
     )
     if eight:
-        d_came, u_came, b_far, right, h_send = together(d_came, u_came, b_far, right, h_send)
+        d_came, u_came, b_send, right, h_send = together(d_came, u_came, b_send, right, h_send)
     h_came = swap(h_send, "tensor", 1)
+    b_came = swap(b_send, "tensor", 1)
+    h_came, b_came = together(h_came, b_came)
     w_mod_late, _ = together(w_mod, mixed_grad)
     if eight:
         ffn_keep, ffn_send = weight_step(
@@ -1110,6 +1138,9 @@
     )
     part, _ = together(part, held)
     part_far = swap(part, "tensor", 2)
+    b_own, b_part = join_split(b_keep, b_came)
+    if not eight:
+        b_far = swap(b_part, "tensor", 2)
     for step, bit in enumerate(bits):
         came = swap(held, "dp", bit)
         if step == len(bits) - 1:
@@ -1127,6 +1158,8 @@
             came, _, _ = together(came, grad_tokens, block_out)
             break
         slots = 1 << step
+        if eight and step == 1:
+            came, part_far = together(came, part_far)
 
         def kernel(*refs, slots=slots):
             kernel_gather(slots, *refs)
@@ -1135,7 +1168,8 @@
             kernel, [], [held, came], [], [vmem((2 * slots + 2, 8, WIDTH), bf16)], [], 4, 10**5, 10**5
         )
         if eight and step == 0:
-            a_came, ffn_came, _ = together(a_came, ffn_came, held)
+            a_came, ffn_came, b_part, _ = together(a_came, ffn_came, b_part, held)
+            b_far = swap(b_part, "tensor", 2)
             a_keep, a_send = weight_step(kernel_v_one, [(2 * BLOCK, WIDTH)], a_keep, a_came)
             a_came = swap(a_send, "dp", 2)
     if eight:
@@ -1144,6 +1178,17 @@
         a_came = swap(a_send, "dp", 4)
         came, _ = together(came, a_send)
 
+    if eight:
+        rows = plain((BLOCK, WIDTH), f32)
+        flat = plain((WIDTH,), f32)
+        grad_down, grad_up, grad_k_ffn, grad_b_up, grad_b_down, ids = call(
+            kernel_w_end, [], [ffn_keep, ffn_came], [],
+            [rows, rows, plain((9, WIDTH), f32), flat, flat, plain((1, 128), jnp.int32)],
+            [], 4, 10**6, 2 * 10**6,
+        )
+        ids = ids[0, :items]
+    else:
+        ids = (32.0 * early[11, :items] + early[12, :items]).astype(jnp.int32)
     share = w_mod.shape[0] // items
 
     def kernel(*refs):
@@ -1163,12 +1208,6 @@
     )
 
     if eight:
-        rows = plain((BLOCK, WIDTH), f32)
-        flat = plain((WIDTH,), f32)
-        grad_down, grad_up, grad_k_ffn, grad_b_up, grad_b_down = call(
-            kernel_w_end, [], [ffn_keep, ffn_came], [],
-            [rows, rows, plain((9, WIDTH), f32), flat, flat], [], 4, 10**6, 2 * 10**6,
-        )
         a_came, _, _ = together(a_came, grad_b_mod, grad_b_up)
         grad_qkv, grad_out = call(
             kernel_v_end, [], [a_keep, a_came], [],

time: 151 us -> 139 us (0.921)
  Pallas kernels: 80.4 us -> 69.8 us
  waiting for transfers between devices: 30.9 us -> 34.1 us
  starting transfers between devices: 27.2 us -> 24.3 us
  other arithmetic: 3.11 us -> 0.82 us
    pallas_call x30 -> x32, Pallas kernels: 80.4 us -> 69.8 us  [call(): pl.pallas_call(kernel, out_shape=tuple(outs), in_specs=spots, out_specs=t...]
    ppermute x24 -> x21, waiting for transfers between devices: 30.9 us -> 34.1 us  [swap(): return lax.ppermute(values, axis, [(i, i ^ bit) for i in range(size)])]
    ppermute x24 -> x21, starting transfers between devices: 27.2 us -> 24.3 us  [swap(): return lax.ppermute(values, axis, [(i, i ^ bit) for i in range(size)])]
    concatenate x3 -> x0, other arithmetic: 2.29 us -> none  [gather_xor(): values = jnp.concatenate([values, swap(values, 'dp', bit)], axis=0)]
  transfers between devices with their start and end apart: 24 -> 21, of which waited for: 10 -> 10; matrix products, arithmetic and copies ran while one was open for 2% -> 0% of each run, Pallas kernels for 28% -> 29%
where the time goes in v5:
time: 139 us
  Pallas kernels  69.8 us (50%)
  waiting for transfers between devices  34.1 us (25%)
  starting transfers between devices  24.3 us (17%)
  blocking collectives  5.56 us (4%)
  between operations  2.98 us (2%)
    pallas_call x32, Pallas kernels, call(): pl.pallas_call(kernel, out_shape=tuple(outs), in_specs=spots, out_specs=t...  69.8 us
    ppermute x21, waiting for transfers between devices, swap(): return lax.ppermute(values, axis, [(i, i ^ bit) for i in range(size)])  34.1 us
    ppermute x21, starting transfers between devices, swap(): return lax.ppermute(values, axis, [(i, i ^ bit) for i in range(size)])  24.3 us
    all_gather x1, blocking collectives, shards(): late = lax.all_gather(late, 'tensor')  5.56 us
  transfers between devices with their start and end apart: 21, of which 10 were waited for; matrix products, arithmetic and copies ran while one was open for 0% of the time, Pallas kernels for 29%

profile of v5, /device:TPU:0, one launch (start us, length us, event | category | flops | bytes accessed | tf_op | source)
XLA Modules:
  0.0 138.7 jit_solution(16039743944063885387)
XLA Ops:
  2.8 12.9 %shard_map.272 = (f32[8,768]{1,0:T(8,128)S(1)}, bf16[512,768]{1,0:T(8,128)(2,1)S(1)}, bf16[512,768]{1,0:T(8,128)(2,1)S(1)}, f32[8,768]{1,0:T(8,128)S(1)}, bf16[1...) custom-call(bf16[16,768]{1,0:T(8,128)(2,1)S(1)} %broadcast_in_dim.10, ...), custom_call_target="tpu_custom_call" | custom-call | tf_op jit(solution)/shard_map/pallas_call | solution.py:893
  16.2 1.9 %collective-permute-done.came = bf16[512,768]{1,0:T(8,128)(2,1)S(1)} collective-permute-done((bf16[512,768]{1,0:T(8,128)(2,1)S(1)}, bf16[512,768]{1,0:T(8,128)(2,1)S(1)}, u32[]{:S(2)}, u32[]{:S(2)}) %collective-permute-start) | collective-permute-done | bytes 786464 | tf_op jit(solution)/shard_map/ppermute | solution.py:910
  18.3 2.9 %collective-permute-start.1 = (bf16[512,768]{1,0:T(8,128)(2,1)S(1)}, bf16[512,768]{1,0:T(8,128)(2,1)S(1)}, u32[]{:S(2)}, u32[]{:S(2)}) collective-permute-start(bf16[512,768]{1,0:T(8,128)(2,1)S(1)} %shard_map.273.chip), channel_id=1, source_target_pairs={{0,2},{1,3},{2,0},{3,1},{4,6},{5,7},{6,4},{7,5},{8,10},{9,11},{10,... | collective-permute-start | bytes 2359304 | tf_op jit(solution)/shard_map/ppermute | solution.py:910
  23.3 5.0 %shard_map.274 = (f32[8,768]{1,0:T(8,128)S(1)}, bf16[1024,768]{1,0:T(8,128)(2,1)S(1)}, bf16[512,768]{1,0:T(8,128)(2,1)S(1)}, bf16[512,768]{1,0:T(8,128)(2,1)S(1)}) custom-call(s32[1]{0:T(128)S(6)} %copy.31.count, bf16[1024,768]{1,0:T(8,128)(2,1)S(1)} %copy-done.5, bf16[16,768]{1,0:T(8,128)(2,1)S(1)} %broadcast_in_dim.10.act, bf16[4608]{0:T(1024)(128)(2,1)S(1)} %copy-done.11, ...), custom_call_target="tpu_custom_call" | custom-call | tf_op jit(solution)/shard_map/pallas_call | solution.py:893
  28.3 1.9 %shard_map.276.grad_act = f32[1024,768]{1,0:T(8,128)S(1)} custom-call(bf16[1024,768]{1,0:T(8,128)(2,1)S(1)} %get-tuple-element.124.grad_branch.grad, bf16[768,768]{1,0:T(8,128)(2,1)S(1)} %copy-done.1), custom_call_target="tpu_custom_call" | custom-call | tf_op jit(solution)/shard_map/pallas_call | solution.py:893
  30.2 8.8 %collective-permute-done.1.far = bf16[512,768]{1,0:T(8,128)(2,1)S(1)} collective-permute-done((bf16[512,768]{1,0:T(8,128)(2,1)S(1)}, bf16[512,768]{1,0:T(8,128)(2,1)S(1)}, u32[]{:S(2)}, u32[]{:S(2)}) %collective-permute-start.1) | collective-permute-done | bytes 786464 | tf_op jit(solution)/shard_map/ppermute | solution.py:910
  40.2 2.3 %collective-permute-done.2.other = bf16[512,768]{1,0:T(8,128)(2,1)S(1)} collective-permute-done((bf16[512,768]{1,0:T(8,128)(2,1)S(1)}, bf16[512,768]{1,0:T(8,128)(2,1)S(1)}, u32[]{:S(2)}, u32[]{:S(2)}) %collective-permute-start.2) | collective-permute-done | bytes 786464 | tf_op jit(solution)/shard_map/ppermute | solution.py:910
  42.5 13.1 %shard_map.278 = (bf16[1024,768]{1,0:T(8,128)(2,1)S(1)}, bf16[1024,768]{1,0:T(8,128)(2,1)S(1)}, bf16[1024,768]{1,0:T(8,128)(2,1)S(1)}, f32[16,768]{1,0:T(8,128)S...) custom-call(s32[1]{0:T(128)} %copy.33.class_id, bf16[512,768]{1,0:T(8,128)(2,1)S(1)} %get-tuple-element.128.own, ...), custom_call_target="tpu_custom_call" | custom-call | tf_op jit(solution)/shard_map/pallas_call | solution.py:893
  55.8 2.0 %shard_map.279 = (f32[400,768]{1,0:T(8,128)S(1)}, bf16[400,768]{1,0:T(8,128)(2,1)S(1)}) custom-call(bf16[1024,768]{1,0:T(8,128)(2,1)S(1)} %get-tuple-element.124.grad_branch.grad, bf16[1024,768]{1,0:T(8,128)(2,1)S(1)} %get-tuple-element.139.activated, f32[16,768]{1,0:T(8,128)S(1)} %get-tuple-element.130.sums), custom_call_target="tpu_custom_call" | custom-call | tf_op jit(solution)/shard_map/pallas_call | solution.py:893
  61.5 2.2 %shard_map.281 = (f32[384,768]{1,0:T(8,128)S(1)}, bf16[384,768]{1,0:T(8,128)(2,1)S(1)}) custom-call(bf16[1024,768]{1,0:T(8,128)(2,1)S(1)} %get-tuple-element.136.shaped, bf16[1024,768]{1,0:T(8,128)(2,1)S(1)} %get-tuple-element.137.hidden), custom_call_target="tpu_custom_call" | custom-call | tf_op jit(solution)/shard_map/pallas_call | solution.py:893
  67.9 1.8 %shard_map.283.natural = f32[6,1024,128]{2,1,0:T(8,128)S(1)} custom-call(bf16[1024,768]{1,0:T(8,128)(2,1)S(1)} %copy-done), custom_call_target="tpu_custom_call" | custom-call | tf_op jit(solution)/shard_map/pallas_call | solution.py:893
  71.0 6.9 %collective-permute-done.4.far = bf16[512,768]{1,0:T(8,128)(2,1)S(1)} collective-permute-done((bf16[512,768]{1,0:T(8,128)(2,1)S(1)}, bf16[512,768]{1,0:T(8,128)(2,1)S(1)}, u32[]{:S(2)}, u32[]{:S(2)}) %collective-permute-start.4) | collective-permute-done | bytes 786464 | tf_op jit(solution)/shard_map/ppermute | solution.py:910
  78.7 2.0 %shard_map.286 = (f32[512,768]{1,0:T(8,128)S(1)}, bf16[512,768]{1,0:T(8,128)(2,1)S(1)}, f32[8,768]{1,0:T(8,128)S(1)}) custom-call(bf16[512,768]{1,0:T(8,128)(2,1)S(1)} %shard_map.280.chip, bf16[512,768]{1,0:T(8,128)(2,1)S(1)} %collective-permute-done.4.far, f32[512,768]{1,0:T(8,128)S(1)} %get-tuple-element.154.branch, ...), custom_call_target="tpu_custom_call" | custom-call | tf_op jit(solution)/shard_map/pallas_call | solution.py:893
  83.8 6.7 %shard_map.288 = (bf16[1024,768]{1,0:T(8,128)(2,1)S(1)}, bf16[1024,768]{1,0:T(8,128)(2,1)S(1)}, bf16[1024,768]{1,0:T(8,128)(2,1)S(1)}, bf16[1024,768]{1,0:T(8,12...) custom-call(bf16[512,768]{1,0:T(8,128)(2,1)S(1)} %get-tuple-element.156.own, ...), custom_call_target="tpu_custom_call" | custom-call | tf_op jit(solution)/shard_map/pallas_call | solution.py:893
  92.4 2.4 %shard_map.290 = (f32[384,768]{1,0:T(8,128)S(1)}, bf16[384,768]{1,0:T(8,128)(2,1)S(1)}) custom-call(bf16[1024,768]{1,0:T(8,128)(2,1)S(1)} %get-tuple-element.173.mixed, bf16[1024,768]{1,0:T(8,128)(2,1)S(1)} %get-tuple-element.174.grad_branch, bf16[1024,768]{1,0:T(8,128)(2,1)S(1)} %get-tuple-element.175.right), custom_call_target="tpu_custom_call" | custom-call | tf_op jit(solution)/shard_map/pallas_call | solution.py:893
  96.0 2.7 %collective-permute-start.13 = (bf16[208,768]{1,0:T(8,128)(2,1)S(1)}, bf16[208,768]{1,0:T(8,128)(2,1)S(1)}, u32[]{:S(2)}, u32[]{:S(2)}) collective-permute-start(bf16[208,768]{1,0:T(8,128)(2,1)S(1)} %get-tuple-element.181), channel_id=1, source_target_pairs={{0,16},{4,20},{8,24},{12,28},{16,0},{20,4},{24,8},{28,12},{1,17},{... | collective-permute-start | bytes 958472 | tf_op jit(solution)/shard_map/ppermute | solution.py:910
  98.9 2.9 %shard_map.293 = bf16[16,768]{1,0:T(8,128)(2,1)S(1)} custom-call(f32[6,1024,128]{2,1,0:T(8,128)S(1)} %shard_map.283.natural, bf16[1024,768]{1,0:T(8,128)(2,1)S(1)} %get-tuple-element.188.mixed, f32[8,768]{1,0:T(8,128)S(1)} %get-tuple-element.189.mods, bf16[9,768]{1,0:T(8,128)(2,1)S(1)} %copy-done.10, f32[8,768]{1,0:T(8,128)S(1)} %get-tuple-element.190.sums_d, ...), custom_call_target="tpu_custom_call" | custom-call | tf_op jit(solution)/shard_map/pallas_call | solution.py:893
  101.8 5.6 %all-gather = bf16[64,768]{1,0:T(8,128)(2,1)S(1)} all-gather(bf16[16,768]{1,0:T(8,128)(2,1)S(1)} %shard_map.293), channel_id=2, replica_groups=mesh['dp'=8,'tensor'=4] {'tensor'}, dimensions={0}, use_global_device_ids=true | all-gather | bytes 122880 | tf_op jit(solution)/shard_map/all_gather | solution.py:1135
  109.7 3.3 %collective-permute-done.14.refs_1_ = bf16[3,8,768]{2,1,0:T(8,128)(2,1)S(1)} collective-permute-done((bf16[3,8,768]{2,1,0:T(8,128)(2,1)S(1)}, bf16[3,8,768]{2,1,0:T(8,128)(2,1)S(1)}, u32[]{:S(2)}, u32[]{:S(2)}) %collective-permute-start.14) | collective-permute-done | bytes 36896 | tf_op jit(solution)/shard_map/ppermute | solution.py:910
  114.7 1.9 %collective-permute-start.16 = (bf16[4,8,768]{2,1,0:T(8,128)(2,1)S(1)}, bf16[4,8,768]{2,1,0:T(8,128)(2,1)S(1)}, u32[]{:S(2)}, u32[]{:S(2)}) collective-permute-start(bf16[4,8,768]{2,1,0:T(8,128)(2,1)S(1)} %shard_map.295.refs_0_), channel_id=1, source_target_pairs={{0,8},{4,12},{8,0},{12,4},{16,24},{20,28},{24,16},{28,20},{1,9},{5... | collective-permute-start | bytes 147464 | tf_op jit(solution)/shard_map/ppermute | solution.py:910
  117.5 5.3 %collective-permute-done.16.refs_1_ = bf16[4,8,768]{2,1,0:T(8,128)(2,1)S(1)} collective-permute-done((bf16[4,8,768]{2,1,0:T(8,128)(2,1)S(1)}, bf16[4,8,768]{2,1,0:T(8,128)(2,1)S(1)}, u32[]{:S(2)}, u32[]{:S(2)}) %collective-permute-start.16) | collective-permute-done | bytes 49184 | tf_op jit(solution)/shard_map/ppermute | solution.py:910
  126.0 3.4 %collective-permute-done.15.far = bf16[256,768]{1,0:T(8,128)(2,1)S(1)} collective-permute-done((bf16[256,768]{1,0:T(8,128)(2,1)S(1)}, bf16[256,768]{1,0:T(8,128)(2,1)S(1)}, u32[]{:S(2)}, u32[]{:S(2)}) %collective-permute-start.15) | collective-permute-done | bytes 393248 | tf_op jit(solution)/shard_map/ppermute | solution.py:910
  130.4 2.9 %shard_map.298 = f32[256,768]{1,0:T(8,128)} custom-call(bf16[1024,768]{1,0:T(8,128)(2,1)S(1)} %copy-done, bf16[320,768]{1,0:T(8,128)(2,1)S(1)} %get-tuple-element.192.near, bf16[320,768]{1,0:T(8,128)(2,1)S(1)} %collective-permute-done.17.far, f32[512,768]{1,0:T(8,128)S(1)} %get-tuple-element.197.grad_middle, f32[8,768]{1,0:T(8,128)S(1)} %get-tuple-element.189.mods, ...), custom_call_target="tpu_custom_call" | custom-call | tf_op jit(solution)/shard_map/pallas_call | solution.py:893
  133.3 4.5 %shard_map.302 = (f32[576,768]{1,0:T(8,128)}, f32[4608]{0:T(1024)}, f32[1001,768]{1,0:T(8,128)}, f32[9,768]{1,0:T(8,128)}, f32[768]{0:T(1024)}) custom-call(s32[8]{0:T(128)S(1)} %slice_bitcast_fusion.refs_0_, bf16[6,8,768]{2,1,0:T(8,128)(2,1)S(1)} %shard_map.297.refs_1_, bf16[6,8,768]{2,1,0:T(8,128)(2,1)S(1)} %collective-permute-done.18.refs_2_, ...), custom_call_target="tpu_custom_call" | custom-call | tf_op jit(solution)/shard_map/pallas_call | solution.py:893
  (92 shorter events, 30.4 us)
Async XLA Ops:
  15.6 6.2 %copy-start = (bf16[1024,768]{1,0:T(8,128)(2,1)S(1)}, bf16[1024,768]{1,0:T(8,128)(2,1)}, u32[]{:S(2)}) copy-start(bf16[1024,768]{1,0:T(8,128)(2,1)} %tokens.3) | copy-start | bytes 4718596
  15.6 2.4 %collective-permute-start = (bf16[512,768]{1,0:T(8,128)(2,1)S(1)}, bf16[512,768]{1,0:T(8,128)(2,1)S(1)}, u32[]{:S(2)}, u32[]{:S(2)}) collective-permute-start(bf16[512,768]{1,0:T(8,128)(2,1)S(1)} %get-tuple-element.120), channel_id=1, source_target_pairs={{0,1},{1,0},{2,3},{3,2},{4,5},{5,4},{6,7},{7,6},{8,9},{9,8},{10,11... | collective-permute-start | bytes 2359304 | tf_op jit(solution)/shard_map/ppermute | solution.py:910
  18.3 20.8 %collective-permute-start.1 = (bf16[512,768]{1,0:T(8,128)(2,1)S(1)}, bf16[512,768]{1,0:T(8,128)(2,1)S(1)}, u32[]{:S(2)}, u32[]{:S(2)}) collective-permute-start(bf16[512,768]{1,0:T(8,128)(2,1)S(1)} %shard_map.273.chip), channel_id=1, source_target_pairs={{0,2},{1,3},{2,0},{3,1},{4,6},{5,7},{6,4},{7,5},{8,10},{9,11},{10,... | collective-permute-start | bytes 2359304 | tf_op jit(solution)/shard_map/ppermute | solution.py:910
  28.3 10.8 %copy-start.15 = (bf16[768]{0:T(1024)(128)(2,1)S(1)}, bf16[768]{0:T(1024)(128)(2,1)}, u32[]{:S(2)}) copy-start(bf16[768]{0:T(1024)(128)(2,1)} %b_out.1) | copy-start | bytes 4612
  40.2 2.4 %collective-permute-start.2 = (bf16[512,768]{1,0:T(8,128)(2,1)S(1)}, bf16[512,768]{1,0:T(8,128)(2,1)S(1)}, u32[]{:S(2)}, u32[]{:S(2)}) collective-permute-start(bf16[512,768]{1,0:T(8,128)(2,1)S(1)} %get-tuple-element.128.own), channel_id=1, source_target_pairs={{0,1},{1,0},{2,3},{3,2},{4,5},{5,4},{6,7},{7,6},{8,9},{9,8},{10,11... | collective-permute-start | bytes 2359304 | tf_op jit(solution)/shard_map/ppermute | solution.py:910
  55.6 2.4 %collective-permute-start.3 = (bf16[512,768]{1,0:T(8,128)(2,1)S(1)}, bf16[512,768]{1,0:T(8,128)(2,1)S(1)}, u32[]{:S(2)}, u32[]{:S(2)}) collective-permute-start(bf16[512,768]{1,0:T(8,128)(2,1)S(1)} %get-tuple-element.133), channel_id=1, source_target_pairs={{0,1},{1,0},{2,3},{3,2},{4,5},{5,4},{6,7},{7,6},{8,9},{9,8},{10,11... | collective-permute-start | bytes 2359304 | tf_op jit(solution)/shard_map/ppermute | solution.py:910
  58.1 19.8 %collective-permute-start.4 = (bf16[512,768]{1,0:T(8,128)(2,1)S(1)}, bf16[512,768]{1,0:T(8,128)(2,1)S(1)}, u32[]{:S(2)}, u32[]{:S(2)}) collective-permute-start(bf16[512,768]{1,0:T(8,128)(2,1)S(1)} %shard_map.280.chip), channel_id=1, source_target_pairs={{0,2},{1,3},{2,0},{3,1},{4,6},{5,7},{6,4},{7,5},{8,10},{9,11},{10,... | collective-permute-start | bytes 2359304 | tf_op jit(solution)/shard_map/ppermute | solution.py:910
  59.9 18.0 %collective-permute-start.5 = (bf16[400,768]{1,0:T(8,128)(2,1)S(1)}, bf16[400,768]{1,0:T(8,128)(2,1)S(1)}, u32[]{:S(2)}, u32[]{:S(2)}) collective-permute-start(bf16[400,768]{1,0:T(8,128)(2,1)S(1)} %get-tuple-element.131), channel_id=1, source_target_pairs={{0,4},{4,0},{8,12},{12,8},{16,20},{20,16},{24,28},{28,24},{1,5},{5... | collective-permute-start | bytes 1843208 | tf_op jit(solution)/shard_map/ppermute | solution.py:910
  63.7 15.0 %collective-permute-start.6 = (bf16[384,768]{1,0:T(8,128)(2,1)S(1)}, bf16[384,768]{1,0:T(8,128)(2,1)S(1)}, u32[]{:S(2)}, u32[]{:S(2)}) collective-permute-start(bf16[384,768]{1,0:T(8,128)(2,1)S(1)} %get-tuple-element.138), channel_id=1, source_target_pairs={{0,8},{4,12},{8,0},{12,4},{16,24},{20,28},{24,16},{28,20},{1,9},{5... | collective-permute-start | bytes 1769480 | tf_op jit(solution)/shard_map/ppermute | solution.py:910
  80.7 3.1 %collective-permute-start.9 = (bf16[512,768]{1,0:T(8,128)(2,1)S(1)}, bf16[512,768]{1,0:T(8,128)(2,1)S(1)}, u32[]{:S(2)}, u32[]{:S(2)}) collective-permute-start(bf16[512,768]{1,0:T(8,128)(2,1)S(1)} %get-tuple-element.156.own), channel_id=1, source_target_pairs={{0,1},{1,0},{2,3},{3,2},{4,5},{5,4},{6,7},{7,6},{8,9},{9,8},{10,11... | collective-permute-start | bytes 2359304 | tf_op jit(solution)/shard_map/ppermute | solution.py:910
  81.2 10.7 %collective-permute-start.7 = (bf16[208,768]{1,0:T(8,128)(2,1)S(1)}, bf16[208,768]{1,0:T(8,128)(2,1)S(1)}, u32[]{:S(2)}, u32[]{:S(2)}) collective-permute-start(bf16[208,768]{1,0:T(8,128)(2,1)S(1)} %get-tuple-element.160), channel_id=1, source_target_pairs={{0,8},{4,12},{8,0},{12,4},{16,24},{20,28},{24,16},{28,20},{1,9},{5... | collective-permute-start | bytes 958472 | tf_op jit(solution)/shard_map/ppermute | solution.py:910
  82.8 9.1 %collective-permute-start.8 = (bf16[192,768]{1,0:T(8,128)(2,1)S(1)}, bf16[192,768]{1,0:T(8,128)(2,1)S(1)}, u32[]{:S(2)}, u32[]{:S(2)}) collective-permute-start(bf16[192,768]{1,0:T(8,128)(2,1)S(1)} %get-tuple-element.161), channel_id=1, source_target_pairs={{0,4},{4,0},{8,12},{12,8},{16,20},{20,16},{24,28},{28,24},{1,5},{5... | collective-permute-start | bytes 884744 | tf_op jit(solution)/shard_map/ppermute | solution.py:910
  91.9 6.7 %collective-permute-start.10 = (bf16[640,768]{1,0:T(8,128)(2,1)S(1)}, bf16[640,768]{1,0:T(8,128)(2,1)S(1)}, u32[]{:S(2)}, u32[]{:S(2)}) collective-permute-start(bf16[640,768]{1,0:T(8,128)(2,1)S(1)} %get-tuple-element.169), channel_id=1, source_target_pairs={{0,1},{1,0},{2,3},{3,2},{4,5},{5,4},{6,7},{7,6},{8,9},{9,8},{10,11... | collective-permute-start | bytes 2949128 | tf_op jit(solution)/shard_map/ppermute | solution.py:910
  91.9 6.7 %collective-permute-start.11 = (bf16[512,768]{1,0:T(8,128)(2,1)S(1)}, bf16[512,768]{1,0:T(8,128)(2,1)S(1)}, u32[]{:S(2)}, u32[]{:S(2)}) collective-permute-start(bf16[512,768]{1,0:T(8,128)(2,1)S(1)} %get-tuple-element.170.send), channel_id=1, source_target_pairs={{0,1},{1,0},{2,3},{3,2},{4,5},{5,4},{6,7},{7,6},{8,9},{9,8},{10,11... | collective-permute-start | bytes 2359304 | tf_op jit(solution)/shard_map/ppermute | solution.py:910
  94.8 18.2 %collective-permute-start.12 = (bf16[384,768]{1,0:T(8,128)(2,1)S(1)}, bf16[384,768]{1,0:T(8,128)(2,1)S(1)}, u32[]{:S(2)}, u32[]{:S(2)}) collective-permute-start(bf16[384,768]{1,0:T(8,128)(2,1)S(1)} %get-tuple-element.176), channel_id=1, source_target_pairs={{0,4},{4,0},{8,12},{12,8},{16,20},{20,16},{24,28},{28,24},{1,5},{5... | collective-permute-start | bytes 1769480 | tf_op jit(solution)/shard_map/ppermute | solution.py:910
  96.0 17.0 %collective-permute-start.13 = (bf16[208,768]{1,0:T(8,128)(2,1)S(1)}, bf16[208,768]{1,0:T(8,128)(2,1)S(1)}, u32[]{:S(2)}, u32[]{:S(2)}) collective-permute-start(bf16[208,768]{1,0:T(8,128)(2,1)S(1)} %get-tuple-element.181), channel_id=1, source_target_pairs={{0,16},{4,20},{8,24},{12,28},{16,0},{20,4},{24,8},{28,12},{1,17},{... | collective-permute-start | bytes 958472 | tf_op jit(solution)/shard_map/ppermute | solution.py:910
  107.4 15.5 %collective-permute-start.17 = (bf16[320,768]{1,0:T(8,128)(2,1)S(1)}, bf16[320,768]{1,0:T(8,128)(2,1)S(1)}, u32[]{:S(2)}, u32[]{:S(2)}) collective-permute-start(bf16[320,768]{1,0:T(8,128)(2,1)S(1)} %get-tuple-element.193), channel_id=1, source_target_pairs={{0,2},{1,3},{2,0},{3,1},{4,6},{5,7},{6,4},{7,5},{8,10},{9,11},{10,... | collective-permute-start | bytes 1474568 | tf_op jit(solution)/shard_map/ppermute | solution.py:910
  109.0 4.0 %collective-permute-start.14 = (bf16[3,8,768]{2,1,0:T(8,128)(2,1)S(1)}, bf16[3,8,768]{2,1,0:T(8,128)(2,1)S(1)}, u32[]{:S(2)}, u32[]{:S(2)}) collective-permute-start(bf16[3,8,768]{2,1,0:T(8,128)(2,1)S(1)} %shard_map.294.refs_0_), channel_id=1, source_target_pairs={{0,4},{4,0},{8,12},{12,8},{16,20},{20,16},{24,28},{28,24},{1,5},{5... | collective-permute-start | bytes 110600 | tf_op jit(solution)/shard_map/ppermute | solution.py:910
  109.5 23.8 %slice-start = ((s8[7077888]{0:T(1024)(128)(4,1)}), s8[4194304]{0:T(1024)(128)(4,1)S(1)}, s32[]{:S(2)}) async-start(s8[7077888]{0:T(1024)(128)(4,1)} %bitcast.9), calls=%async_computation | async-start | bytes 8388608
  113.1 11.1 %collective-permute-start.19 = (bf16[192,768]{1,0:T(8,128)(2,1)S(1)}, bf16[192,768]{1,0:T(8,128)(2,1)S(1)}, u32[]{:S(2)}, u32[]{:S(2)}) collective-permute-start(bf16[192,768]{1,0:T(8,128)(2,1)S(1)} %get-tuple-element.205), channel_id=1, source_target_pairs={{0,8},{4,12},{8,0},{12,4},{16,24},{20,28},{24,16},{28,20},{1,9},{5... | collective-permute-start | bytes 884744 | tf_op jit(solution)/shard_map/ppermute | solution.py:910
  114.0 15.4 %collective-permute-start.15 = (bf16[256,768]{1,0:T(8,128)(2,1)S(1)}, bf16[256,768]{1,0:T(8,128)(2,1)S(1)}, u32[]{:S(2)}, u32[]{:S(2)}) collective-permute-start(bf16[256,768]{1,0:T(8,128)(2,1)S(1)} %get-tuple-element.191), channel_id=1, source_target_pairs={{0,2},{1,3},{2,0},{3,1},{4,6},{5,7},{6,4},{7,5},{8,10},{9,11},{10,... | collective-permute-start | bytes 1179656 | tf_op jit(solution)/shard_map/ppermute | solution.py:910
  114.7 8.2 %collective-permute-start.16 = (bf16[4,8,768]{2,1,0:T(8,128)(2,1)S(1)}, bf16[4,8,768]{2,1,0:T(8,128)(2,1)S(1)}, u32[]{:S(2)}, u32[]{:S(2)}) collective-permute-start(bf16[4,8,768]{2,1,0:T(8,128)(2,1)S(1)} %shard_map.295.refs_0_), channel_id=1, source_target_pairs={{0,8},{4,12},{8,0},{12,4},{16,24},{20,28},{24,16},{28,20},{1,9},{5... | collective-permute-start | bytes 147464 | tf_op jit(solution)/shard_map/ppermute | solution.py:910
  122.9 10.4 %collective-permute-start.18 = (bf16[6,8,768]{2,1,0:T(8,128)(2,1)S(1)}, bf16[6,8,768]{2,1,0:T(8,128)(2,1)S(1)}, u32[]{:S(2)}, u32[]{:S(2)}) collective-permute-start(bf16[6,8,768]{2,1,0:T(8,128)(2,1)S(1)} %shard_map.297.refs_1_), channel_id=1, source_target_pairs={{0,16},{4,20},{8,24},{12,28},{16,0},{20,4},{24,8},{28,12},{1,17},{... | collective-permute-start | bytes 221192 | tf_op jit(solution)/shard_map/ppermute | solution.py:910
  124.2 13.6 %collective-permute-start.20 = (bf16[96,768]{1,0:T(8,128)(2,1)S(1)}, bf16[96,768]{1,0:T(8,128)(2,1)S(1)}, u32[]{:S(2)}, u32[]{:S(2)}) collective-permute-start(bf16[96,768]{1,0:T(8,128)(2,1)S(1)} %get-tuple-element.207), channel_id=1, source_target_pairs={{0,16},{4,20},{8,24},{12,28},{16,0},{20,4},{24,8},{28,12},{1,17},{... | collective-permute-start | bytes 442376 | tf_op jit(solution)/shard_map/ppermute | solution.py:910
  (15 other events, 44.2 us)
